TPU v7x, 32 devices: a whole 2x2x4 slice. The times are simulated.
32 devices in a mesh: ctx: 8 (over z, x), head: 4 (over y, core).
Axes of the slice: x: 2, y: 2, z: 4, core: 2. Of those that a mesh axis runs over, the one named last changes fastest.
Arguments:
- q_nope: bfloat16 [1024, 4096], P('ctx', 'head'), may hold values from -6 to 6
- q_rope: bfloat16 [1024, 2048], P('ctx', 'head'), may hold values from -300 to 300
- latent: bfloat16 [1024, 512], P('ctx'), may hold values from -6 to 6
- k_rope: bfloat16 [1024, 64], P('ctx'), may hold values from -4 to 4
- span_order: int32 [16], replicated, may hold values from 0 to 15, each once
- w_uk: bfloat16 [512, 4096], P(None, 'head'), may hold values from -0.25 to 0.25
- w_uv: bfloat16 [512, 4096], P(None, 'head'), may hold values from -0.25 to 0.25
- w_o: bfloat16 [4096, 7168], P('head', 'ctx'), may hold values from -0.125 to 0.125
Outputs:
- attended: bfloat16 [1024, 7168], P('ctx', 'head')
Inputs may be any that keep to these rules, and one draw needn't show every extreme that they name: `span_order`: a permutation of 0 to 15.
All inputs are finite; a program needn't handle non-finite values.
Results may differ from a plain program's by a relative error of at most 0.014.
Values may be sent and summed in bfloat16 or wider, within the bound.
No kernel may reach another device: no remote copies, remote signals or barrier semaphores. Data moves between devices by JAX's collectives and lax.ppermute only.
A program may use at most 128 MiB of HBM per device.

v0:
```python
import math

import jax
import jax.numpy as jnp
from jax import lax
from jax.sharding import PartitionSpec as P

LAT = 512
ROPE = 64
NOPE = 128
VDIM = 128


def span_place(slot_ids, table):
    match = slot_ids[:, None] == jnp.arange(table.shape[0], dtype=jnp.int32)[None, :]
    return jnp.sum(jnp.where(match, table[None, :], 0), axis=1)


def local(q_nope, q_rope, latent, k_rope, span_order, w_uk, w_uv, w_o):
    rows = q_nope.shape[0]
    half = rows // 2
    heads = w_uk.shape[1] // NOPE
    scale = 1.0 / math.sqrt(NOPE + ROPE)
    local_rows = jnp.arange(rows, dtype=jnp.int32)
    query_slot = lax.axis_index("ctx") * 2 + local_rows // half
    qpos = span_place(query_slot, span_order) * half + local_rows % half
    absorbed = jnp.einsum(
        "thn,lhn->htl",
        q_nope.reshape(rows, heads, NOPE),
        w_uk.reshape(LAT, heads, NOPE),
        preferred_element_type=jnp.float32,
    ).astype(jnp.bfloat16)
    rotary = q_rope.reshape(rows, heads, ROPE)
    lat_piece = lax.all_gather(latent, "ctx", axis=0, tiled=True)
    rope_piece = lax.all_gather(k_rope, "ctx", axis=0, tiled=True)
    count = lat_piece.shape[0]
    key_rows = jnp.arange(count, dtype=jnp.int32)
    kpos = span_place(key_rows // half, span_order) * half + key_rows % half
    running = jnp.full((heads, rows), -1e30, jnp.float32)
    score = jnp.einsum("htl,kl->htk", absorbed, lat_piece, preferred_element_type=jnp.float32)
    score = score + jnp.einsum(
        "thr,kr->htk", rotary, rope_piece, preferred_element_type=jnp.float32
    )
    score = score * scale
    visible = kpos[None, None, :] <= qpos[None, :, None]
    newest = jnp.maximum(running, jnp.max(jnp.where(visible, score, -1e30), axis=-1))
    weight = jnp.where(visible, jnp.exp(score - newest[..., None]), 0.0)
    summed = jnp.sum(weight, axis=-1)
    accum = jnp.einsum(
        "htk,kl->htl", weight.astype(jnp.bfloat16), lat_piece, preferred_element_type=jnp.float32
    )
    running, summed, accum = (newest, summed, accum)
    context = (accum / summed[..., None]).astype(jnp.bfloat16)
    heads_out = jnp.einsum(
        "htl,lhv->thv", context, w_uv.reshape(LAT, heads, VDIM), preferred_element_type=jnp.float32
    ).astype(jnp.bfloat16)
    heads_out = heads_out.reshape(rows, heads * VDIM)
    every_token = jnp.dot(
        lax.all_gather(heads_out, "ctx", axis=0, tiled=True),
        w_o,
        preferred_element_type=jnp.float32,
    ).astype(jnp.bfloat16)
    partial_value = lax.all_to_all(every_token, "ctx", split_axis=0, concat_axis=1, tiled=True)
    return (
        lax.psum_scatter(partial_value, "head", scatter_dimension=1, tiled=True)
        .astype(jnp.float32)
        .astype(jnp.bfloat16)
    )


def solution(mesh):
    placed = (
        P("ctx", "head"),
        P("ctx", "head"),
        P("ctx", None),
        P("ctx", None),
        P(),
        P(None, "head"),
        P(None, "head"),
        P("head", "ctx"),
    )
    return jax.shard_map(
        local, mesh=mesh, in_specs=placed, out_specs=P("ctx", "head"), check_vma=False
    )
```

profile of v0, /device:TPU:0, one launch (start us, length us, event | category | flops | bytes accessed | tf_op | source)
XLA Modules:
  0.0 204.4 jit_solution(16470658505095125386)
XLA Ops:
  6.5 0.0 copy-start
  6.5 0.0 all-gather.3.cloned.1.call-start
  6.5 0.7 all-gather.3.cloned.1.call-update
  7.3 0.0 all-gather.5.cloned.1.call-start
  7.3 1.0 copy.19
  8.3 2.3 %copy.24 = bf16[512,1024]{0,1:T(8,128)(2,1)} copy(bf16[512,1024]{1,0:T(8,128)(2,1)} %param.14) | data formatting | bytes 2097152 | tf_op jit(solution)/shard_map/reshape | solution.py:55
  10.6 28.3 %all_gather.10 = bf16[1024,64]{0,1:T(8,128)(2,1)S(1)} all-gather(bf16[128,64]{0,1:T(8,128)(2,1)} %param.11), channel_id=1, replica_groups=mesh['ctx'=8,'head'=4] {'ctx'}, dimensions={0}, use_global_device_ids=true | all-gather | bytes 147456 | tf_op jit(solution)/shard_map/all_gather | solution.py:35
  39.0 0.7 select_reduce_fusion.2
  39.7 0.7 select_reduce_fusion.1
  40.5 0.1 broadcast_compare_fusion
  40.6 12.1 %all-gather.3.cloned.1.call-done = bf16[1024,512]{1,0:T(8,128)(2,1)} async-done(((bf16[128,512]{1,0:T(8,128)(2,1)}), bf16[1024,512]{1,0:T(8,128)(2,1)}) %all-gather.3.cloned.1.call-update) | async-done | bytes 1048592 | tf_op jit(solution)/shard_map/all_gather | solution.py:34
  52.8 5.1 %fusion.8 = f32[8,128,1024]{2,1,0:T(8,128)} fusion(bf16[1024,512]{1,0:T(8,128)(2,1)} %all-gather.3.cloned.1.call-done, bf16[512,1024]{1,0:T(8,128)(2,1)} %param.13, bf16[128,1024]{1,0:T(8,128)(2,1)} %param.8), kind=kOutput, calls=%fused_computation.13 | convolution fusion | flops 1208483840 | bytes 6553600 | tf_op jit(solution)/shard_map/htl,kl->htk/dot_general | solution.py:40
  57.9 3.3 %select_reduce_fusion = (f32[8,128]{1,0:T(8,128)S(1)}, f32[8,128,1024]{2,1,0:T(8,128)S(1)}) fusion(pred[128,1024]{1,0:T(8,128)(4,1)S(1)} %broadcast_compare_fusion, f32[8,128,1024]{2,1,0:T(8,128)} %fusion.8, bf16[128,8,64]{0,2,1:T(8,128)(2,1)S(1)} %bitcast.53, bf16[1024,64]{0,1:T(8,128)(2,1)S(1)} %all_gather.10), kind=kOutput, calls=%fused_computation.3 | convolution fusion | flops 138411008 | bytes 8785920 | tf_op jit(solution)/shard_map/thr,kr->htk/dot_general | solution.py:41
  61.2 0.0 copy-start.1
  61.2 0.0 copy-start.2
  61.2 1.9 copy-done.1
  63.1 1.1 fusion.1
  64.3 0.0 copy-done.2
  64.3 4.8 %convolution_convert_fusion.2 = bf16[8,128,128]{1,2,0:T(8,128)(2,1)} fusion(bf16[512,8,128]{0,2,1:T(8,128)(2,1)} %bitcast.52, f32[8,128]{1,0:T(8,128)S(1)} %fusion.1, f32[8,128,1024]{2,1,0:T(8,128)} %copy-done.1, f32[8,128]{1,0:T(8,128)S(1)} %broadcast_maximum_fusion, pred[128,1024]{1,0:T(8,128)(4,1)S(1)} %broadcast_compare_fusion, ...), kind=kOutput, calls=%fused_computation.14 | convolution fusion | flops 1212284928 | bytes 6692864 | tf_op jit(solution)/shard_map/htl,lhv->thv/dot_general | solution.py:54
  69.1 0.0 all-gather.5.cloned.1.call-update
  69.1 0.0 reduce-scatter.2.cloned.1.call-start
  69.1 49.2 %all-gather.5.cloned.1.call-done = bf16[1024,1024]{0,1:T(8,128)(2,1)} async-done(((bf16[128,1024]{0,1:T(8,128)(2,1)}), bf16[1024,1024]{0,1:T(8,128)(2,1)}) %all-gather.5.cloned.1.call-update) | async-done | bytes 2097168 | tf_op jit(solution)/shard_map/all_gather | solution.py:59
  118.3 0.0 copy-done
  118.3 4.0 %convolution_convert_fusion = bf16[1024,896]{1,0:T(8,128)(2,1)S(1)} fusion(bf16[1024,1024]{0,1:T(8,128)(2,1)} %all-gather.5.cloned.1.call-done, bf16[1024,896]{1,0:T(8,128)(2,1)S(1)} %copy-done), kind=kOutput, calls=%fused_computation.11 | convolution fusion | flops 1879965696 | bytes 5767168 | tf_op jit(solution)/shard_map/dot_general | solution.py:58
  122.3 45.3 %all_to_all.19 = bf16[8,128,896]{2,1,0:T(8,128)(2,1)S(1)} all-to-all(bf16[8,128,896]{2,1,0:T(8,128)(2,1)S(1)} %bitcast.51), channel_id=1, replica_groups=mesh['ctx'=8,'head'=4] {'ctx'}, dimensions={0} | all-to-all | bytes 3670016 | tf_op jit(solution)/shard_map/all_to_all | solution.py:63
  167.5 1.5 copy.27
  169.1 0.0 reduce-scatter.2.cloned.1.call-update
  169.1 28.8 %reduce-scatter.2.cloned.1.call-done = bf16[128,1792]{1,0:T(8,128)(2,1)} async-done(((bf16[128,7168]{1,0:T(8,128)(2,1)}), bf16[128,1792]{1,0:T(8,128)(2,1)}) %reduce-scatter.2.cloned.1.call-update) | async-done | bytes 458768 | tf_op jit(solution)/shard_map/reduce_scatter | solution.py:65
  (5 shorter events, 0.0 us)
Async XLA Ops:
  6.5 111.8 %copy-start = (bf16[1024,896]{1,0:T(8,128)(2,1)S(1)}, bf16[1024,896]{1,0:T(8,128)(2,1)}, u32[]{:S(2)}) copy-start(bf16[1024,896]{1,0:T(8,128)(2,1)} %param.15) | copy-start | bytes 5505028
  6.5 46.2 %all-gather.3.cloned.1.call-start = ((), (), s32[]{:S(2)}) async-start(), calls=%async_computation.2 | async-start | bytes 1179648 | tf_op jit(solution)/shard_map/all_gather | solution.py:34
  7.3 111.0 %all-gather.5.cloned.1.call-start = ((), (), s32[]{:S(2)}) async-start(), calls=%async_computation.3 | async-start | bytes 2359296 | tf_op jit(solution)/shard_map/all_gather | solution.py:59
  61.2 1.9 copy-start.1
  61.2 3.0 %copy-start.2 = (bf16[1024,512]{1,0:T(8,128)(2,1)S(1)}, bf16[1024,512]{1,0:T(8,128)(2,1)}, u32[]{:S(2)}) copy-start(bf16[1024,512]{1,0:T(8,128)(2,1)} %all-gather.3.cloned.1.call-done) | copy-start | bytes 3145732
  69.1 128.8 %reduce-scatter.2.cloned.1.call-start = ((), (), s32[]{:S(2)}) async-start(), calls=%async_computation.4 | async-start | bytes 2293760 | tf_op jit(solution)/shard_map/reduce_scatter | solution.py:65
Sparse Core Ops, SparseCore 0:
  9.5 43.2 all-gather.2
  69.2 49.0 all-gather.4
  169.2 28.5 reduce-scatter.1
where the time goes:
time: 205 us; the launch traced here: 204 us
  waiting for transfers between devices  90.8 us (44%)
  blocking collectives  73.6 us (36%)
  matrix products  17.2 us (8%)
  between operations  13.2 us (6%)
  local copies, waits for them, and re-layouts  6.76 us (3%)
  other arithmetic  2.76 us (1%)
    all_gather x1, waiting for transfers between devices, local(): lax.all_gather(heads_out, 'ctx', axis=0, tiled=True)  49.2 us
    all_to_all x1, blocking collectives, local(): lax.all_to_all(every_token, 'ctx', split_axis=0, concat_axis=1, tiled=True)  45.3 us
    reduce_scatter x1, waiting for transfers between devices, local(): lax.psum_scatter(partial_value, 'head', scatter_dimension=1, tiled=True)  28.8 us
    all_gather x1, blocking collectives, local(): rope_piece = lax.all_gather(k_rope, 'ctx', axis=0, tiled=True)  28.3 us
    all_gather x1, waiting for transfers between devices, local(): lat_piece = lax.all_gather(latent, 'ctx', axis=0, tiled=True)  12.1 us
    dot_general x1, matrix products, local(): jnp.einsum('htl,kl->htk', absorbed, lat_piece, preferred_element_type=jnp...  5.13 us
    dot_general x1, matrix products, local(): jnp.einsum('htl,lhv->thv', context, w_uv.reshape(LAT, heads, VDIM), prefe...  4.77 us
  transfers between devices with their start and end apart: 3, of which 3 were waited for; matrix products, arithmetic and copies ran while one was open for 2% of the time, Pallas kernels for 0%

commit v1 on v0

v1 whole, which is shorter than its diff:
```python
import functools
import math

import jax
import jax.numpy as jnp
from jax import lax
from jax.experimental import pallas as pl
from jax.experimental.pallas import tpu as pltpu
from jax.sharding import PartitionSpec as P

LAT = 512
ROPE = 64
NOPE = 128
VDIM = 128
AXES = ("ctx", "head")
MIB = 1024 * 1024
NT = (((1,), (1,)), ((), ()))


def key_kernel(latent_ref, rope_ref, out_ref):
    out_ref[:, :LAT] = latent_ref[...]
    out_ref[:, LAT:] = rope_ref[...].T


def query_kernel(q_ref, rope_ref, w_ref, out_ref):
    for h in range(out_ref.shape[0]):
        cols = slice(h * NOPE, (h + 1) * NOPE)
        out_ref[h, :, :LAT] = lax.dot_general(
            q_ref[:, cols], w_ref[:, cols], NT, preferred_element_type=jnp.float32
        ).astype(jnp.bfloat16)
        out_ref[h, :, LAT:] = rope_ref[:, h * ROPE : (h + 1) * ROPE]


def place_keys(pairs, order_ref, place_ref, own_ref, direct, passed, keys):
    rows = direct[0].shape[0]
    half = rows // 2
    c = place_ref[0]
    k = place_ref[1]
    lane = lax.broadcasted_iota(jnp.int32, (1, rows), 1)
    places = []

    def add(distance, value):
        slot = 2 * (c ^ distance)
        first = order_ref[slot] * half
        second = order_ref[slot + 1] * half - half
        at = len(places) * rows
        keys[at : at + rows, :] = value
        places.append(lane + jnp.where(lane < half, first, second))

    if own_ref is not None:
        add(0, own_ref[...])
    for (on_0, on_1), mine, other in zip(pairs, direct, passed):
        if on_0 is None:
            add(on_1, jnp.where(k == 0, other[...], mine[...]))
        else:
            add(jnp.where(k == 0, on_0, on_1), mine[...])
            add(jnp.where(k == 0, on_1, on_0), other[...])
    return jnp.concatenate(places, axis=1)


def early_kernel(pairs, group, scale, order_ref, place_ref, q_ref, own_ref, *refs):
    n = len(pairs)
    out_ref, keys = refs[2 * n :]
    key_place = place_keys(
        pairs, order_ref, place_ref, own_ref, refs[:n], refs[n : 2 * n], keys
    )
    heads, rows, _ = q_ref.shape
    half = rows // 2
    c = place_ref[0]
    row = lax.broadcasted_iota(jnp.int32, (rows, 1), 0)
    first = order_ref[2 * c] * half
    second = order_ref[2 * c + 1] * half - half
    visible = key_place <= row + jnp.where(row < half, first, second)
    lane = lax.broadcasted_iota(jnp.int32, (1, 1, 128), 2)
    for g in range(0, heads, group):
        q = q_ref[g : g + group].reshape(group * rows, LAT + ROPE)
        score = lax.dot_general(q, keys[...], NT, preferred_element_type=jnp.float32)
        score = score.reshape(group, rows, -1) * scale
        score = jnp.where(visible[None], score, -1e30)
        top = jnp.max(score, axis=-1, keepdims=True)
        weight = jnp.exp(score - top)
        total = jnp.sum(weight, axis=-1, keepdims=True)
        weight = weight.astype(jnp.bfloat16).reshape(group * rows, -1)
        accum = jnp.dot(weight, keys[:, :LAT], preferred_element_type=jnp.float32)
        out_ref[g : g + group, :, :LAT] = accum.reshape(group, rows, LAT)
        out_ref[g : g + group, :, LAT:] = jnp.where(lane == 0, top, total)


def late_kernel(pairs, group, scale, span, order_ref, place_ref, q_ref, w_ref, early_ref, *refs):
    n = len(pairs)
    out_ref, keys = refs[2 * n :]
    key_place = place_keys(pairs, order_ref, place_ref, None, refs[:n], refs[n : 2 * n], keys)
    heads, rows, _ = q_ref.shape
    half = rows // 2
    c = place_ref[0]
    row = lax.broadcasted_iota(jnp.int32, (half, 1), 0)
    visible = key_place <= row + order_ref[2 * c + span] * half
    these = slice(span * half, (span + 1) * half)
    for g in range(0, heads, group):
        q = q_ref[g : g + group, these, :].reshape(group * half, LAT + ROPE)
        score = lax.dot_general(q, keys[...], NT, preferred_element_type=jnp.float32)
        score = score.reshape(group, half, -1) * scale
        score = jnp.where(visible[None], score, -1e30)
        old = early_ref[g : g + group, these, LAT : LAT + 1]
        total = early_ref[g : g + group, these, LAT + 1 : LAT + 2]
        top = jnp.maximum(old, jnp.max(score, axis=-1, keepdims=True))
        fade = jnp.exp(old - top)
        weight = jnp.exp(score - top)
        total = total * fade + jnp.sum(weight, axis=-1, keepdims=True)
        weight = weight.astype(jnp.bfloat16).reshape(group * half, -1)
        accum = jnp.dot(weight, keys[:, :LAT], preferred_element_type=jnp.float32)
        accum = accum.reshape(group, half, LAT) + early_ref[g : g + group, these, :LAT] * fade
        context = (accum / total).astype(jnp.bfloat16)
        for i in range(group):
            cols = slice((g + i) * VDIM, (g + i + 1) * VDIM)
            out_ref[:, cols] = jnp.dot(
                context[i], w_ref[:, cols], preferred_element_type=jnp.float32
            ).astype(jnp.bfloat16)


def project_kernel(zs, xs, kept, place_ref, *refs):
    blocks, weights, out_ref = refs[: zs + 2], refs[zs + 2 : -1], refs[-1]
    zl = zs // 2
    k = place_ref[1]
    z = place_ref[2]
    x = place_ref[3]
    inner = (z % 4 == 1) | (z % 4 == 2)
    low_half = (k ^ (z // zl)) == 0 if kept else (k ^ (z // zl)) == 1

    def block(d):
        if d < 2:
            return blocks[d][...]
        if d < 4:
            at = 2 * d - 2
            return jnp.where(inner, blocks[at][...], blocks[at + 1][...])
        return blocks[d + 2][...]

    rows = blocks[0].shape[0]
    tokens = jnp.concatenate(
        [jnp.where(low_half, block(d), block(d + zl)) for d in range(zl)], axis=0
    )
    for dx in range(xs):
        part = jnp.dot(tokens, weights[dx][...], preferred_element_type=jnp.float32)
        part = part.astype(out_ref.dtype).reshape(zl, rows, -1)
        for d in range(zl):
            out_ref[d, x ^ dx] = part[d]


def halve_kernel(bit, span, place_ref, mine_ref, got_ref, keep_ref, away_ref):
    which = place_ref[4 + span]
    low = ((which // bit) % 2) == 0
    for d in range(bit):
        a = mine_ref[d] + got_ref[d].astype(jnp.float32)
        b = mine_ref[d + bit] + got_ref[d + bit].astype(jnp.float32)
        keep_ref[d] = jnp.where(low, a, b)
        away_ref[d] = jnp.where(low, b, a).astype(away_ref.dtype)


def add_kernel(mine_ref, got_ref, out_ref):
    out_ref[...] = (mine_ref[0] + got_ref[0].astype(jnp.float32)).astype(out_ref.dtype)


def output_kernel(*refs):
    out_ref = refs[-1]
    for span, ref in enumerate(refs[:-1]):
        xs, half, cols = ref.shape
        for i in range(xs):
            out_ref[span * half : (span + 1) * half, i * cols : (i + 1) * cols] = ref[i]


def whole():
    return pl.BlockSpec(memory_space=pltpu.VMEM)


def call(kernel, outs, args, smem=0, scratch=(), vmem=16, flops=0, exps=0):
    several = isinstance(outs, list)
    outs = outs if several else [outs]
    shapes = [jax.ShapeDtypeStruct(shape, kind) for shape, kind in outs]
    moved = sum(a.size * a.dtype.itemsize for a in [*args, *shapes])
    result = pl.pallas_call(
        kernel,
        out_shape=shapes,
        in_specs=[pl.BlockSpec(memory_space=pltpu.SMEM)] * smem + [whole()] * (len(args) - smem),
        out_specs=[whole()] * len(shapes),
        scratch_shapes=list(scratch),
        compiler_params=pltpu.CompilerParams(vmem_limit_bytes=vmem * MIB),
        cost_estimate=pl.CostEstimate(flops=flops, bytes_accessed=moved, transcendentals=exps),
    )(*args)
    return result if several else result[0]


def local(ctx_n, head_n, q_nope, q_rope, latent, k_rope, span_order, w_uk, w_uv, w_o):
    rows = q_nope.shape[0]
    half = rows // 2
    heads = w_uk.shape[1] // NOPE
    depth, cols = w_o.shape
    scale = 1.0 / math.sqrt(NOPE + ROPE)
    xs = head_n // 2
    zs = ctx_n // xs
    zl = zs // 2
    c = lax.axis_index("ctx")
    h = lax.axis_index("head")
    k, y, z, x = h % 2, h // 2, c // xs, c % xs
    place = jnp.stack([c, k, z, x, y ^ (z % zl), y ^ (z % zl) ^ (zl - 1)]).astype(jnp.int32)
    bf16, f32 = jnp.bfloat16, jnp.float32

    def send(value, where):
        pairs = []
        for ci in range(ctx_n):
            for hi in range(head_n):
                to = where(ci // xs, ci % xs, hi // 2, hi % 2)
                if to is not None:
                    tz, tx, ty, tk = to
                    pairs.append((ci * head_n + hi, (tz * xs + tx) * head_n + ty * 2 + tk))
        return lax.ppermute(value, AXES, pairs)

    keys = call(key_kernel, ((rows, LAT + ROPE), bf16), (latent, k_rope.T), vmem=4)
    pairs = [(d, d + 1) for d in range(1, ctx_n - 1, 2)] + [(None, ctx_n - 1)]

    def across(pair):
        def where(z, x, y, k):
            d = pair[k]
            return None if d is None else (z ^ (d // xs), x ^ (d % xs), y, k)

        return where

    def to_other(pair):
        return lambda z, x, y, k: (z, x, y, 1 - k) if pair[k] is not None else None

    def inner_only(where):
        return lambda z, x, y, k: where(z, x, y, k) if z % 4 in (1, 2) else None

    direct = []
    for pair in pairs:
        direct.append(send(keys, across(pair)))
    matrices = [w_o] + [
        send(w_o, lambda z, x, y, k: (z, x ^ dx, y, k)) for dx in range(1, xs)
    ]
    queries = call(
        query_kernel,
        ((heads, rows, LAT + ROPE), bf16),
        (q_nope, q_rope, w_uk),
        flops=2 * rows * heads * NOPE * LAT,
    )
    first = len(pairs) // 2
    direct[:first], queries = lax.optimization_barrier((direct[:first], queries))
    passed = [send(direct[i], to_other(pairs[i])) for i in range(first)]
    n_early = 1 + 2 * first
    n_late = ctx_n - n_early

    def work(queries_n, keys_n):
        return 2 * queries_n * heads * keys_n * (2 * LAT + ROPE)

    early = call(
        functools.partial(early_kernel, pairs[:first], 2, scale),
        ((heads, rows, LAT + 128), f32),
        (span_order, place, queries, keys, *direct[:first], *passed[:first]),
        smem=2,
        scratch=(pltpu.VMEM((n_early * rows, LAT + ROPE), bf16),),
        vmem=32,
        flops=work(rows, n_early * rows),
        exps=rows * heads * n_early * rows,
    )
    direct[first:], early = lax.optimization_barrier((direct[first:], early))
    passed += [send(direct[i], to_other(pairs[i])) for i in range(first, len(pairs))]
    results = []
    for span in range(2):
        flip = span * (zl - 1)
        heads_out = call(
            functools.partial(late_kernel, pairs[first:], 4, scale, span),
            ((half, heads * VDIM), bf16),
            (span_order, place, queries, w_uv, early, *direct[first:], *passed[first:]),
            smem=2,
            scratch=(pltpu.VMEM((n_late * rows, LAT + ROPE), bf16),),
            vmem=32,
            flops=work(half, n_late * rows) + 2 * half * heads * LAT * VDIM,
            exps=half * heads * n_late * rows,
        )
        beside = send(heads_out, lambda z, x, y, k: (z ^ 1, x, y, k))
        middle = send(heads_out, inner_only(lambda z, x, y, k: (z ^ 3, x, y, k)))
        outer_2 = send(middle, inner_only(lambda z, x, y, k: (z ^ 1, x, y, k)))
        inner_2 = send(beside, inner_only(lambda z, x, y, k: (z ^ 3, x, y, k)))
        outer_3 = send(inner_2, inner_only(lambda z, x, y, k: (z ^ 1, x, y, k)))
        along = [heads_out, beside, inner_2, outer_2, middle, outer_3]
        along += [
            send(heads_out, lambda z, x, y, k: (z ^ d, x, y, k)) for d in range(4, zs)
        ]

        def project(kept, kind):
            return call(
                functools.partial(project_kernel, zs, xs, kept),
                ((zl, xs, half, cols), kind),
                (place, *along, *matrices),
                smem=1,
                flops=2 * zl * half * depth * xs * cols,
            )

        away = project(False, bf16)
        got = send(away, lambda z, x, y, k: (z, x, y, 1 - k))
        mine = project(True, f32)
        bit = zl // 2
        while bit:
            block = (bit, xs, half, cols)
            mine, away = call(
                functools.partial(halve_kernel, bit, span),
                [(block, f32), (block, bf16)],
                (place, mine, got),
                smem=1,
            )
            got = send(away, lambda z, x, y, k: (z, x, y ^ bit, k))
            bit //= 2
        block = call(add_kernel, ((xs, half, cols), bf16), (mine, got))
        results.append(send(block, lambda z, x, y, k: (k * zl + (y ^ flip), x, z // 2, z % 2)))
    return call(output_kernel, ((rows, xs * cols), bf16), tuple(results))


def solution(mesh):
    placed = (
        P("ctx", "head"),
        P("ctx", "head"),
        P("ctx", None),
        P("ctx", None),
        P(),
        P(None, "head"),
        P(None, "head"),
        P("head", "ctx"),
    )
    ctx_n, head_n = mesh.shape["ctx"], mesh.shape["head"]

    def step(*args):
        return local(ctx_n, head_n, *args)

    return jax.shard_map(
        step, mesh=mesh, in_specs=placed, out_specs=P("ctx", "head"), check_vma=False
    )
```

time: 205 us -> 129 us (0.63)
  the two profiles are of different devices: /device:TPU:0 before, /device:TPU:1 now
where the time goes in v1:
time: 129 us; the launch traced here: 128 us
  starting transfers between devices  75.1 us (58%)
  waiting for transfers between devices  29.7 us (23%)
  Pallas kernels  18.5 us (14%)
  local copies, waits for them, and re-layouts  4.79 us (4%)
    ppermute x25, starting transfers between devices, send(): return lax.ppermute(value, AXES, pairs)  75.1 us
    ppermute x25, waiting for transfers between devices, send(): return lax.ppermute(value, AXES, pairs)  29.7 us
    pallas_call x14, Pallas kernels, call(): pl.pallas_call(kernel, out_shape=shapes, in_specs=[pl.BlockSpec(memory_sp...  18.5 us
    unnamed x16, local copies, waits for them, and re-layouts  4.71 us
  transfers between devices with their start and end apart: 25, of which 11 were waited for; matrix products, arithmetic and copies ran while one was open for 0% of the time, Pallas kernels for 14%

profile of v1, /device:TPU:1, one launch (start us, length us, event | category | flops | bytes accessed | tf_op | source)
XLA Modules:
  0.0 128.3 jit_solution(16179639429941660472)
XLA Ops:
  0.0 2.0 %collective-permute-start.13 = (bf16[1024,896]{1,0:T(8,128)(2,1)}, bf16[1024,896]{1,0:T(8,128)(2,1)S(1)}, u32[]{:S(2)}, u32[]{:S(2)}) collective-permute-start(bf16[1024,896]{1,0:T(8,128)(2,1)} %refs_6_.7), channel_id=1, source_target_pairs={{0,4},{1,5},{2,6},{3,7},{4,0},{5,1},{6,2},{7,3},{8,12},{9,13},{10,... | collective-permute-start | bytes 5505032 | tf_op jit(solution)/shard_map/ppermute | solution.py:215
  4.4 2.3 %collective-permute-start.1 = (bf16[128,576]{1,0:T(8,128)(2,1)}, bf16[128,576]{1,0:T(8,128)(2,1)}, u32[]{:S(2)}, u32[]{:S(2)}) collective-permute-start(bf16[128,576]{1,0:T(8,128)(2,1)} %shard_map.82.own_ref), channel_id=1, source_target_pairs={{0,12},{1,17},{2,14},{3,19},{4,8},{5,21},{6,10},{7,23},{8,4},{9,25... | collective-permute-start | bytes 442376 | tf_op jit(solution)/shard_map/ppermute | solution.py:215
  6.7 1.3 %collective-permute-start = (bf16[128,576]{1,0:T(8,128)(2,1)}, bf16[128,576]{1,0:T(8,128)(2,1)}, u32[]{:S(2)}, u32[]{:S(2)}) collective-permute-start(bf16[128,576]{1,0:T(8,128)(2,1)} %shard_map.82.own_ref), channel_id=1, source_target_pairs={{0,4},{1,9},{2,6},{3,11},{4,0},{5,13},{6,2},{7,15},{8,12},{9,1},{1... | collective-permute-start | bytes 442376 | tf_op jit(solution)/shard_map/ppermute | solution.py:215
  11.8 1.8 %collective-permute-done.refs_0_ = bf16[128,576]{1,0:T(8,128)(2,1)} collective-permute-done((bf16[128,576]{1,0:T(8,128)(2,1)}, bf16[128,576]{1,0:T(8,128)(2,1)}, u32[]{:S(2)}, u32[]{:S(2)}) %collective-permute-start) | collective-permute-done | bytes 147488 | tf_op jit(solution)/shard_map/ppermute | solution.py:215
  13.6 33.2 %collective-permute-start.4 = (bf16[128,576]{1,0:T(8,128)(2,1)}, bf16[128,576]{1,0:T(8,128)(2,1)}, u32[]{:S(2)}, u32[]{:S(2)}) collective-permute-start(bf16[128,576]{1,0:T(8,128)(2,1)} %collective-permute-done.refs_0_), channel_id=1, source_target_pairs={{0,1},{1,0},{2,3},{3,2},{4,5},{5,4},{6,7},{7,6},{8,9},{9,8},{10,11... | collective-permute-start | bytes 442376 | tf_op jit(solution)/shard_map/ppermute | solution.py:215
  46.8 6.4 %collective-permute-start.3 = (bf16[128,576]{1,0:T(8,128)(2,1)}, bf16[128,576]{1,0:T(8,128)(2,1)S(1)}, u32[]{:S(2)}, u32[]{:S(2)}) collective-permute-start(bf16[128,576]{1,0:T(8,128)(2,1)} %shard_map.82.own_ref), channel_id=1, source_target_pairs={{1,29},{3,31},{5,25},{7,27},{9,21},{11,23},{13,17},{15,19},{17,13}... | collective-permute-start | bytes 442376 | tf_op jit(solution)/shard_map/ppermute | solution.py:215
  53.5 4.5 %shard_map.84.early_ref = f32[8,128,640]{2,1,0:T(8,128)S(1)} custom-call(s32[16]{0:T(128)S(1)} %copy-done.7, s32[6]{0:T(128)S(1)} %stack.27.place_ref, bf16[8,128,576]{2,1,0:T(8,128)(2,1)S(1)} %shard_map.83.q_ref, bf16[128,576]{1,0:T(8,128)(2,1)} %shard_map.82.own_ref, bf16[128,576]{1,0:T(8,128)(2,1)} %collective-permute-done.refs_0_, ...), custom_call_target="tpu_custom_call" | custom-call | flops 1426063360 | bytes 4538456 | tf_op jit(solution)/shard_map/pallas_call | solution.py:180
  58.0 1.9 %collective-permute-done.2.refs_0_ = bf16[128,576]{1,0:T(8,128)(2,1)S(1)} collective-permute-done((bf16[128,576]{1,0:T(8,128)(2,1)}, bf16[128,576]{1,0:T(8,128)(2,1)S(1)}, u32[]{:S(2)}, u32[]{:S(2)}) %collective-permute-start.2) | collective-permute-done | bytes 147488 | tf_op jit(solution)/shard_map/ppermute | solution.py:215
  59.8 2.0 %collective-permute-start.6 = (bf16[128,576]{1,0:T(8,128)(2,1)S(1)}, bf16[128,576]{1,0:T(8,128)(2,1)S(1)}, u32[]{:S(2)}, u32[]{:S(2)}) collective-permute-start(bf16[128,576]{1,0:T(8,128)(2,1)S(1)} %collective-permute-done.2.refs_0_), channel_id=1, source_target_pairs={{0,1},{1,0},{2,3},{3,2},{4,5},{5,4},{6,7},{7,6},{8,9},{9,8},{10,11... | collective-permute-start | bytes 442376 | tf_op jit(solution)/shard_map/ppermute | solution.py:215
  61.9 1.9 %collective-permute-start.7 = (bf16[128,576]{1,0:T(8,128)(2,1)S(1)}, bf16[128,576]{1,0:T(8,128)(2,1)S(1)}, u32[]{:S(2)}, u32[]{:S(2)}) collective-permute-start(bf16[128,576]{1,0:T(8,128)(2,1)S(1)} %collective-permute-done.3.refs_1_), channel_id=1, source_target_pairs={{1,0},{3,2},{5,4},{7,6},{9,8},{11,10},{13,12},{15,14},{17,16},{19,... | collective-permute-start | bytes 442376 | tf_op jit(solution)/shard_map/ppermute | solution.py:215
  64.8 2.7 %shard_map.85.refs_0_ = bf16[64,1024]{1,0:T(8,128)(2,1)S(1)} custom-call(s32[16]{0:T(128)S(1)} %copy-done.7, s32[6]{0:T(128)S(1)} %stack.27.place_ref, bf16[8,128,576]{2,1,0:T(8,128)(2,1)S(1)} %shard_map.83.q_ref, bf16[512,1024]{1,0:T(8,128)(2,1)S(1)} %copy-done.1, f32[8,128,640]{2,1,0:T(8,128)S(1)} %shard_map.84.early_ref, ...), custom_call_target="tpu_custom_call" | custom-call | flops 494927872 | bytes 5570648 | tf_op jit(solution)/shard_map/pallas_call | solution.py:180
  67.5 2.7 %collective-permute-start.8 = (bf16[64,1024]{1,0:T(8,128)(2,1)S(1)}, bf16[64,1024]{1,0:T(8,128)(2,1)S(1)}, u32[]{:S(2)}, u32[]{:S(2)}) collective-permute-start(bf16[64,1024]{1,0:T(8,128)(2,1)S(1)} %shard_map.85.refs_0_), channel_id=1, source_target_pairs={{0,8},{1,9},{2,10},{3,11},{4,12},{5,13},{6,14},{7,15},{8,0},{9,1},... | collective-permute-start | bytes 393224 | tf_op jit(solution)/shard_map/ppermute | solution.py:215
  70.2 2.7 %shard_map.90.refs_0_ = bf16[64,1024]{1,0:T(8,128)(2,1)S(1)} custom-call(s32[16]{0:T(128)S(1)} %copy-done.7, s32[6]{0:T(128)S(1)} %stack.27.place_ref, bf16[8,128,576]{2,1,0:T(8,128)(2,1)S(1)} %shard_map.83.q_ref, bf16[512,1024]{1,0:T(8,128)(2,1)S(1)} %copy-done.1, f32[8,128,640]{2,1,0:T(8,128)S(1)} %shard_map.84.early_ref, ...), custom_call_target="tpu_custom_call" | custom-call | flops 494927872 | bytes 5570648 | tf_op jit(solution)/shard_map/pallas_call | solution.py:180
  75.0 2.3 %collective-permute-done.17.refs_1_ = bf16[64,1024]{1,0:T(8,128)(2,1)S(1)} collective-permute-done((bf16[64,1024]{1,0:T(8,128)(2,1)S(1)}, bf16[64,1024]{1,0:T(8,128)(2,1)S(1)}, u32[]{:S(2)}, u32[]{:S(2)}) %collective-permute-start.17) | collective-permute-done | bytes 131104 | tf_op jit(solution)/shard_map/ppermute | solution.py:215
  78.0 1.3 %collective-permute-start.11 = (bf16[64,1024]{1,0:T(8,128)(2,1)S(1)}, bf16[64,1024]{1,0:T(8,128)(2,1)S(1)}, u32[]{:S(2)}, u32[]{:S(2)}) collective-permute-start(bf16[64,1024]{1,0:T(8,128)(2,1)S(1)} %collective-permute-done.10.refs_4_), channel_id=1, source_target_pairs={{8,0},{9,1},{10,2},{11,3},{12,4},{13,5},{14,6},{15,7},{16,24},{17,... | collective-permute-start | bytes 393224 | tf_op jit(solution)/shard_map/ppermute | solution.py:215
  79.3 1.3 %collective-permute-start.12 = (bf16[64,1024]{1,0:T(8,128)(2,1)S(1)}, bf16[64,1024]{1,0:T(8,128)(2,1)S(1)}, u32[]{:S(2)}, u32[]{:S(2)}) collective-permute-start(bf16[64,1024]{1,0:T(8,128)(2,1)S(1)} %collective-permute-done.9.refs_2_), channel_id=1, source_target_pairs={{8,0},{9,1},{10,2},{11,3},{12,4},{13,5},{14,6},{15,7},{16,24},{17,... | collective-permute-start | bytes 393224 | tf_op jit(solution)/shard_map/ppermute | solution.py:215
  80.6 1.3 %collective-permute-start.20 = (bf16[64,1024]{1,0:T(8,128)(2,1)S(1)}, bf16[64,1024]{1,0:T(8,128)(2,1)S(1)}, u32[]{:S(2)}, u32[]{:S(2)}) collective-permute-start(bf16[64,1024]{1,0:T(8,128)(2,1)S(1)} %collective-permute-done.19.refs_4_), channel_id=1, source_target_pairs={{8,0},{9,1},{10,2},{11,3},{12,4},{13,5},{14,6},{15,7},{16,24},{17,... | collective-permute-start | bytes 393224 | tf_op jit(solution)/shard_map/ppermute | solution.py:215
  81.9 1.3 %collective-permute-start.21 = (bf16[64,1024]{1,0:T(8,128)(2,1)S(1)}, bf16[64,1024]{1,0:T(8,128)(2,1)S(1)}, u32[]{:S(2)}, u32[]{:S(2)}) collective-permute-start(bf16[64,1024]{1,0:T(8,128)(2,1)S(1)} %collective-permute-done.18.refs_2_), channel_id=1, source_target_pairs={{8,0},{9,1},{10,2},{11,3},{12,4},{13,5},{14,6},{15,7},{16,24},{17,... | collective-permute-start | bytes 393224 | tf_op jit(solution)/shard_map/ppermute | solution.py:215
  83.2 5.5 %collective-permute-done.11.refs_3_ = bf16[64,1024]{1,0:T(8,128)(2,1)S(1)} collective-permute-done((bf16[64,1024]{1,0:T(8,128)(2,1)S(1)}, bf16[64,1024]{1,0:T(8,128)(2,1)S(1)}, u32[]{:S(2)}, u32[]{:S(2)}) %collective-permute-start.11) | collective-permute-done | bytes 131104 | tf_op jit(solution)/shard_map/ppermute | solution.py:215
  88.8 2.4 %collective-permute-done.12.refs_5_ = bf16[64,1024]{1,0:T(8,128)(2,1)S(1)} collective-permute-done((bf16[64,1024]{1,0:T(8,128)(2,1)S(1)}, bf16[64,1024]{1,0:T(8,128)(2,1)S(1)}, u32[]{:S(2)}, u32[]{:S(2)}) %collective-permute-start.12) | collective-permute-done | bytes 131104 | tf_op jit(solution)/shard_map/ppermute | solution.py:215
  91.2 1.3 %shard_map.87 = bf16[2,2,64,896]{3,2,1,0:T(8,128)(2,1)S(1)} custom-call(s32[6]{0:T(128)S(1)} %stack.27.place_ref, bf16[64,1024]{1,0:T(8,128)(2,1)S(1)} %shard_map.85.refs_0_, bf16[64,1024]{1,0:T(8,128)(2,1)S(1)} %collective-permute-done.8.refs_1_, bf16[64,1024]{1,0:T(8,128)(2,1)S(1)} %collective-permute-done.9.refs_2_, ...), custom_call_target="tpu_custom_call" | custom-call | flops 469762048 | bytes 4915224 | tf_op jit(solution)/shard_map/pallas_call | solution.py:180
  92.5 4.6 %collective-permute-start.14 = (bf16[2,2,64,896]{3,2,1,0:T(8,128)(2,1)S(1)}, bf16[2,2,64,896]{3,2,1,0:T(8,128)(2,1)S(1)}, u32[]{:S(2)}, u32[]{:S(2)}) collective-permute-start(bf16[2,2,64,896]{3,2,1,0:T(8,128)(2,1)S(1)} %shard_map.87), channel_id=1, source_target_pairs={{0,1},{1,0},{2,3},{3,2},{4,5},{5,4},{6,7},{7,6},{8,9},{9,8},{10,11... | collective-permute-start | bytes 1376264 | tf_op jit(solution)/shard_map/ppermute | solution.py:215
  97.1 1.3 %shard_map.92 = bf16[2,2,64,896]{3,2,1,0:T(8,128)(2,1)S(1)} custom-call(s32[6]{0:T(128)S(1)} %stack.27.place_ref, bf16[64,1024]{1,0:T(8,128)(2,1)S(1)} %shard_map.90.refs_0_, bf16[64,1024]{1,0:T(8,128)(2,1)S(1)} %collective-permute-done.17.refs_1_, bf16[64,1024]{1,0:T(8,128)(2,1)S(1)} %collective-permute-done.18.refs_2_, ...), custom_call_target="tpu_custom_call" | custom-call | flops 469762048 | bytes 4915224 | tf_op jit(solution)/shard_map/pallas_call | solution.py:180
  98.4 2.2 %collective-permute-start.22 = (bf16[2,2,64,896]{3,2,1,0:T(8,128)(2,1)S(1)}, bf16[2,2,64,896]{3,2,1,0:T(8,128)(2,1)S(1)}, u32[]{:S(2)}, u32[]{:S(2)}) collective-permute-start(bf16[2,2,64,896]{3,2,1,0:T(8,128)(2,1)S(1)} %shard_map.92), channel_id=1, source_target_pairs={{0,1},{1,0},{2,3},{3,2},{4,5},{5,4},{6,7},{7,6},{8,9},{9,8},{10,11... | collective-permute-start | bytes 1376264 | tf_op jit(solution)/shard_map/ppermute | solution.py:215
  100.7 1.3 %shard_map.91.mine_ref = f32[2,2,64,896]{3,2,1,0:T(8,128)S(1)} custom-call(s32[6]{0:T(128)S(1)} %stack.27.place_ref, bf16[64,1024]{1,0:T(8,128)(2,1)S(1)} %shard_map.90.refs_0_, bf16[64,1024]{1,0:T(8,128)(2,1)S(1)} %collective-permute-done.17.refs_1_, bf16[64,1024]{1,0:T(8,128)(2,1)S(1)} %collective-permute-done.18.refs_2_, ...), custom_call_target="tpu_custom_call" | custom-call | flops 469762048 | bytes 5373976 | tf_op jit(solution)/shard_map/pallas_call | solution.py:180
  102.0 1.3 shard_map.86.mine_ref
  103.9 1.3 %collective-permute-start.15 = (bf16[1,2,64,896]{3,2,1,0:T(8,128)(2,1)S(1)}, bf16[1,2,64,896]{3,2,1,0:T(8,128)(2,1)S(1)}, u32[]{:S(2)}, u32[]{:S(2)}) collective-permute-start(bf16[1,2,64,896]{3,2,1,0:T(8,128)(2,1)S(1)} %get-tuple-element.22), channel_id=1, source_target_pairs={{0,2},{1,3},{2,0},{3,1},{4,6},{5,7},{6,4},{7,5},{8,10},{9,11},{10,... | collective-permute-start | bytes 688136 | tf_op jit(solution)/shard_map/ppermute | solution.py:215
  106.2 4.9 %collective-permute-done.15.got_ref = bf16[1,2,64,896]{3,2,1,0:T(8,128)(2,1)S(1)} collective-permute-done((bf16[1,2,64,896]{3,2,1,0:T(8,128)(2,1)S(1)}, bf16[1,2,64,896]{3,2,1,0:T(8,128)(2,1)S(1)}, u32[]{:S(2)}, u32[]{:S(2)}) %collective-permute-start.15) | collective-permute-done | bytes 229408 | tf_op jit(solution)/shard_map/ppermute | solution.py:215
  111.2 3.6 %collective-permute-start.16 = (bf16[2,64,896]{2,1,0:T(8,128)(2,1)S(1)}, bf16[2,64,896]{2,1,0:T(8,128)(2,1)S(1)}, u32[]{:S(2)}, u32[]{:S(2)}) collective-permute-start(bf16[2,64,896]{2,1,0:T(8,128)(2,1)S(1)} %shard_map.89), channel_id=1, source_target_pairs={{0,0},{1,16},{2,8},{3,24},{4,4},{5,20},{6,12},{7,28},{8,1},{9,17},... | collective-permute-start | bytes 688136 | tf_op jit(solution)/shard_map/ppermute | solution.py:215
  114.8 1.3 %collective-permute-done.23.got_ref = bf16[1,2,64,896]{3,2,1,0:T(8,128)(2,1)S(1)} collective-permute-done((bf16[1,2,64,896]{3,2,1,0:T(8,128)(2,1)S(1)}, bf16[1,2,64,896]{3,2,1,0:T(8,128)(2,1)S(1)}, u32[]{:S(2)}, u32[]{:S(2)}) %collective-permute-start.23) | collective-permute-done | bytes 229408 | tf_op jit(solution)/shard_map/ppermute | solution.py:215
  116.1 3.2 %collective-permute-start.24 = (bf16[2,64,896]{2,1,0:T(8,128)(2,1)S(1)}, bf16[2,64,896]{2,1,0:T(8,128)(2,1)S(1)}, u32[]{:S(2)}, u32[]{:S(2)}) collective-permute-start(bf16[2,64,896]{2,1,0:T(8,128)(2,1)S(1)} %shard_map.94), channel_id=1, source_target_pairs={{0,8},{1,24},{2,0},{3,16},{4,12},{5,28},{6,4},{7,20},{8,9},{9,25},... | collective-permute-start | bytes 688136 | tf_op jit(solution)/shard_map/ppermute | solution.py:215
  119.3 8.2 %collective-permute-done.24.refs_1_ = bf16[2,64,896]{2,1,0:T(8,128)(2,1)S(1)} collective-permute-done((bf16[2,64,896]{2,1,0:T(8,128)(2,1)S(1)}, bf16[2,64,896]{2,1,0:T(8,128)(2,1)S(1)}, u32[]{:S(2)}, u32[]{:S(2)}) %collective-permute-start.24) | collective-permute-done | bytes 229408 | tf_op jit(solution)/shard_map/ppermute | solution.py:215
  (49 shorter events, 12.7 us)
Async XLA Ops:
  0.0 53.5 %copy-start.7 = (s32[16]{0:T(128)S(1)}, s32[16]{0:T(128)}, u32[]{:S(2)}) copy-start(s32[16]{0:T(128)} %order_ref.5) | copy-start | bytes 196
  0.0 91.2 %collective-permute-start.13 = (bf16[1024,896]{1,0:T(8,128)(2,1)}, bf16[1024,896]{1,0:T(8,128)(2,1)S(1)}, u32[]{:S(2)}, u32[]{:S(2)}) collective-permute-start(bf16[1024,896]{1,0:T(8,128)(2,1)} %refs_6_.7), channel_id=1, source_target_pairs={{0,4},{1,5},{2,6},{3,7},{4,0},{5,1},{6,2},{7,3},{8,12},{9,13},{10,... | collective-permute-start | bytes 5505032 | tf_op jit(solution)/shard_map/ppermute | solution.py:215
  2.0 0.9 copy-start.4
  4.4 7.4 %collective-permute-start.1 = (bf16[128,576]{1,0:T(8,128)(2,1)}, bf16[128,576]{1,0:T(8,128)(2,1)}, u32[]{:S(2)}, u32[]{:S(2)}) collective-permute-start(bf16[128,576]{1,0:T(8,128)(2,1)} %shard_map.82.own_ref), channel_id=1, source_target_pairs={{0,12},{1,17},{2,14},{3,19},{4,8},{5,21},{6,10},{7,23},{8,4},{9,25... | collective-permute-start | bytes 442376 | tf_op jit(solution)/shard_map/ppermute | solution.py:215
  6.7 6.9 %collective-permute-start = (bf16[128,576]{1,0:T(8,128)(2,1)}, bf16[128,576]{1,0:T(8,128)(2,1)}, u32[]{:S(2)}, u32[]{:S(2)}) collective-permute-start(bf16[128,576]{1,0:T(8,128)(2,1)} %shard_map.82.own_ref), channel_id=1, source_target_pairs={{0,4},{1,9},{2,6},{3,11},{4,0},{5,13},{6,2},{7,15},{8,12},{9,1},{1... | collective-permute-start | bytes 442376 | tf_op jit(solution)/shard_map/ppermute | solution.py:215
  8.0 1.2 copy-start.2
  9.2 0.9 copy-start.3
  10.2 0.9 copy-start.5
  13.6 39.9 %collective-permute-start.4 = (bf16[128,576]{1,0:T(8,128)(2,1)}, bf16[128,576]{1,0:T(8,128)(2,1)}, u32[]{:S(2)}, u32[]{:S(2)}) collective-permute-start(bf16[128,576]{1,0:T(8,128)(2,1)} %collective-permute-done.refs_0_), channel_id=1, source_target_pairs={{0,1},{1,0},{2,3},{3,2},{4,5},{5,4},{6,7},{7,6},{8,9},{9,8},{10,11... | collective-permute-start | bytes 442376 | tf_op jit(solution)/shard_map/ppermute | solution.py:215
  46.8 6.6 %collective-permute-start.5 = (bf16[128,576]{1,0:T(8,128)(2,1)}, bf16[128,576]{1,0:T(8,128)(2,1)}, u32[]{:S(2)}, u32[]{:S(2)}) collective-permute-start(bf16[128,576]{1,0:T(8,128)(2,1)} %collective-permute-done.1.refs_1_), channel_id=1, source_target_pairs={{0,1},{1,0},{2,3},{3,2},{4,5},{5,4},{6,7},{7,6},{8,9},{9,8},{10,11... | collective-permute-start | bytes 442376 | tf_op jit(solution)/shard_map/ppermute | solution.py:215
  46.8 11.2 %collective-permute-start.3 = (bf16[128,576]{1,0:T(8,128)(2,1)}, bf16[128,576]{1,0:T(8,128)(2,1)S(1)}, u32[]{:S(2)}, u32[]{:S(2)}) collective-permute-start(bf16[128,576]{1,0:T(8,128)(2,1)} %shard_map.82.own_ref), channel_id=1, source_target_pairs={{1,29},{3,31},{5,25},{7,27},{9,21},{11,23},{13,17},{15,19},{17,13}... | collective-permute-start | bytes 442376 | tf_op jit(solution)/shard_map/ppermute | solution.py:215
  53.2 6.6 %collective-permute-start.2 = (bf16[128,576]{1,0:T(8,128)(2,1)}, bf16[128,576]{1,0:T(8,128)(2,1)S(1)}, u32[]{:S(2)}, u32[]{:S(2)}) collective-permute-start(bf16[128,576]{1,0:T(8,128)(2,1)} %shard_map.82.own_ref), channel_id=1, source_target_pairs={{0,20},{1,25},{2,22},{3,27},{4,16},{5,29},{6,18},{7,31},{8,28},{9,... | collective-permute-start | bytes 442376 | tf_op jit(solution)/shard_map/ppermute | solution.py:215
  53.4 11.3 %copy-start.1 = (bf16[512,1024]{1,0:T(8,128)(2,1)S(1)}, bf16[512,1024]{1,0:T(8,128)(2,1)}, u32[]{:S(2)}) copy-start(bf16[512,1024]{1,0:T(8,128)(2,1)} %w_ref.5) | copy-start | bytes 3145732
  59.8 3.9 %collective-permute-start.6 = (bf16[128,576]{1,0:T(8,128)(2,1)S(1)}, bf16[128,576]{1,0:T(8,128)(2,1)S(1)}, u32[]{:S(2)}, u32[]{:S(2)}) collective-permute-start(bf16[128,576]{1,0:T(8,128)(2,1)S(1)} %collective-permute-done.2.refs_0_), channel_id=1, source_target_pairs={{0,1},{1,0},{2,3},{3,2},{4,5},{5,4},{6,7},{7,6},{8,9},{9,8},{10,11... | collective-permute-start | bytes 442376 | tf_op jit(solution)/shard_map/ppermute | solution.py:215
  61.9 2.9 %collective-permute-start.7 = (bf16[128,576]{1,0:T(8,128)(2,1)S(1)}, bf16[128,576]{1,0:T(8,128)(2,1)S(1)}, u32[]{:S(2)}, u32[]{:S(2)}) collective-permute-start(bf16[128,576]{1,0:T(8,128)(2,1)S(1)} %collective-permute-done.3.refs_1_), channel_id=1, source_target_pairs={{1,0},{3,2},{5,4},{7,6},{9,8},{11,10},{13,12},{15,14},{17,16},{19,... | collective-permute-start | bytes 442376 | tf_op jit(solution)/shard_map/ppermute | solution.py:215
  67.5 23.7 %copy-start = (bf16[1024,896]{1,0:T(8,128)(2,1)S(1)}, bf16[1024,896]{1,0:T(8,128)(2,1)}, u32[]{:S(2)}) copy-start(bf16[1024,896]{1,0:T(8,128)(2,1)} %refs_6_.7) | copy-start | bytes 5505028
  67.5 6.2 %collective-permute-start.8 = (bf16[64,1024]{1,0:T(8,128)(2,1)S(1)}, bf16[64,1024]{1,0:T(8,128)(2,1)S(1)}, u32[]{:S(2)}, u32[]{:S(2)}) collective-permute-start(bf16[64,1024]{1,0:T(8,128)(2,1)S(1)} %shard_map.85.refs_0_), channel_id=1, source_target_pairs={{0,8},{1,9},{2,10},{3,11},{4,12},{5,13},{6,14},{7,15},{8,0},{9,1},... | collective-permute-start | bytes 393224 | tf_op jit(solution)/shard_map/ppermute | solution.py:215
  72.9 4.5 %collective-permute-start.17 = (bf16[64,1024]{1,0:T(8,128)(2,1)S(1)}, bf16[64,1024]{1,0:T(8,128)(2,1)S(1)}, u32[]{:S(2)}, u32[]{:S(2)}) collective-permute-start(bf16[64,1024]{1,0:T(8,128)(2,1)S(1)} %shard_map.90.refs_0_), channel_id=1, source_target_pairs={{0,8},{1,9},{2,10},{3,11},{4,12},{5,13},{6,14},{7,15},{8,0},{9,1},... | collective-permute-start | bytes 393224 | tf_op jit(solution)/shard_map/ppermute | solution.py:215
  73.0 5.1 %collective-permute-start.10 = (bf16[64,1024]{1,0:T(8,128)(2,1)S(1)}, bf16[64,1024]{1,0:T(8,128)(2,1)S(1)}, u32[]{:S(2)}, u32[]{:S(2)}) collective-permute-start(bf16[64,1024]{1,0:T(8,128)(2,1)S(1)} %shard_map.85.refs_0_), channel_id=1, source_target_pairs={{8,16},{9,17},{10,18},{11,19},{12,20},{13,21},{14,22},{15,23},{16,... | collective-permute-start | bytes 393224 | tf_op jit(solution)/shard_map/ppermute | solution.py:215
  73.7 5.6 %collective-permute-start.9 = (bf16[64,1024]{1,0:T(8,128)(2,1)S(1)}, bf16[64,1024]{1,0:T(8,128)(2,1)S(1)}, u32[]{:S(2)}, u32[]{:S(2)}) collective-permute-start(bf16[64,1024]{1,0:T(8,128)(2,1)S(1)} %collective-permute-done.8.refs_1_), channel_id=1, source_target_pairs={{8,16},{9,17},{10,18},{11,19},{12,20},{13,21},{14,22},{15,23},{16,... | collective-permute-start | bytes 393224 | tf_op jit(solution)/shard_map/ppermute | solution.py:215
  74.4 6.3 %collective-permute-start.19 = (bf16[64,1024]{1,0:T(8,128)(2,1)S(1)}, bf16[64,1024]{1,0:T(8,128)(2,1)S(1)}, u32[]{:S(2)}, u32[]{:S(2)}) collective-permute-start(bf16[64,1024]{1,0:T(8,128)(2,1)S(1)} %shard_map.90.refs_0_), channel_id=1, source_target_pairs={{8,16},{9,17},{10,18},{11,19},{12,20},{13,21},{14,22},{15,23},{16,... | collective-permute-start | bytes 393224 | tf_op jit(solution)/shard_map/ppermute | solution.py:215
  77.3 4.6 %collective-permute-start.18 = (bf16[64,1024]{1,0:T(8,128)(2,1)S(1)}, bf16[64,1024]{1,0:T(8,128)(2,1)S(1)}, u32[]{:S(2)}, u32[]{:S(2)}) collective-permute-start(bf16[64,1024]{1,0:T(8,128)(2,1)S(1)} %collective-permute-done.17.refs_1_), channel_id=1, source_target_pairs={{8,16},{9,17},{10,18},{11,19},{12,20},{13,21},{14,22},{15,23},{16,... | collective-permute-start | bytes 393224 | tf_op jit(solution)/shard_map/ppermute | solution.py:215
  78.0 10.8 %collective-permute-start.11 = (bf16[64,1024]{1,0:T(8,128)(2,1)S(1)}, bf16[64,1024]{1,0:T(8,128)(2,1)S(1)}, u32[]{:S(2)}, u32[]{:S(2)}) collective-permute-start(bf16[64,1024]{1,0:T(8,128)(2,1)S(1)} %collective-permute-done.10.refs_4_), channel_id=1, source_target_pairs={{8,0},{9,1},{10,2},{11,3},{12,4},{13,5},{14,6},{15,7},{16,24},{17,... | collective-permute-start | bytes 393224 | tf_op jit(solution)/shard_map/ppermute | solution.py:215
  79.3 11.9 %collective-permute-start.12 = (bf16[64,1024]{1,0:T(8,128)(2,1)S(1)}, bf16[64,1024]{1,0:T(8,128)(2,1)S(1)}, u32[]{:S(2)}, u32[]{:S(2)}) collective-permute-start(bf16[64,1024]{1,0:T(8,128)(2,1)S(1)} %collective-permute-done.9.refs_2_), channel_id=1, source_target_pairs={{8,0},{9,1},{10,2},{11,3},{12,4},{13,5},{14,6},{15,7},{16,24},{17,... | collective-permute-start | bytes 393224 | tf_op jit(solution)/shard_map/ppermute | solution.py:215
  80.6 16.5 %collective-permute-start.20 = (bf16[64,1024]{1,0:T(8,128)(2,1)S(1)}, bf16[64,1024]{1,0:T(8,128)(2,1)S(1)}, u32[]{:S(2)}, u32[]{:S(2)}) collective-permute-start(bf16[64,1024]{1,0:T(8,128)(2,1)S(1)} %collective-permute-done.19.refs_4_), channel_id=1, source_target_pairs={{8,0},{9,1},{10,2},{11,3},{12,4},{13,5},{14,6},{15,7},{16,24},{17,... | collective-permute-start | bytes 393224 | tf_op jit(solution)/shard_map/ppermute | solution.py:215
  81.9 15.2 %collective-permute-start.21 = (bf16[64,1024]{1,0:T(8,128)(2,1)S(1)}, bf16[64,1024]{1,0:T(8,128)(2,1)S(1)}, u32[]{:S(2)}, u32[]{:S(2)}) collective-permute-start(bf16[64,1024]{1,0:T(8,128)(2,1)S(1)} %collective-permute-done.18.refs_2_), channel_id=1, source_target_pairs={{8,0},{9,1},{10,2},{11,3},{12,4},{13,5},{14,6},{15,7},{16,24},{17,... | collective-permute-start | bytes 393224 | tf_op jit(solution)/shard_map/ppermute | solution.py:215
  92.5 10.8 %collective-permute-start.14 = (bf16[2,2,64,896]{3,2,1,0:T(8,128)(2,1)S(1)}, bf16[2,2,64,896]{3,2,1,0:T(8,128)(2,1)S(1)}, u32[]{:S(2)}, u32[]{:S(2)}) collective-permute-start(bf16[2,2,64,896]{3,2,1,0:T(8,128)(2,1)S(1)} %shard_map.87), channel_id=1, source_target_pairs={{0,1},{1,0},{2,3},{3,2},{4,5},{5,4},{6,7},{7,6},{8,9},{9,8},{10,11... | collective-permute-start | bytes 1376264 | tf_op jit(solution)/shard_map/ppermute | solution.py:215
  98.4 6.8 %collective-permute-start.22 = (bf16[2,2,64,896]{3,2,1,0:T(8,128)(2,1)S(1)}, bf16[2,2,64,896]{3,2,1,0:T(8,128)(2,1)S(1)}, u32[]{:S(2)}, u32[]{:S(2)}) collective-permute-start(bf16[2,2,64,896]{3,2,1,0:T(8,128)(2,1)S(1)} %shard_map.92), channel_id=1, source_target_pairs={{0,1},{1,0},{2,3},{3,2},{4,5},{5,4},{6,7},{7,6},{8,9},{9,8},{10,11... | collective-permute-start | bytes 1376264 | tf_op jit(solution)/shard_map/ppermute | solution.py:215
  103.9 7.2 %collective-permute-start.15 = (bf16[1,2,64,896]{3,2,1,0:T(8,128)(2,1)S(1)}, bf16[1,2,64,896]{3,2,1,0:T(8,128)(2,1)S(1)}, u32[]{:S(2)}, u32[]{:S(2)}) collective-permute-start(bf16[1,2,64,896]{3,2,1,0:T(8,128)(2,1)S(1)} %get-tuple-element.22), channel_id=1, source_target_pairs={{0,2},{1,3},{2,0},{3,1},{4,6},{5,7},{6,4},{7,5},{8,10},{9,11},{10,... | collective-permute-start | bytes 688136 | tf_op jit(solution)/shard_map/ppermute | solution.py:215
  105.9 10.1 %collective-permute-start.23 = (bf16[1,2,64,896]{3,2,1,0:T(8,128)(2,1)S(1)}, bf16[1,2,64,896]{3,2,1,0:T(8,128)(2,1)S(1)}, u32[]{:S(2)}, u32[]{:S(2)}) collective-permute-start(bf16[1,2,64,896]{3,2,1,0:T(8,128)(2,1)S(1)} %get-tuple-element.24), channel_id=1, source_target_pairs={{0,2},{1,3},{2,0},{3,1},{4,6},{5,7},{6,4},{7,5},{8,10},{9,11},{10,... | collective-permute-start | bytes 688136 | tf_op jit(solution)/shard_map/ppermute | solution.py:215
  111.2 8.1 %collective-permute-start.16 = (bf16[2,64,896]{2,1,0:T(8,128)(2,1)S(1)}, bf16[2,64,896]{2,1,0:T(8,128)(2,1)S(1)}, u32[]{:S(2)}, u32[]{:S(2)}) collective-permute-start(bf16[2,64,896]{2,1,0:T(8,128)(2,1)S(1)} %shard_map.89), channel_id=1, source_target_pairs={{0,0},{1,16},{2,8},{3,24},{4,4},{5,20},{6,12},{7,28},{8,1},{9,17},... | collective-permute-start | bytes 688136 | tf_op jit(solution)/shard_map/ppermute | solution.py:215
  116.1 11.4 %collective-permute-start.24 = (bf16[2,64,896]{2,1,0:T(8,128)(2,1)S(1)}, bf16[2,64,896]{2,1,0:T(8,128)(2,1)S(1)}, u32[]{:S(2)}, u32[]{:S(2)}) collective-permute-start(bf16[2,64,896]{2,1,0:T(8,128)(2,1)S(1)} %shard_map.94), channel_id=1, source_target_pairs={{0,8},{1,24},{2,0},{3,16},{4,12},{5,28},{6,4},{7,20},{8,9},{9,25},... | collective-permute-start | bytes 688136 | tf_op jit(solution)/shard_map/ppermute | solution.py:215
  (1 other events, 0.7 us)

commit v2 on v1

--- a/solution.py
+++ b/solution.py
@@ -118,54 +118,68 @@
             ).astype(jnp.bfloat16)
 
 
-def project_kernel(zs, xs, kept, place_ref, *refs):
-    blocks, weights, out_ref = refs[: zs + 2], refs[zs + 2 : -1], refs[-1]
+def ring_place(z, zs):
+    return jnp.where(z % 2 == 1, (z + 1) // 2, (zs - z // 2) % zs)
+
+
+def ring_member(at, zs):
+    return jnp.where(at > zs // 2, 2 * (zs - at), jnp.maximum(2 * at - 1, 0))
+
+
+def project_kernel(zs, kept, place_ref, w_ref, *refs):
+    blocks, out_ref, tokens = refs[:-2], refs[-2], refs[-1]
     zl = zs // 2
     k = place_ref[1]
-    z = place_ref[2]
+    half = blocks[0].shape[0]
+    rows = half * len(blocks) // zs
+    for i, block in enumerate(blocks):
+        span, step = divmod(i, zs)
+        member = ring_member((ring_place(place_ref[2], zs) + zs - step) % zs, zs)
+        tokens[pl.ds(pl.multiple_of(member * rows + span * half, half), half), :] = block[...]
+    side = k if kept else 1 - k
+    these = tokens[pl.ds(pl.multiple_of(side * (zl * rows), zl * rows), zl * rows), :]
+    part = jnp.dot(these, w_ref[...], preferred_element_type=jnp.float32)
+    out_ref[...] = part.astype(out_ref.dtype).reshape(out_ref.shape)
+
+
+def halve_kernel(bit, turn, place_ref, mine_ref, *refs):
+    got_refs, keep_ref, away_refs = refs[:-3], refs[-3], refs[-2:]
+    half = away_refs[0].shape[1]
+    for span, away_ref in enumerate(away_refs):
+        these = slice(span * half, (span + 1) * half)
+        low = ((place_ref[4 + (turn + span) % 2] // bit) % 2) == 0
+
+        def total(d):
+            if len(got_refs) == 1:
+                got = got_refs[0][d, these]
+            else:
+                got = got_refs[span][d]
+            return mine_ref[d, these] + got.astype(jnp.float32)
+
+        for d in range(bit):
+            a = total(d)
+            b = total(d + bit)
+            keep_ref[d, these] = jnp.where(low, a, b)
+            away_ref[d] = jnp.where(low, b, a).astype(away_ref.dtype)
+
+
+def add_kernel(span, mine_ref, got_ref, out_ref):
+    half = out_ref.shape[0]
+    mine = mine_ref[0, span * half : (span + 1) * half]
+    out_ref[...] = (mine + got_ref[0].astype(jnp.float32)).astype(out_ref.dtype)
+
+
+def output_kernel(place_ref, *refs):
+    blocks, out_ref = refs[:-1], refs[-1]
+    xs = len(blocks) // 2
     x = place_ref[3]
-    inner = (z % 4 == 1) | (z % 4 == 2)
-    low_half = (k ^ (z // zl)) == 0 if kept else (k ^ (z // zl)) == 1
-
-    def block(d):
-        if d < 2:
-            return blocks[d][...]
-        if d < 4:
-            at = 2 * d - 2
-            return jnp.where(inner, blocks[at][...], blocks[at + 1][...])
-        return blocks[d + 2][...]
-
-    rows = blocks[0].shape[0]
-    tokens = jnp.concatenate(
-        [jnp.where(low_half, block(d), block(d + zl)) for d in range(zl)], axis=0
-    )
-    for dx in range(xs):
-        part = jnp.dot(tokens, weights[dx][...], preferred_element_type=jnp.float32)
-        part = part.astype(out_ref.dtype).reshape(zl, rows, -1)
-        for d in range(zl):
-            out_ref[d, x ^ dx] = part[d]
-
-
-def halve_kernel(bit, span, place_ref, mine_ref, got_ref, keep_ref, away_ref):
-    which = place_ref[4 + span]
-    low = ((which // bit) % 2) == 0
-    for d in range(bit):
-        a = mine_ref[d] + got_ref[d].astype(jnp.float32)
-        b = mine_ref[d + bit] + got_ref[d + bit].astype(jnp.float32)
-        keep_ref[d] = jnp.where(low, a, b)
-        away_ref[d] = jnp.where(low, b, a).astype(away_ref.dtype)
-
-
-def add_kernel(mine_ref, got_ref, out_ref):
-    out_ref[...] = (mine_ref[0] + got_ref[0].astype(jnp.float32)).astype(out_ref.dtype)
-
-
-def output_kernel(*refs):
-    out_ref = refs[-1]
-    for span, ref in enumerate(refs[:-1]):
-        xs, half, cols = ref.shape
-        for i in range(xs):
-            out_ref[span * half : (span + 1) * half, i * cols : (i + 1) * cols] = ref[i]
+    half, cols = blocks[0].shape
+    for i in range(xs):
+        for span in range(2):
+            block = blocks[span][...]
+            for dx in range(1, xs):
+                block = jnp.where((x ^ i) == dx, blocks[2 * dx + span][...], block)
+            out_ref[span * half : (span + 1) * half, i * cols : (i + 1) * cols] = block
 
 
 def whole():
@@ -201,7 +215,7 @@
     c = lax.axis_index("ctx")
     h = lax.axis_index("head")
     k, y, z, x = h % 2, h // 2, c // xs, c % xs
-    place = jnp.stack([c, k, z, x, y ^ (z % zl), y ^ (z % zl) ^ (zl - 1)]).astype(jnp.int32)
+    place = jnp.stack([c, k, z, x, y, y ^ (zl - 1)]).astype(jnp.int32)
     bf16, f32 = jnp.bfloat16, jnp.float32
 
     def send(value, where):
@@ -214,7 +228,7 @@
                     pairs.append((ci * head_n + hi, (tz * xs + tx) * head_n + ty * 2 + tk))
         return lax.ppermute(value, AXES, pairs)
 
-    keys = call(key_kernel, ((rows, LAT + ROPE), bf16), (latent, k_rope.T), vmem=4)
+    keys = call(key_kernel, ((rows, LAT + ROPE), bf16), (latent, k_rope.T), vmem=60)
     pairs = [(d, d + 1) for d in range(1, ctx_n - 1, 2)] + [(None, ctx_n - 1)]
 
     def across(pair):
@@ -227,8 +241,8 @@
     def to_other(pair):
         return lambda z, x, y, k: (z, x, y, 1 - k) if pair[k] is not None else None
 
-    def inner_only(where):
-        return lambda z, x, y, k: where(z, x, y, k) if z % 4 in (1, 2) else None
+    ring = [0, *range(1, zs, 2), *range(zs - 2, 0, -2)]
+    following = {z: ring[(i + 1) % zs] for i, z in enumerate(ring)}
 
     direct = []
     for pair in pairs:
@@ -240,6 +254,7 @@
         query_kernel,
         ((heads, rows, LAT + ROPE), bf16),
         (q_nope, q_rope, w_uk),
+        vmem=60,
         flops=2 * rows * heads * NOPE * LAT,
     )
     first = len(pairs) // 2
@@ -263,9 +278,8 @@
     )
     direct[first:], early = lax.optimization_barrier((direct[first:], early))
     passed += [send(direct[i], to_other(pairs[i])) for i in range(first, len(pairs))]
-    results = []
+    blocks = []
     for span in range(2):
-        flip = span * (zl - 1)
         heads_out = call(
             functools.partial(late_kernel, pairs[first:], 4, scale, span),
             ((half, heads * VDIM), bf16),
@@ -276,42 +290,50 @@
             flops=work(half, n_late * rows) + 2 * half * heads * LAT * VDIM,
             exps=half * heads * n_late * rows,
         )
-        beside = send(heads_out, lambda z, x, y, k: (z ^ 1, x, y, k))
-        middle = send(heads_out, inner_only(lambda z, x, y, k: (z ^ 3, x, y, k)))
-        outer_2 = send(middle, inner_only(lambda z, x, y, k: (z ^ 1, x, y, k)))
-        inner_2 = send(beside, inner_only(lambda z, x, y, k: (z ^ 3, x, y, k)))
-        outer_3 = send(inner_2, inner_only(lambda z, x, y, k: (z ^ 1, x, y, k)))
-        along = [heads_out, beside, inner_2, outer_2, middle, outer_3]
-        along += [
-            send(heads_out, lambda z, x, y, k: (z ^ d, x, y, k)) for d in range(4, zs)
-        ]
+        along = [heads_out]
+        for _ in range(1, zs):
+            along.append(send(along[-1], lambda z, x, y, k: (following[z], x, y, k)))
+        blocks += along
+
+    results = []
+    for dx in range(xs):
+        turn = dx % 2
+        if dx:
+            matrices[dx], mine = lax.optimization_barrier((matrices[dx], mine))
 
         def project(kept, kind):
             return call(
-                functools.partial(project_kernel, zs, xs, kept),
-                ((zl, xs, half, cols), kind),
-                (place, *along, *matrices),
+                functools.partial(project_kernel, zs, kept),
+                ((zl, rows, cols), kind),
+                (place, matrices[dx], *blocks),
                 smem=1,
-                flops=2 * zl * half * depth * xs * cols,
+                scratch=(pltpu.VMEM((zs * rows, depth), bf16),),
+                flops=2 * zl * rows * depth * cols,
             )
 
         away = project(False, bf16)
-        got = send(away, lambda z, x, y, k: (z, x, y, 1 - k))
+        got = [send(away, lambda z, x, y, k: (z, x, y, 1 - k))]
         mine = project(True, f32)
         bit = zl // 2
         while bit:
-            block = (bit, xs, half, cols)
-            mine, away = call(
-                functools.partial(halve_kernel, bit, span),
-                [(block, f32), (block, bf16)],
-                (place, mine, got),
+            part = ((bit, half, cols), bf16)
+            mine, *away = call(
+                functools.partial(halve_kernel, bit, turn),
+                [((bit, rows, cols), f32), part, part],
+                (place, mine, *got),
                 smem=1,
             )
-            got = send(away, lambda z, x, y, k: (z, x, y ^ bit, k))
+            got = [send(value, lambda z, x, y, k: (z, x, y ^ bit, k)) for value in away]
             bit //= 2
-        block = call(add_kernel, ((xs, half, cols), bf16), (mine, got))
-        results.append(send(block, lambda z, x, y, k: (k * zl + (y ^ flip), x, z // 2, z % 2)))
-    return call(output_kernel, ((rows, xs * cols), bf16), tuple(results))
+        for span in range(2):
+            block = call(
+                functools.partial(add_kernel, span), ((half, cols), bf16), (mine, got[span])
+            )
+            flip = (turn + span) % 2 * (zl - 1)
+            results.append(
+                send(block, lambda z, x, y, k: (k * zl + (y ^ flip), x, z // 2, z % 2))
+            )
+    return call(output_kernel, ((rows, xs * cols), bf16), (place, *results), smem=1)
 
 
 def solution(mesh):

time: 129 us -> 122 us (0.946)
  the two profiles are of different devices: /device:TPU:1 before, /device:TPU:24 now
where the time goes in v2:
time: 122 us
  waiting for transfers between devices  78.9 us (65%)
  Pallas kernels  21.6 us (18%)
  starting transfers between devices  19.7 us (16%)
  local copies, waits for them, and re-layouts  1.41 us (1%)
    ppermute x25, waiting for transfers between devices, send(): return lax.ppermute(value, AXES, pairs)  78.9 us
    pallas_call x16, Pallas kernels, call(): pl.pallas_call(kernel, out_shape=shapes, in_specs=[pl.BlockSpec(memory_sp...  21.6 us
    ppermute x25, starting transfers between devices, send(): return lax.ppermute(value, AXES, pairs)  19.7 us
  transfers between devices with their start and end apart: 25, of which 16 were waited for; matrix products, arithmetic and copies ran while one was open for 0% of the time, Pallas kernels for 16%

profile of v2, /device:TPU:24, one launch (start us, length us, event | category | flops | bytes accessed | tf_op | source)
XLA Modules:
  0.0 121.9 jit_solution(10993087478616581386)
XLA Ops:
  0.0 1.5 %collective-permute-start.19 = (bf16[1024,896]{1,0:T(8,128)(2,1)}, bf16[1024,896]{1,0:T(8,128)(2,1)S(1)}, u32[]{:S(2)}, u32[]{:S(2)}) collective-permute-start(bf16[1024,896]{1,0:T(8,128)(2,1)} %w_ref.9), channel_id=1, source_target_pairs={{0,4},{1,5},{2,6},{3,7},{4,0},{5,1},{6,2},{7,3},{8,12},{9,13},{10,... | collective-permute-start | bytes 5505032 | tf_op jit(solution)/shard_map/ppermute | solution.py:229
  1.5 1.6 %shard_map.82.own_ref = bf16[128,576]{1,0:T(8,128)(2,1)} custom-call(bf16[128,512]{1,0:T(8,128)(2,1)} %latent_ref.1, bf16[64,128]{1,0:T(8,128)(2,1)} %bitcast.7), custom_call_target="tpu_custom_call" | custom-call | bytes 294912 | tf_op jit(solution)/shard_map/pallas_call | solution.py:194
  3.6 1.5 %collective-permute-start = (bf16[128,576]{1,0:T(8,128)(2,1)}, bf16[128,576]{1,0:T(8,128)(2,1)S(1)}, u32[]{:S(2)}, u32[]{:S(2)}) collective-permute-start(bf16[128,576]{1,0:T(8,128)(2,1)} %shard_map.82.own_ref), channel_id=1, source_target_pairs={{0,4},{1,9},{2,6},{3,11},{4,0},{5,13},{6,2},{7,15},{8,12},{9,1},{1... | collective-permute-start | bytes 442376 | tf_op jit(solution)/shard_map/ppermute | solution.py:229
  5.1 2.9 %shard_map.83.q_ref = bf16[8,128,576]{2,1,0:T(8,128)(2,1)} custom-call(bf16[128,1024]{1,0:T(8,128)(2,1)} %q_ref.1, bf16[128,512]{1,0:T(8,128)(2,1)} %rope_ref.1, bf16[512,1024]{1,0:T(8,128)(2,1)} %w_ref.5), custom_call_target="tpu_custom_call" | custom-call | flops 134217728 | bytes 2621440 | tf_op jit(solution)/shard_map/pallas_call | solution.py:194
  8.0 3.3 %collective-permute-done.1.refs_1_ = bf16[128,576]{1,0:T(8,128)(2,1)S(1)} collective-permute-done((bf16[128,576]{1,0:T(8,128)(2,1)}, bf16[128,576]{1,0:T(8,128)(2,1)S(1)}, u32[]{:S(2)}, u32[]{:S(2)}) %collective-permute-start.1) | collective-permute-done | bytes 147488 | tf_op jit(solution)/shard_map/ppermute | solution.py:229
  11.3 34.2 %collective-permute-done.refs_0_ = bf16[128,576]{1,0:T(8,128)(2,1)S(1)} collective-permute-done((bf16[128,576]{1,0:T(8,128)(2,1)}, bf16[128,576]{1,0:T(8,128)(2,1)S(1)}, u32[]{:S(2)}, u32[]{:S(2)}) %collective-permute-start) | collective-permute-done | bytes 147488 | tf_op jit(solution)/shard_map/ppermute | solution.py:229
  46.7 1.3 %collective-permute-start.2 = (bf16[128,576]{1,0:T(8,128)(2,1)S(1)}, bf16[128,576]{1,0:T(8,128)(2,1)S(1)}, u32[]{:S(2)}, u32[]{:S(2)}) collective-permute-start(bf16[128,576]{1,0:T(8,128)(2,1)S(1)} %copy-done.3), channel_id=1, source_target_pairs={{0,20},{1,25},{2,22},{3,27},{4,16},{5,29},{6,18},{7,31},{8,28},{9,... | collective-permute-start | bytes 442376 | tf_op jit(solution)/shard_map/ppermute | solution.py:229
  48.1 1.3 %copy-done = bf16[8,128,576]{2,1,0:T(8,128)(2,1)S(1)} copy-done((bf16[8,128,576]{2,1,0:T(8,128)(2,1)S(1)}, bf16[8,128,576]{2,1,0:T(8,128)(2,1)}, u32[]{:S(2)}) %copy-start) | copy-done | bytes 1179672
  49.4 3.7 %shard_map.84.early_ref = f32[8,128,640]{2,1,0:T(8,128)S(1)} custom-call(s32[16]{0:T(128)S(1)} %copy-done.4, s32[6]{0:T(128)S(1)} %stack.27.place_ref, bf16[8,128,576]{2,1,0:T(8,128)(2,1)S(1)} %copy-done, bf16[128,576]{1,0:T(8,128)(2,1)S(1)} %copy-done.3, bf16[128,576]{1,0:T(8,128)(2,1)S(1)} %collective-permute-done.refs_0_, ...), custom_call_target="tpu_custom_call" | custom-call | flops 1426063360 | bytes 4538456 | tf_op jit(solution)/shard_map/pallas_call | solution.py:194
  53.2 7.7 %collective-permute-done.2.refs_0_ = bf16[128,576]{1,0:T(8,128)(2,1)S(1)} collective-permute-done((bf16[128,576]{1,0:T(8,128)(2,1)S(1)}, bf16[128,576]{1,0:T(8,128)(2,1)S(1)}, u32[]{:S(2)}, u32[]{:S(2)}) %collective-permute-start.2) | collective-permute-done | bytes 147488 | tf_op jit(solution)/shard_map/ppermute | solution.py:229
  62.2 1.9 %collective-permute-done.7.refs_3_ = bf16[128,576]{1,0:T(8,128)(2,1)S(1)} collective-permute-done((bf16[128,576]{1,0:T(8,128)(2,1)S(1)}, bf16[128,576]{1,0:T(8,128)(2,1)S(1)}, u32[]{:S(2)}, u32[]{:S(2)}) %collective-permute-start.7) | collective-permute-done | bytes 147488 | tf_op jit(solution)/shard_map/ppermute | solution.py:229
  64.1 2.6 %shard_map.85.refs_0_ = bf16[64,1024]{1,0:T(8,128)(2,1)S(1)} custom-call(s32[16]{0:T(128)S(1)} %copy-done.4, s32[6]{0:T(128)S(1)} %stack.27.place_ref, bf16[8,128,576]{2,1,0:T(8,128)(2,1)S(1)} %copy-done, bf16[512,1024]{1,0:T(8,128)(2,1)S(1)} %copy-done.2, f32[8,128,640]{2,1,0:T(8,128)S(1)} %shard_map.84.early_ref, ...), custom_call_target="tpu_custom_call" | custom-call | flops 494927872 | bytes 5570648 | tf_op jit(solution)/shard_map/pallas_call | solution.py:194
  66.8 1.4 %collective-permute-start.8 = (bf16[64,1024]{1,0:T(8,128)(2,1)S(1)}, bf16[64,1024]{1,0:T(8,128)(2,1)S(1)}, u32[]{:S(2)}, u32[]{:S(2)}) collective-permute-start(bf16[64,1024]{1,0:T(8,128)(2,1)S(1)} %shard_map.85.refs_0_), channel_id=1, source_target_pairs={{0,8},{1,9},{2,10},{3,11},{4,12},{5,13},{6,14},{7,15},{8,24},{9,25... | collective-permute-start | bytes 393224 | tf_op jit(solution)/shard_map/ppermute | solution.py:229
  68.2 2.6 %shard_map.86.refs_4_ = bf16[64,1024]{1,0:T(8,128)(2,1)S(1)} custom-call(s32[16]{0:T(128)S(1)} %copy-done.4, s32[6]{0:T(128)S(1)} %stack.27.place_ref, bf16[8,128,576]{2,1,0:T(8,128)(2,1)S(1)} %copy-done, bf16[512,1024]{1,0:T(8,128)(2,1)S(1)} %copy-done.2, f32[8,128,640]{2,1,0:T(8,128)S(1)} %shard_map.84.early_ref, ...), custom_call_target="tpu_custom_call" | custom-call | flops 494927872 | bytes 5570648 | tf_op jit(solution)/shard_map/pallas_call | solution.py:194
  70.9 2.4 %collective-permute-done.8.refs_1_ = bf16[64,1024]{1,0:T(8,128)(2,1)S(1)} collective-permute-done((bf16[64,1024]{1,0:T(8,128)(2,1)S(1)}, bf16[64,1024]{1,0:T(8,128)(2,1)S(1)}, u32[]{:S(2)}, u32[]{:S(2)}) %collective-permute-start.8) | collective-permute-done | bytes 131104 | tf_op jit(solution)/shard_map/ppermute | solution.py:229
  73.8 4.1 %collective-permute-done.11.refs_5_ = bf16[64,1024]{1,0:T(8,128)(2,1)S(1)} collective-permute-done((bf16[64,1024]{1,0:T(8,128)(2,1)S(1)}, bf16[64,1024]{1,0:T(8,128)(2,1)S(1)}, u32[]{:S(2)}, u32[]{:S(2)}) %collective-permute-start.11) | collective-permute-done | bytes 131104 | tf_op jit(solution)/shard_map/ppermute | solution.py:229
  77.9 2.2 %collective-permute-done.9.refs_2_ = bf16[64,1024]{1,0:T(8,128)(2,1)S(1)} collective-permute-done((bf16[64,1024]{1,0:T(8,128)(2,1)S(1)}, bf16[64,1024]{1,0:T(8,128)(2,1)S(1)}, u32[]{:S(2)}, u32[]{:S(2)}) %collective-permute-start.9) | collective-permute-done | bytes 131104 | tf_op jit(solution)/shard_map/ppermute | solution.py:229
  80.1 5.0 %collective-permute-done.12.refs_6_ = bf16[64,1024]{1,0:T(8,128)(2,1)S(1)} collective-permute-done((bf16[64,1024]{1,0:T(8,128)(2,1)S(1)}, bf16[64,1024]{1,0:T(8,128)(2,1)S(1)}, u32[]{:S(2)}, u32[]{:S(2)}) %collective-permute-start.12) | collective-permute-done | bytes 131104 | tf_op jit(solution)/shard_map/ppermute | solution.py:229
  85.1 2.8 %collective-permute-done.10.refs_3_ = bf16[64,1024]{1,0:T(8,128)(2,1)S(1)} collective-permute-done((bf16[64,1024]{1,0:T(8,128)(2,1)S(1)}, bf16[64,1024]{1,0:T(8,128)(2,1)S(1)}, u32[]{:S(2)}, u32[]{:S(2)}) %collective-permute-start.10) | collective-permute-done | bytes 131104 | tf_op jit(solution)/shard_map/ppermute | solution.py:229
  87.9 3.1 %collective-permute-done.13.refs_7_ = bf16[64,1024]{1,0:T(8,128)(2,1)S(1)} collective-permute-done((bf16[64,1024]{1,0:T(8,128)(2,1)S(1)}, bf16[64,1024]{1,0:T(8,128)(2,1)S(1)}, u32[]{:S(2)}, u32[]{:S(2)}) %collective-permute-start.13) | collective-permute-done | bytes 131104 | tf_op jit(solution)/shard_map/ppermute | solution.py:229
  91.0 1.3 %shard_map.88 = bf16[2,128,896]{2,1,0:T(8,128)(2,1)S(1)} custom-call(s32[6]{0:T(128)S(1)} %stack.27.place_ref, bf16[1024,896]{1,0:T(8,128)(2,1)S(1)} %copy-done.1, bf16[64,1024]{1,0:T(8,128)(2,1)S(1)} %shard_map.85.refs_0_, bf16[64,1024]{1,0:T(8,128)(2,1)S(1)} %collective-permute-done.8.refs_1_, bf16[64,1024]{1,0:T(8,128)(2,1)S(1)} %collective-permute-done.9.refs_2_, ...), custom_call_target="tpu_custom_call" | custom-call | flops 469762048 | bytes 3342360 | tf_op jit(solution)/shard_map/pallas_call | solution.py:194
  92.4 1.3 %shard_map.87.mine_ref = f32[2,128,896]{2,1,0:T(8,128)S(1)} custom-call(s32[6]{0:T(128)S(1)} %stack.27.place_ref, bf16[1024,896]{1,0:T(8,128)(2,1)S(1)} %copy-done.1, bf16[64,1024]{1,0:T(8,128)(2,1)S(1)} %shard_map.85.refs_0_, bf16[64,1024]{1,0:T(8,128)(2,1)S(1)} %collective-permute-done.8.refs_1_, bf16[64,1024]{1,0:T(8,128)(2,1)S(1)} %collective-permute-done.9.refs_2_, ...), custom_call_target="tpu_custom_call" | custom-call | flops 469762048 | bytes 3801112 | tf_op jit(solution)/shard_map/pallas_call | solution.py:194
  94.9 1.3 %shard_map.93 = bf16[2,128,896]{2,1,0:T(8,128)(2,1)S(1)} custom-call(s32[6]{0:T(128)S(1)} %stack.27.place_ref, bf16[1024,896]{1,0:T(8,128)(2,1)S(1)} %collective-permute-done.19.w_ref, bf16[64,1024]{1,0:T(8,128)(2,1)S(1)} %shard_map.85.refs_0_, bf16[64,1024]{1,0:T(8,128)(2,1)S(1)} %collective-permute-done.8.refs_1_, ...), custom_call_target="tpu_custom_call" | custom-call | flops 469762048 | bytes 3342360 | tf_op jit(solution)/shard_map/pallas_call | solution.py:194
  96.4 1.6 %collective-permute-start.15 = (bf16[1,64,896]{2,1,0:T(8,128)(2,1)S(1)}, bf16[1,64,896]{2,1,0:T(8,128)(2,1)S(1)}, u32[]{:S(2)}, u32[]{:S(2)}) collective-permute-start(bf16[1,64,896]{2,1,0:T(8,128)(2,1)S(1)} %get-tuple-element.25), channel_id=1, source_target_pairs={{0,2},{1,3},{2,0},{3,1},{4,6},{5,7},{6,4},{7,5},{8,10},{9,11},{10,... | collective-permute-start | bytes 344072 | tf_op jit(solution)/shard_map/ppermute | solution.py:229
  98.4 1.3 %shard_map.92.mine_ref = f32[2,128,896]{2,1,0:T(8,128)S(1)} custom-call(s32[6]{0:T(128)S(1)} %stack.27.place_ref, bf16[1024,896]{1,0:T(8,128)(2,1)S(1)} %collective-permute-done.19.w_ref, bf16[64,1024]{1,0:T(8,128)(2,1)S(1)} %shard_map.85.refs_0_, bf16[64,1024]{1,0:T(8,128)(2,1)S(1)} %collective-permute-done.8.refs_1_, ...), custom_call_target="tpu_custom_call" | custom-call | flops 469762048 | bytes 3801112 | tf_op jit(solution)/shard_map/pallas_call | solution.py:194
  100.4 1.6 %collective-permute-start.21 = (bf16[1,64,896]{2,1,0:T(8,128)(2,1)S(1)}, bf16[1,64,896]{2,1,0:T(8,128)(2,1)S(1)}, u32[]{:S(2)}, u32[]{:S(2)}) collective-permute-start(bf16[1,64,896]{2,1,0:T(8,128)(2,1)S(1)} %get-tuple-element.29), channel_id=1, source_target_pairs={{0,2},{1,3},{2,0},{3,1},{4,6},{5,7},{6,4},{7,5},{8,10},{9,11},{10,... | collective-permute-start | bytes 344072 | tf_op jit(solution)/shard_map/ppermute | solution.py:229
  102.6 2.0 %collective-permute-start.16 = (bf16[64,896]{1,0:T(8,128)(2,1)S(1)}, bf16[64,896]{1,0:T(8,128)(2,1)S(1)}, u32[]{:S(2)}, u32[]{:S(2)}) collective-permute-start(bf16[64,896]{1,0:T(8,128)(2,1)S(1)} %shard_map.90), channel_id=1, source_target_pairs={{0,0},{1,16},{2,8},{3,24},{4,4},{5,20},{6,12},{7,28},{8,1},{9,17},... | collective-permute-start | bytes 344072 | tf_op jit(solution)/shard_map/ppermute | solution.py:229
  104.9 2.1 %collective-permute-start.18 = (bf16[64,896]{1,0:T(8,128)(2,1)S(1)}, bf16[64,896]{1,0:T(8,128)(2,1)S(1)}, u32[]{:S(2)}, u32[]{:S(2)}) collective-permute-start(bf16[64,896]{1,0:T(8,128)(2,1)S(1)} %shard_map.91), channel_id=1, source_target_pairs={{0,8},{1,24},{2,0},{3,16},{4,12},{5,28},{6,4},{7,20},{8,9},{9,25},... | collective-permute-start | bytes 344072 | tf_op jit(solution)/shard_map/ppermute | solution.py:229
  107.5 4.2 %collective-permute-done.23.got_ref = bf16[1,64,896]{2,1,0:T(8,128)(2,1)S(1)} collective-permute-done((bf16[1,64,896]{2,1,0:T(8,128)(2,1)S(1)}, bf16[1,64,896]{2,1,0:T(8,128)(2,1)S(1)}, u32[]{:S(2)}, u32[]{:S(2)}) %collective-permute-start.23) | collective-permute-done | bytes 114720 | tf_op jit(solution)/shard_map/ppermute | solution.py:229
  111.7 1.9 %collective-permute-start.24 = (bf16[64,896]{1,0:T(8,128)(2,1)S(1)}, bf16[64,896]{1,0:T(8,128)(2,1)S(1)}, u32[]{:S(2)}, u32[]{:S(2)}) collective-permute-start(bf16[64,896]{1,0:T(8,128)(2,1)S(1)} %shard_map.96), channel_id=1, source_target_pairs={{0,0},{1,16},{2,8},{3,24},{4,4},{5,20},{6,12},{7,28},{8,1},{9,17},... | collective-permute-start | bytes 344072 | tf_op jit(solution)/shard_map/ppermute | solution.py:229
  113.7 6.8 %collective-permute-done.24.refs_3_ = bf16[64,896]{1,0:T(8,128)(2,1)S(1)} collective-permute-done((bf16[64,896]{1,0:T(8,128)(2,1)S(1)}, bf16[64,896]{1,0:T(8,128)(2,1)S(1)}, u32[]{:S(2)}, u32[]{:S(2)}) %collective-permute-start.24) | collective-permute-done | bytes 114720 | tf_op jit(solution)/shard_map/ppermute | solution.py:229
  120.5 1.4 %shard_map.97 = bf16[128,1792]{1,0:T(8,128)(2,1)} custom-call(s32[6]{0:T(128)S(1)} %stack.27.place_ref, bf16[64,896]{1,0:T(8,128)(2,1)S(1)} %collective-permute-done.16.refs_0_, bf16[64,896]{1,0:T(8,128)(2,1)S(1)} %collective-permute-done.18.refs_1_, bf16[64,896]{1,0:T(8,128)(2,1)S(1)} %collective-permute-done.22.refs_2_, ...), custom_call_target="tpu_custom_call" | custom-call | bytes 917528 | tf_op jit(solution)/shard_map/pallas_call | solution.py:194
  (45 shorter events, 7.5 us)
Async XLA Ops:
  0.0 48.1 %copy-start.4 = (s32[16]{0:T(128)S(1)}, s32[16]{0:T(128)}, u32[]{:S(2)}) copy-start(s32[16]{0:T(128)} %order_ref.5) | copy-start | bytes 196
  0.0 94.9 %collective-permute-start.19 = (bf16[1024,896]{1,0:T(8,128)(2,1)}, bf16[1024,896]{1,0:T(8,128)(2,1)S(1)}, u32[]{:S(2)}, u32[]{:S(2)}) collective-permute-start(bf16[1024,896]{1,0:T(8,128)(2,1)} %w_ref.9), channel_id=1, source_target_pairs={{0,4},{1,5},{2,6},{3,7},{4,0},{5,1},{6,2},{7,3},{8,12},{9,13},{10,... | collective-permute-start | bytes 5505032 | tf_op jit(solution)/shard_map/ppermute | solution.py:229
  3.1 42.9 %copy-start.3 = (bf16[128,576]{1,0:T(8,128)(2,1)S(1)}, bf16[128,576]{1,0:T(8,128)(2,1)}, u32[]{:S(2)}) copy-start(bf16[128,576]{1,0:T(8,128)(2,1)} %shard_map.82.own_ref) | copy-start | bytes 442372
  3.1 8.2 %collective-permute-start.1 = (bf16[128,576]{1,0:T(8,128)(2,1)}, bf16[128,576]{1,0:T(8,128)(2,1)S(1)}, u32[]{:S(2)}, u32[]{:S(2)}) collective-permute-start(bf16[128,576]{1,0:T(8,128)(2,1)} %shard_map.82.own_ref), channel_id=1, source_target_pairs={{0,12},{1,17},{2,14},{3,19},{4,8},{5,21},{6,10},{7,23},{8,4},{9,25... | collective-permute-start | bytes 442376 | tf_op jit(solution)/shard_map/ppermute | solution.py:229
  3.6 41.9 %collective-permute-start = (bf16[128,576]{1,0:T(8,128)(2,1)}, bf16[128,576]{1,0:T(8,128)(2,1)S(1)}, u32[]{:S(2)}, u32[]{:S(2)}) collective-permute-start(bf16[128,576]{1,0:T(8,128)(2,1)} %shard_map.82.own_ref), channel_id=1, source_target_pairs={{0,4},{1,9},{2,6},{3,11},{4,0},{5,13},{6,2},{7,15},{8,12},{9,1},{1... | collective-permute-start | bytes 442376 | tf_op jit(solution)/shard_map/ppermute | solution.py:229
  45.5 2.6 %collective-permute-start.4 = (bf16[128,576]{1,0:T(8,128)(2,1)S(1)}, bf16[128,576]{1,0:T(8,128)(2,1)S(1)}, u32[]{:S(2)}, u32[]{:S(2)}) collective-permute-start(bf16[128,576]{1,0:T(8,128)(2,1)S(1)} %collective-permute-done.refs_0_), channel_id=1, source_target_pairs={{0,1},{1,0},{2,3},{3,2},{4,5},{5,4},{6,7},{7,6},{8,9},{9,8},{10,11... | collective-permute-start | bytes 442376 | tf_op jit(solution)/shard_map/ppermute | solution.py:229
  45.5 2.6 %collective-permute-start.5 = (bf16[128,576]{1,0:T(8,128)(2,1)S(1)}, bf16[128,576]{1,0:T(8,128)(2,1)S(1)}, u32[]{:S(2)}, u32[]{:S(2)}) collective-permute-start(bf16[128,576]{1,0:T(8,128)(2,1)S(1)} %collective-permute-done.1.refs_1_), channel_id=1, source_target_pairs={{0,1},{1,0},{2,3},{3,2},{4,5},{5,4},{6,7},{7,6},{8,9},{9,8},{10,11... | collective-permute-start | bytes 442376 | tf_op jit(solution)/shard_map/ppermute | solution.py:229
  46.0 7.2 %collective-permute-start.3 = (bf16[128,576]{1,0:T(8,128)(2,1)S(1)}, bf16[128,576]{1,0:T(8,128)(2,1)S(1)}, u32[]{:S(2)}, u32[]{:S(2)}) collective-permute-start(bf16[128,576]{1,0:T(8,128)(2,1)S(1)} %copy-done.3), channel_id=1, source_target_pairs={{1,29},{3,31},{5,25},{7,27},{9,21},{11,23},{13,17},{15,19},{17,13}... | collective-permute-start | bytes 442376 | tf_op jit(solution)/shard_map/ppermute | solution.py:229
  46.7 14.2 %collective-permute-start.2 = (bf16[128,576]{1,0:T(8,128)(2,1)S(1)}, bf16[128,576]{1,0:T(8,128)(2,1)S(1)}, u32[]{:S(2)}, u32[]{:S(2)}) collective-permute-start(bf16[128,576]{1,0:T(8,128)(2,1)S(1)} %copy-done.3), channel_id=1, source_target_pairs={{0,20},{1,25},{2,22},{3,27},{4,16},{5,29},{6,18},{7,31},{8,28},{9,... | collective-permute-start | bytes 442376 | tf_op jit(solution)/shard_map/ppermute | solution.py:229
  48.1 1.3 %copy-start = (bf16[8,128,576]{2,1,0:T(8,128)(2,1)S(1)}, bf16[8,128,576]{2,1,0:T(8,128)(2,1)}, u32[]{:S(2)}) copy-start(bf16[8,128,576]{2,1,0:T(8,128)(2,1)} %shard_map.83.q_ref) | copy-start | bytes 3538948
  49.4 14.7 %copy-start.2 = (bf16[512,1024]{1,0:T(8,128)(2,1)S(1)}, bf16[512,1024]{1,0:T(8,128)(2,1)}, u32[]{:S(2)}) copy-start(bf16[512,1024]{1,0:T(8,128)(2,1)} %w_ref.7) | copy-start | bytes 3145732
  60.8 1.4 %collective-permute-start.6 = (bf16[128,576]{1,0:T(8,128)(2,1)S(1)}, bf16[128,576]{1,0:T(8,128)(2,1)S(1)}, u32[]{:S(2)}, u32[]{:S(2)}) collective-permute-start(bf16[128,576]{1,0:T(8,128)(2,1)S(1)} %collective-permute-done.2.refs_0_), channel_id=1, source_target_pairs={{0,1},{1,0},{2,3},{3,2},{4,5},{5,4},{6,7},{7,6},{8,9},{9,8},{10,11... | collective-permute-start | bytes 442376 | tf_op jit(solution)/shard_map/ppermute | solution.py:229
  60.8 3.3 %collective-permute-start.7 = (bf16[128,576]{1,0:T(8,128)(2,1)S(1)}, bf16[128,576]{1,0:T(8,128)(2,1)S(1)}, u32[]{:S(2)}, u32[]{:S(2)}) collective-permute-start(bf16[128,576]{1,0:T(8,128)(2,1)S(1)} %collective-permute-done.3.refs_1_), channel_id=1, source_target_pairs={{1,0},{3,2},{5,4},{7,6},{9,8},{11,10},{13,12},{15,14},{17,16},{19,... | collective-permute-start | bytes 442376 | tf_op jit(solution)/shard_map/ppermute | solution.py:229
  66.8 24.2 %copy-start.1 = (bf16[1024,896]{1,0:T(8,128)(2,1)S(1)}, bf16[1024,896]{1,0:T(8,128)(2,1)}, u32[]{:S(2)}) copy-start(bf16[1024,896]{1,0:T(8,128)(2,1)} %w_ref.9) | copy-start | bytes 5505028
  66.8 6.5 %collective-permute-start.8 = (bf16[64,1024]{1,0:T(8,128)(2,1)S(1)}, bf16[64,1024]{1,0:T(8,128)(2,1)S(1)}, u32[]{:S(2)}, u32[]{:S(2)}) collective-permute-start(bf16[64,1024]{1,0:T(8,128)(2,1)S(1)} %shard_map.85.refs_0_), channel_id=1, source_target_pairs={{0,8},{1,9},{2,10},{3,11},{4,12},{5,13},{6,14},{7,15},{8,24},{9,25... | collective-permute-start | bytes 393224 | tf_op jit(solution)/shard_map/ppermute | solution.py:229
  70.8 7.1 %collective-permute-start.11 = (bf16[64,1024]{1,0:T(8,128)(2,1)S(1)}, bf16[64,1024]{1,0:T(8,128)(2,1)S(1)}, u32[]{:S(2)}, u32[]{:S(2)}) collective-permute-start(bf16[64,1024]{1,0:T(8,128)(2,1)S(1)} %shard_map.86.refs_4_), channel_id=1, source_target_pairs={{0,8},{1,9},{2,10},{3,11},{4,12},{5,13},{6,14},{7,15},{8,24},{9,25... | collective-permute-start | bytes 393224 | tf_op jit(solution)/shard_map/ppermute | solution.py:229
  73.3 6.9 %collective-permute-start.9 = (bf16[64,1024]{1,0:T(8,128)(2,1)S(1)}, bf16[64,1024]{1,0:T(8,128)(2,1)S(1)}, u32[]{:S(2)}, u32[]{:S(2)}) collective-permute-start(bf16[64,1024]{1,0:T(8,128)(2,1)S(1)} %collective-permute-done.8.refs_1_), channel_id=1, source_target_pairs={{0,8},{1,9},{2,10},{3,11},{4,12},{5,13},{6,14},{7,15},{8,24},{9,25... | collective-permute-start | bytes 393224 | tf_op jit(solution)/shard_map/ppermute | solution.py:229
  77.9 7.2 %collective-permute-start.12 = (bf16[64,1024]{1,0:T(8,128)(2,1)S(1)}, bf16[64,1024]{1,0:T(8,128)(2,1)S(1)}, u32[]{:S(2)}, u32[]{:S(2)}) collective-permute-start(bf16[64,1024]{1,0:T(8,128)(2,1)S(1)} %collective-permute-done.11.refs_5_), channel_id=1, source_target_pairs={{0,8},{1,9},{2,10},{3,11},{4,12},{5,13},{6,14},{7,15},{8,24},{9,25... | collective-permute-start | bytes 393224 | tf_op jit(solution)/shard_map/ppermute | solution.py:229
  80.1 7.8 %collective-permute-start.10 = (bf16[64,1024]{1,0:T(8,128)(2,1)S(1)}, bf16[64,1024]{1,0:T(8,128)(2,1)S(1)}, u32[]{:S(2)}, u32[]{:S(2)}) collective-permute-start(bf16[64,1024]{1,0:T(8,128)(2,1)S(1)} %collective-permute-done.9.refs_2_), channel_id=1, source_target_pairs={{0,8},{1,9},{2,10},{3,11},{4,12},{5,13},{6,14},{7,15},{8,24},{9,25... | collective-permute-start | bytes 393224 | tf_op jit(solution)/shard_map/ppermute | solution.py:229
  85.1 5.9 %collective-permute-start.13 = (bf16[64,1024]{1,0:T(8,128)(2,1)S(1)}, bf16[64,1024]{1,0:T(8,128)(2,1)S(1)}, u32[]{:S(2)}, u32[]{:S(2)}) collective-permute-start(bf16[64,1024]{1,0:T(8,128)(2,1)S(1)} %collective-permute-done.12.refs_6_), channel_id=1, source_target_pairs={{0,8},{1,9},{2,10},{3,11},{4,12},{5,13},{6,14},{7,15},{8,24},{9,25... | collective-permute-start | bytes 393224 | tf_op jit(solution)/shard_map/ppermute | solution.py:229
  92.3 1.9 %collective-permute-start.14 = (bf16[2,128,896]{2,1,0:T(8,128)(2,1)S(1)}, bf16[2,128,896]{2,1,0:T(8,128)(2,1)S(1)}, u32[]{:S(2)}, u32[]{:S(2)}) collective-permute-start(bf16[2,128,896]{2,1,0:T(8,128)(2,1)S(1)} %shard_map.88), channel_id=1, source_target_pairs={{0,1},{1,0},{2,3},{3,2},{4,5},{5,4},{6,7},{7,6},{8,9},{9,8},{10,11... | collective-permute-start | bytes 1376264 | tf_op jit(solution)/shard_map/ppermute | solution.py:229
  96.2 3.6 %collective-permute-start.20 = (bf16[2,128,896]{2,1,0:T(8,128)(2,1)S(1)}, bf16[2,128,896]{2,1,0:T(8,128)(2,1)S(1)}, u32[]{:S(2)}, u32[]{:S(2)}) collective-permute-start(bf16[2,128,896]{2,1,0:T(8,128)(2,1)S(1)} %shard_map.93), channel_id=1, source_target_pairs={{0,1},{1,0},{2,3},{3,2},{4,5},{5,4},{6,7},{7,6},{8,9},{9,8},{10,11... | collective-permute-start | bytes 1376264 | tf_op jit(solution)/shard_map/ppermute | solution.py:229
  96.4 6.1 %collective-permute-start.15 = (bf16[1,64,896]{2,1,0:T(8,128)(2,1)S(1)}, bf16[1,64,896]{2,1,0:T(8,128)(2,1)S(1)}, u32[]{:S(2)}, u32[]{:S(2)}) collective-permute-start(bf16[1,64,896]{2,1,0:T(8,128)(2,1)S(1)} %get-tuple-element.25), channel_id=1, source_target_pairs={{0,2},{1,3},{2,0},{3,1},{4,6},{5,7},{6,4},{7,5},{8,10},{9,11},{10,... | collective-permute-start | bytes 344072 | tf_op jit(solution)/shard_map/ppermute | solution.py:229
  98.0 6.9 %collective-permute-start.17 = (bf16[1,64,896]{2,1,0:T(8,128)(2,1)S(1)}, bf16[1,64,896]{2,1,0:T(8,128)(2,1)S(1)}, u32[]{:S(2)}, u32[]{:S(2)}) collective-permute-start(bf16[1,64,896]{2,1,0:T(8,128)(2,1)S(1)} %get-tuple-element.26), channel_id=1, source_target_pairs={{0,2},{1,3},{2,0},{3,1},{4,6},{5,7},{6,4},{7,5},{8,10},{9,11},{10,... | collective-permute-start | bytes 344072 | tf_op jit(solution)/shard_map/ppermute | solution.py:229
  100.4 6.9 %collective-permute-start.21 = (bf16[1,64,896]{2,1,0:T(8,128)(2,1)S(1)}, bf16[1,64,896]{2,1,0:T(8,128)(2,1)S(1)}, u32[]{:S(2)}, u32[]{:S(2)}) collective-permute-start(bf16[1,64,896]{2,1,0:T(8,128)(2,1)S(1)} %get-tuple-element.29), channel_id=1, source_target_pairs={{0,2},{1,3},{2,0},{3,1},{4,6},{5,7},{6,4},{7,5},{8,10},{9,11},{10,... | collective-permute-start | bytes 344072 | tf_op jit(solution)/shard_map/ppermute | solution.py:229
  102.1 9.6 %collective-permute-start.23 = (bf16[1,64,896]{2,1,0:T(8,128)(2,1)S(1)}, bf16[1,64,896]{2,1,0:T(8,128)(2,1)S(1)}, u32[]{:S(2)}, u32[]{:S(2)}) collective-permute-start(bf16[1,64,896]{2,1,0:T(8,128)(2,1)S(1)} %get-tuple-element.30), channel_id=1, source_target_pairs={{0,2},{1,3},{2,0},{3,1},{4,6},{5,7},{6,4},{7,5},{8,10},{9,11},{10,... | collective-permute-start | bytes 344072 | tf_op jit(solution)/shard_map/ppermute | solution.py:229
  102.6 11.1 %collective-permute-start.16 = (bf16[64,896]{1,0:T(8,128)(2,1)S(1)}, bf16[64,896]{1,0:T(8,128)(2,1)S(1)}, u32[]{:S(2)}, u32[]{:S(2)}) collective-permute-start(bf16[64,896]{1,0:T(8,128)(2,1)S(1)} %shard_map.90), channel_id=1, source_target_pairs={{0,0},{1,16},{2,8},{3,24},{4,4},{5,20},{6,12},{7,28},{8,1},{9,17},... | collective-permute-start | bytes 344072 | tf_op jit(solution)/shard_map/ppermute | solution.py:229
  104.9 8.7 %collective-permute-start.18 = (bf16[64,896]{1,0:T(8,128)(2,1)S(1)}, bf16[64,896]{1,0:T(8,128)(2,1)S(1)}, u32[]{:S(2)}, u32[]{:S(2)}) collective-permute-start(bf16[64,896]{1,0:T(8,128)(2,1)S(1)} %shard_map.91), channel_id=1, source_target_pairs={{0,8},{1,24},{2,0},{3,16},{4,12},{5,28},{6,4},{7,20},{8,9},{9,25},... | collective-permute-start | bytes 344072 | tf_op jit(solution)/shard_map/ppermute | solution.py:229
  107.4 6.3 %collective-permute-start.22 = (bf16[64,896]{1,0:T(8,128)(2,1)S(1)}, bf16[64,896]{1,0:T(8,128)(2,1)S(1)}, u32[]{:S(2)}, u32[]{:S(2)}) collective-permute-start(bf16[64,896]{1,0:T(8,128)(2,1)S(1)} %shard_map.95), channel_id=1, source_target_pairs={{0,8},{1,24},{2,0},{3,16},{4,12},{5,28},{6,4},{7,20},{8,9},{9,25},... | collective-permute-start | bytes 344072 | tf_op jit(solution)/shard_map/ppermute | solution.py:229
  111.7 8.8 %collective-permute-start.24 = (bf16[64,896]{1,0:T(8,128)(2,1)S(1)}, bf16[64,896]{1,0:T(8,128)(2,1)S(1)}, u32[]{:S(2)}, u32[]{:S(2)}) collective-permute-start(bf16[64,896]{1,0:T(8,128)(2,1)S(1)} %shard_map.96), channel_id=1, source_target_pairs={{0,0},{1,16},{2,8},{3,24},{4,4},{5,20},{6,12},{7,28},{8,1},{9,17},... | collective-permute-start | bytes 344072 | tf_op jit(solution)/shard_map/ppermute | solution.py:229

commit v3 on v2

--- a/solution.py
+++ b/solution.py
@@ -14,6 +14,7 @@
 VDIM = 128
 AXES = ("ctx", "head")
 MIB = 1024 * 1024
+COUNTS = ([1], [1])
 NT = (((1,), (1,)), ((), ()))
 
 
@@ -126,60 +127,57 @@
     return jnp.where(at > zs // 2, 2 * (zs - at), jnp.maximum(2 * at - 1, 0))
 
 
-def project_kernel(zs, kept, place_ref, w_ref, *refs):
-    blocks, out_ref, tokens = refs[:-2], refs[-2], refs[-1]
+def project_kernel(zs, place_ref, w_ref, *refs):
+    blocks, mine_ref, away_ref, tokens = refs[:zs], refs[zs], refs[zs + 1], refs[zs + 2]
     zl = zs // 2
     k = place_ref[1]
     half = blocks[0].shape[0]
-    rows = half * len(blocks) // zs
-    for i, block in enumerate(blocks):
-        span, step = divmod(i, zs)
+    for step, block in enumerate(blocks):
         member = ring_member((ring_place(place_ref[2], zs) + zs - step) % zs, zs)
-        tokens[pl.ds(pl.multiple_of(member * rows + span * half, half), half), :] = block[...]
-    side = k if kept else 1 - k
-    these = tokens[pl.ds(pl.multiple_of(side * (zl * rows), zl * rows), zl * rows), :]
-    part = jnp.dot(these, w_ref[...], preferred_element_type=jnp.float32)
-    out_ref[...] = part.astype(out_ref.dtype).reshape(out_ref.shape)
-
-
-def halve_kernel(bit, turn, place_ref, mine_ref, *refs):
-    got_refs, keep_ref, away_refs = refs[:-3], refs[-3], refs[-2:]
-    half = away_refs[0].shape[1]
-    for span, away_ref in enumerate(away_refs):
-        these = slice(span * half, (span + 1) * half)
-        low = ((place_ref[4 + (turn + span) % 2] // bit) % 2) == 0
-
-        def total(d):
-            if len(got_refs) == 1:
-                got = got_refs[0][d, these]
-            else:
-                got = got_refs[span][d]
-            return mine_ref[d, these] + got.astype(jnp.float32)
-
-        for d in range(bit):
-            a = total(d)
-            b = total(d + bit)
-            keep_ref[d, these] = jnp.where(low, a, b)
-            away_ref[d] = jnp.where(low, b, a).astype(away_ref.dtype)
-
-
-def add_kernel(span, mine_ref, got_ref, out_ref):
-    half = out_ref.shape[0]
-    mine = mine_ref[0, span * half : (span + 1) * half]
-    out_ref[...] = (mine + got_ref[0].astype(jnp.float32)).astype(out_ref.dtype)
-
-
-def output_kernel(place_ref, *refs):
-    blocks, out_ref = refs[:-1], refs[-1]
-    xs = len(blocks) // 2
+        at = jnp.where(member // zl == k, 0, zl) + member % zl
+        tokens[pl.ds(pl.multiple_of(at * half, half), half), :] = block[...]
+    part = jnp.dot(tokens[...], w_ref[...], preferred_element_type=jnp.float32)
+    part = part.reshape(zs, half, -1)
+    mine_ref[...] = part[:zl]
+    away_ref[...] = part[zl:].astype(away_ref.dtype)
+
+
+def halve_kernel(bit, place_ref, mine_ref, got_ref, keep_ref, away_ref):
+    low = (place_ref[0] // bit) % 2 == 0
+    for d in range(bit):
+        a = mine_ref[d] + got_ref[d].astype(jnp.float32)
+        b = mine_ref[d + bit] + got_ref[d + bit].astype(jnp.float32)
+        keep_ref[d] = jnp.where(low, a, b)
+        away_ref[d] = jnp.where(low, b, a).astype(away_ref.dtype)
+
+
+def add_kernel(*refs):
+    out_ref = refs[-1]
+    half = refs[0].shape[1]
+    for i in range(len(refs) // 2):
+        total = refs[2 * i][0] + refs[2 * i + 1][0].astype(jnp.float32)
+        out_ref[i * half : (i + 1) * half] = total.astype(out_ref.dtype)
+
+
+def output_kernel(counts, place_ref, *refs):
+    out_ref = refs[-1]
     x = place_ref[3]
-    half, cols = blocks[0].shape
-    for i in range(xs):
+    rows = out_ref.shape[0]
+    cols = refs[0].shape[1]
+    half = rows // 2
+
+    def rows_of(dx, span):
+        first = sum(counts[:dx])
+        if counts[dx] == 2:
+            return refs[first + span][...]
+        return refs[first][span * half : (span + 1) * half]
+
+    for at in range(len(counts)):
         for span in range(2):
-            block = blocks[span][...]
-            for dx in range(1, xs):
-                block = jnp.where((x ^ i) == dx, blocks[2 * dx + span][...], block)
-            out_ref[span * half : (span + 1) * half, i * cols : (i + 1) * cols] = block
+            block = rows_of(0, span)
+            for dx in range(1, len(counts)):
+                block = jnp.where((x ^ at) == dx, rows_of(dx, span), block)
+            out_ref[span * half : (span + 1) * half, at * cols : (at + 1) * cols] = block
 
 
 def whole():
@@ -293,47 +291,53 @@
         along = [heads_out]
         for _ in range(1, zs):
             along.append(send(along[-1], lambda z, x, y, k: (following[z], x, y, k)))
-        blocks += along
+        blocks.append(along)
 
     results = []
-    for dx in range(xs):
-        turn = dx % 2
-        if dx:
-            matrices[dx], mine = lax.optimization_barrier((matrices[dx], mine))
-
-        def project(kept, kind):
-            return call(
-                functools.partial(project_kernel, zs, kept),
-                ((zl, rows, cols), kind),
-                (place, matrices[dx], *blocks),
+    counts = COUNTS[0] * (xs - 1) + COUNTS[1]
+    sums = {}
+    for dx, count in enumerate(counts):
+        for span in range(2):
+            flip = (dx + span * (count - 1)) % 2 * (zl - 1)
+            owner = (y ^ flip).reshape(1).astype(jnp.int32)
+            mine, away = call(
+                functools.partial(project_kernel, zs),
+                [((zl, half, cols), f32), ((zl, half, cols), bf16)],
+                (place, matrices[dx], *blocks[span]),
                 smem=1,
-                scratch=(pltpu.VMEM((zs * rows, depth), bf16),),
-                flops=2 * zl * rows * depth * cols,
+                scratch=(pltpu.VMEM((zs * half, depth), bf16),),
+                flops=2 * zs * half * depth * cols,
             )
-
-        away = project(False, bf16)
-        got = [send(away, lambda z, x, y, k: (z, x, y, 1 - k))]
-        mine = project(True, f32)
-        bit = zl // 2
-        while bit:
-            part = ((bit, half, cols), bf16)
-            mine, *away = call(
-                functools.partial(halve_kernel, bit, turn),
-                [((bit, rows, cols), f32), part, part],
-                (place, mine, *got),
-                smem=1,
-            )
-            got = [send(value, lambda z, x, y, k: (z, x, y ^ bit, k)) for value in away]
-            bit //= 2
-        for span in range(2):
-            block = call(
-                functools.partial(add_kernel, span), ((half, cols), bf16), (mine, got[span])
-            )
-            flip = (turn + span) % 2 * (zl - 1)
-            results.append(
-                send(block, lambda z, x, y, k: (k * zl + (y ^ flip), x, z // 2, z % 2))
-            )
-    return call(output_kernel, ((rows, xs * cols), bf16), (place, *results), smem=1)
+            got = send(away, lambda z, x, y, k: (z, x, y, 1 - k))
+            bit = zl // 2
+            while bit:
+                shape = (bit, half, cols)
+                mine, away = call(
+                    functools.partial(halve_kernel, bit),
+                    [(shape, f32), (shape, bf16)],
+                    (owner, mine, got),
+                    smem=1,
+                )
+                got = send(away, lambda z, x, y, k: (z, x, y ^ bit, k))
+                bit //= 2
+            sums[dx, span] = (mine, got, flip)
+    last = mine
+    for dx, count in enumerate(counts):
+        pieces = [sums[dx, 0][:2], sums[dx, 1][:2]]
+        if count == 1:
+            pieces = [pieces[0] + pieces[1]]
+        for i, piece in enumerate(pieces):
+            if dx < xs - 1:
+                piece, last = lax.optimization_barrier((piece, last))
+            block = call(add_kernel, ((rows // count, cols), bf16), piece)
+            flip = sums[dx, i][2]
+            results.append(send(block, lambda z, x, y, k: (k * zl + (y ^ flip), x, z // 2, z % 2)))
+    return call(
+        functools.partial(output_kernel, counts),
+        ((rows, xs * cols), bf16),
+        (place, *results),
+        smem=1,
+    )
 
 
 def solution(mesh):

time: 122 us -> 122 us (level)
  the two profiles are of different devices: /device:TPU:24 before, /device:TPU:0 now
where the time goes in v3:
time: 122 us; the launch traced here: 120 us
  waiting for transfers between devices  68.9 us (56%)
  starting transfers between devices  29.3 us (24%)
  Pallas kernels  20.5 us (17%)
  local copies, waits for them, and re-layouts  1.41 us (1%)
    ppermute x25, waiting for transfers between devices, send(): return lax.ppermute(value, AXES, pairs)  68.9 us
    ppermute x25, starting transfers between devices, send(): return lax.ppermute(value, AXES, pairs)  29.3 us
    pallas_call x16, Pallas kernels, call(): pl.pallas_call(kernel, out_shape=shapes, in_specs=[pl.BlockSpec(memory_sp...  20.5 us
  transfers between devices with their start and end apart: 25, of which 16 were waited for; matrix products, arithmetic and copies ran while one was open for 0% of the time, Pallas kernels for 16%

profile of v3, /device:TPU:0, one launch (start us, length us, event | category | flops | bytes accessed | tf_op | source)
XLA Modules:
  0.0 120.2 jit_solution(13508639686230313052)
XLA Ops:
  0.0 3.0 %collective-permute-start.18 = (bf16[1024,896]{1,0:T(8,128)(2,1)}, bf16[1024,896]{1,0:T(8,128)(2,1)S(1)}, u32[]{:S(2)}, u32[]{:S(2)}) collective-permute-start(bf16[1024,896]{1,0:T(8,128)(2,1)} %w_ref.9), channel_id=1, source_target_pairs={{0,4},{1,5},{2,6},{3,7},{4,0},{5,1},{6,2},{7,3},{8,12},{9,13},{10,... | collective-permute-start | bytes 5505032 | tf_op jit(solution)/shard_map/ppermute | solution.py:227
  3.0 1.6 %shard_map.82.own_ref = bf16[128,576]{1,0:T(8,128)(2,1)} custom-call(bf16[128,512]{1,0:T(8,128)(2,1)} %latent_ref.1, bf16[64,128]{1,0:T(8,128)(2,1)} %bitcast.7), custom_call_target="tpu_custom_call" | custom-call | bytes 294912 | tf_op jit(solution)/shard_map/pallas_call | solution.py:192
  4.6 1.5 %collective-permute-start.1 = (bf16[128,576]{1,0:T(8,128)(2,1)}, bf16[128,576]{1,0:T(8,128)(2,1)S(1)}, u32[]{:S(2)}, u32[]{:S(2)}) collective-permute-start(bf16[128,576]{1,0:T(8,128)(2,1)} %shard_map.82.own_ref), channel_id=1, source_target_pairs={{0,12},{1,17},{2,14},{3,19},{4,8},{5,21},{6,10},{7,23},{8,4},{9,25... | collective-permute-start | bytes 442376 | tf_op jit(solution)/shard_map/ppermute | solution.py:227
  6.2 1.5 %collective-permute-start = (bf16[128,576]{1,0:T(8,128)(2,1)}, bf16[128,576]{1,0:T(8,128)(2,1)S(1)}, u32[]{:S(2)}, u32[]{:S(2)}) collective-permute-start(bf16[128,576]{1,0:T(8,128)(2,1)} %shard_map.82.own_ref), channel_id=1, source_target_pairs={{0,4},{1,9},{2,6},{3,11},{4,0},{5,13},{6,2},{7,15},{8,12},{9,1},{1... | collective-permute-start | bytes 442376 | tf_op jit(solution)/shard_map/ppermute | solution.py:227
  7.7 2.9 %shard_map.83.q_ref = bf16[8,128,576]{2,1,0:T(8,128)(2,1)} custom-call(bf16[128,1024]{1,0:T(8,128)(2,1)} %q_ref.1, bf16[128,512]{1,0:T(8,128)(2,1)} %rope_ref.1, bf16[512,1024]{1,0:T(8,128)(2,1)} %w_ref.5), custom_call_target="tpu_custom_call" | custom-call | flops 134217728 | bytes 2621440 | tf_op jit(solution)/shard_map/pallas_call | solution.py:192
  10.6 2.9 %collective-permute-done.1.refs_1_ = bf16[128,576]{1,0:T(8,128)(2,1)S(1)} collective-permute-done((bf16[128,576]{1,0:T(8,128)(2,1)}, bf16[128,576]{1,0:T(8,128)(2,1)S(1)}, u32[]{:S(2)}, u32[]{:S(2)}) %collective-permute-start.1) | collective-permute-done | bytes 147488 | tf_op jit(solution)/shard_map/ppermute | solution.py:227
  13.5 33.2 %collective-permute-done.refs_0_ = bf16[128,576]{1,0:T(8,128)(2,1)S(1)} collective-permute-done((bf16[128,576]{1,0:T(8,128)(2,1)}, bf16[128,576]{1,0:T(8,128)(2,1)S(1)}, u32[]{:S(2)}, u32[]{:S(2)}) %collective-permute-start) | collective-permute-done | bytes 147488 | tf_op jit(solution)/shard_map/ppermute | solution.py:227
  47.9 3.8 %collective-permute-start.2 = (bf16[128,576]{1,0:T(8,128)(2,1)S(1)}, bf16[128,576]{1,0:T(8,128)(2,1)S(1)}, u32[]{:S(2)}, u32[]{:S(2)}) collective-permute-start(bf16[128,576]{1,0:T(8,128)(2,1)S(1)} %copy-done.3), channel_id=1, source_target_pairs={{0,20},{1,25},{2,22},{3,27},{4,16},{5,29},{6,18},{7,31},{8,28},{9,... | collective-permute-start | bytes 442376 | tf_op jit(solution)/shard_map/ppermute | solution.py:227
  53.1 3.7 %shard_map.84.early_ref = f32[8,128,640]{2,1,0:T(8,128)S(1)} custom-call(s32[16]{0:T(128)S(1)} %copy-done.4, s32[6]{0:T(128)S(1)} %stack.27.place_ref, bf16[8,128,576]{2,1,0:T(8,128)(2,1)S(1)} %copy-done, bf16[128,576]{1,0:T(8,128)(2,1)S(1)} %copy-done.3, bf16[128,576]{1,0:T(8,128)(2,1)S(1)} %collective-permute-done.refs_0_, ...), custom_call_target="tpu_custom_call" | custom-call | flops 1426063360 | bytes 4538456 | tf_op jit(solution)/shard_map/pallas_call | solution.py:192
  56.9 4.7 %collective-permute-done.2.refs_0_ = bf16[128,576]{1,0:T(8,128)(2,1)S(1)} collective-permute-done((bf16[128,576]{1,0:T(8,128)(2,1)S(1)}, bf16[128,576]{1,0:T(8,128)(2,1)S(1)}, u32[]{:S(2)}, u32[]{:S(2)}) %collective-permute-start.2) | collective-permute-done | bytes 147488 | tf_op jit(solution)/shard_map/ppermute | solution.py:227
  62.9 1.9 %collective-permute-done.7.refs_3_ = bf16[128,576]{1,0:T(8,128)(2,1)S(1)} collective-permute-done((bf16[128,576]{1,0:T(8,128)(2,1)S(1)}, bf16[128,576]{1,0:T(8,128)(2,1)S(1)}, u32[]{:S(2)}, u32[]{:S(2)}) %collective-permute-start.7) | collective-permute-done | bytes 147488 | tf_op jit(solution)/shard_map/ppermute | solution.py:227
  64.8 2.6 %shard_map.88.refs_0_ = bf16[64,1024]{1,0:T(8,128)(2,1)S(1)} custom-call(s32[16]{0:T(128)S(1)} %copy-done.4, s32[6]{0:T(128)S(1)} %stack.27.place_ref, bf16[8,128,576]{2,1,0:T(8,128)(2,1)S(1)} %copy-done, bf16[512,1024]{1,0:T(8,128)(2,1)S(1)} %copy-done.2, f32[8,128,640]{2,1,0:T(8,128)S(1)} %shard_map.84.early_ref, ...), custom_call_target="tpu_custom_call" | custom-call | flops 494927872 | bytes 5570648 | tf_op jit(solution)/shard_map/pallas_call | solution.py:192
  67.5 3.0 %collective-permute-start.13 = (bf16[64,1024]{1,0:T(8,128)(2,1)S(1)}, bf16[64,1024]{1,0:T(8,128)(2,1)S(1)}, u32[]{:S(2)}, u32[]{:S(2)}) collective-permute-start(bf16[64,1024]{1,0:T(8,128)(2,1)S(1)} %shard_map.88.refs_0_), channel_id=1, source_target_pairs={{0,8},{1,9},{2,10},{3,11},{4,12},{5,13},{6,14},{7,15},{8,24},{9,25... | collective-permute-start | bytes 393224 | tf_op jit(solution)/shard_map/ppermute | solution.py:227
  70.5 2.6 %shard_map.85.refs_0_ = bf16[64,1024]{1,0:T(8,128)(2,1)S(1)} custom-call(s32[16]{0:T(128)S(1)} %copy-done.4, s32[6]{0:T(128)S(1)} %stack.27.place_ref, bf16[8,128,576]{2,1,0:T(8,128)(2,1)S(1)} %copy-done, bf16[512,1024]{1,0:T(8,128)(2,1)S(1)} %copy-done.2, f32[8,128,640]{2,1,0:T(8,128)S(1)} %shard_map.84.early_ref, ...), custom_call_target="tpu_custom_call" | custom-call | flops 494927872 | bytes 5570648 | tf_op jit(solution)/shard_map/pallas_call | solution.py:192
  73.1 2.0 %collective-permute-start.8 = (bf16[64,1024]{1,0:T(8,128)(2,1)S(1)}, bf16[64,1024]{1,0:T(8,128)(2,1)S(1)}, u32[]{:S(2)}, u32[]{:S(2)}) collective-permute-start(bf16[64,1024]{1,0:T(8,128)(2,1)S(1)} %shard_map.85.refs_0_), channel_id=1, source_target_pairs={{0,8},{1,9},{2,10},{3,11},{4,12},{5,13},{6,14},{7,15},{8,24},{9,25... | collective-permute-start | bytes 393224 | tf_op jit(solution)/shard_map/ppermute | solution.py:227
  76.5 3.5 %collective-permute-done.8.refs_1_ = bf16[64,1024]{1,0:T(8,128)(2,1)S(1)} collective-permute-done((bf16[64,1024]{1,0:T(8,128)(2,1)S(1)}, bf16[64,1024]{1,0:T(8,128)(2,1)S(1)}, u32[]{:S(2)}, u32[]{:S(2)}) %collective-permute-start.8) | collective-permute-done | bytes 131104 | tf_op jit(solution)/shard_map/ppermute | solution.py:227
  80.0 1.5 %collective-permute-start.9 = (bf16[64,1024]{1,0:T(8,128)(2,1)S(1)}, bf16[64,1024]{1,0:T(8,128)(2,1)S(1)}, u32[]{:S(2)}, u32[]{:S(2)}) collective-permute-start(bf16[64,1024]{1,0:T(8,128)(2,1)S(1)} %collective-permute-done.8.refs_1_), channel_id=1, source_target_pairs={{0,8},{1,9},{2,10},{3,11},{4,12},{5,13},{6,14},{7,15},{8,24},{9,25... | collective-permute-start | bytes 393224 | tf_op jit(solution)/shard_map/ppermute | solution.py:227
  82.4 1.9 %collective-permute-start.15 = (bf16[64,1024]{1,0:T(8,128)(2,1)S(1)}, bf16[64,1024]{1,0:T(8,128)(2,1)S(1)}, u32[]{:S(2)}, u32[]{:S(2)}) collective-permute-start(bf16[64,1024]{1,0:T(8,128)(2,1)S(1)} %collective-permute-done.14.refs_2_), channel_id=1, source_target_pairs={{0,8},{1,9},{2,10},{3,11},{4,12},{5,13},{6,14},{7,15},{8,24},{9,25... | collective-permute-start | bytes 393224 | tf_op jit(solution)/shard_map/ppermute | solution.py:227
  84.3 2.4 %collective-permute-done.9.refs_2_ = bf16[64,1024]{1,0:T(8,128)(2,1)S(1)} collective-permute-done((bf16[64,1024]{1,0:T(8,128)(2,1)S(1)}, bf16[64,1024]{1,0:T(8,128)(2,1)S(1)}, u32[]{:S(2)}, u32[]{:S(2)}) %collective-permute-start.9) | collective-permute-done | bytes 131104 | tf_op jit(solution)/shard_map/ppermute | solution.py:227
  87.9 1.8 %collective-permute-done.15.refs_3_ = bf16[64,1024]{1,0:T(8,128)(2,1)S(1)} collective-permute-done((bf16[64,1024]{1,0:T(8,128)(2,1)S(1)}, bf16[64,1024]{1,0:T(8,128)(2,1)S(1)}, u32[]{:S(2)}, u32[]{:S(2)}) %collective-permute-start.15) | collective-permute-done | bytes 131104 | tf_op jit(solution)/shard_map/ppermute | solution.py:227
  89.7 1.3 %shard_map.89 = (f32[2,64,896]{2,1,0:T(8,128)S(1)}, bf16[2,64,896]{2,1,0:T(8,128)(2,1)S(1)}) custom-call(s32[6]{0:T(128)S(1)} %stack.27.place_ref, bf16[1024,896]{1,0:T(8,128)(2,1)S(1)} %copy-done.1, bf16[64,1024]{1,0:T(8,128)(2,1)S(1)} %shard_map.88.refs_0_, bf16[64,1024]{1,0:T(8,128)(2,1)S(1)} %collective-permute-done.13.refs_1_, ...), custom_call_target="tpu_custom_call" | custom-call | flops 469762048 | bytes 3047448 | tf_op jit(solution)/shard_map/pallas_call | solution.py:192
  91.1 1.5 %collective-permute-done.10.refs_3_ = bf16[64,1024]{1,0:T(8,128)(2,1)S(1)} collective-permute-done((bf16[64,1024]{1,0:T(8,128)(2,1)S(1)}, bf16[64,1024]{1,0:T(8,128)(2,1)S(1)}, u32[]{:S(2)}, u32[]{:S(2)}) %collective-permute-start.10) | collective-permute-done | bytes 131104 | tf_op jit(solution)/shard_map/ppermute | solution.py:227
  94.0 1.3 %shard_map.94 = (f32[2,64,896]{2,1,0:T(8,128)S(1)}, bf16[2,64,896]{2,1,0:T(8,128)(2,1)S(1)}) custom-call(s32[6]{0:T(128)S(1)} %stack.27.place_ref, bf16[1024,896]{1,0:T(8,128)(2,1)S(1)} %collective-permute-done.18.w_ref, bf16[64,1024]{1,0:T(8,128)(2,1)S(1)} %shard_map.85.refs_0_, bf16[64,1024]{1,0:T(8,128)(2,1)S(1)} %collective-permute-done.8.refs_1_, ...), custom_call_target="tpu_custom_call" | custom-call | flops 469762048 | bytes 3047448 | tf_op jit(solution)/shard_map/pallas_call | solution.py:192
  95.8 1.3 %shard_map.91 = (f32[2,64,896]{2,1,0:T(8,128)S(1)}, bf16[2,64,896]{2,1,0:T(8,128)(2,1)S(1)}) custom-call(s32[6]{0:T(128)S(1)} %stack.27.place_ref, bf16[1024,896]{1,0:T(8,128)(2,1)S(1)} %collective-permute-done.18.w_ref, bf16[64,1024]{1,0:T(8,128)(2,1)S(1)} %shard_map.88.refs_0_, bf16[64,1024]{1,0:T(8,128)(2,1)S(1)} %collective-permute-done.13.refs_1_, ...), custom_call_target="tpu_custom_call" | custom-call | flops 469762048 | bytes 3047448 | tf_op jit(solution)/shard_map/pallas_call | solution.py:192
  97.3 1.6 %collective-permute-start.17 = (bf16[1,64,896]{2,1,0:T(8,128)(2,1)S(1)}, bf16[1,64,896]{2,1,0:T(8,128)(2,1)S(1)}, u32[]{:S(2)}, u32[]{:S(2)}) collective-permute-start(bf16[1,64,896]{2,1,0:T(8,128)(2,1)S(1)} %get-tuple-element.44), channel_id=1, source_target_pairs={{0,2},{1,3},{2,0},{3,1},{4,6},{5,7},{6,4},{7,5},{8,10},{9,11},{10,... | collective-permute-start | bytes 344072 | tf_op jit(solution)/shard_map/ppermute | solution.py:227
  99.6 1.6 %collective-permute-start.22 = (bf16[1,64,896]{2,1,0:T(8,128)(2,1)S(1)}, bf16[1,64,896]{2,1,0:T(8,128)(2,1)S(1)}, u32[]{:S(2)}, u32[]{:S(2)}) collective-permute-start(bf16[1,64,896]{2,1,0:T(8,128)(2,1)S(1)} %get-tuple-element.55), channel_id=1, source_target_pairs={{0,2},{1,3},{2,0},{3,1},{4,6},{5,7},{6,4},{7,5},{8,10},{9,11},{10,... | collective-permute-start | bytes 344072 | tf_op jit(solution)/shard_map/ppermute | solution.py:227
  101.8 1.6 %collective-permute-done.17.refs_3_ = bf16[1,64,896]{2,1,0:T(8,128)(2,1)S(1)} collective-permute-done((bf16[1,64,896]{2,1,0:T(8,128)(2,1)S(1)}, bf16[1,64,896]{2,1,0:T(8,128)(2,1)S(1)}, u32[]{:S(2)}, u32[]{:S(2)}) %collective-permute-start.17) | collective-permute-done | bytes 114720 | tf_op jit(solution)/shard_map/ppermute | solution.py:227
  103.4 2.5 %collective-permute-done.12.refs_1_ = bf16[1,64,896]{2,1,0:T(8,128)(2,1)S(1)} collective-permute-done((bf16[1,64,896]{2,1,0:T(8,128)(2,1)S(1)}, bf16[1,64,896]{2,1,0:T(8,128)(2,1)S(1)}, u32[]{:S(2)}, u32[]{:S(2)}) %collective-permute-start.12) | collective-permute-done | bytes 114720 | tf_op jit(solution)/shard_map/ppermute | solution.py:227
  106.6 1.7 %collective-permute-done.22.refs_1_ = bf16[1,64,896]{2,1,0:T(8,128)(2,1)S(1)} collective-permute-done((bf16[1,64,896]{2,1,0:T(8,128)(2,1)S(1)}, bf16[1,64,896]{2,1,0:T(8,128)(2,1)S(1)}, u32[]{:S(2)}, u32[]{:S(2)}) %collective-permute-start.22) | collective-permute-done | bytes 114720 | tf_op jit(solution)/shard_map/ppermute | solution.py:227
  108.3 2.0 %collective-permute-done.23.refs_3_ = bf16[1,64,896]{2,1,0:T(8,128)(2,1)S(1)} collective-permute-done((bf16[1,64,896]{2,1,0:T(8,128)(2,1)S(1)}, bf16[1,64,896]{2,1,0:T(8,128)(2,1)S(1)}, u32[]{:S(2)}, u32[]{:S(2)}) %collective-permute-start.23) | collective-permute-done | bytes 114720 | tf_op jit(solution)/shard_map/ppermute | solution.py:227
  111.1 7.7 %collective-permute-done.24.refs_1_ = bf16[128,896]{1,0:T(8,128)(2,1)S(1)} collective-permute-done((bf16[128,896]{1,0:T(8,128)(2,1)S(1)}, bf16[128,896]{1,0:T(8,128)(2,1)S(1)}, u32[]{:S(2)}, u32[]{:S(2)}) %collective-permute-start.24) | collective-permute-done | bytes 229408 | tf_op jit(solution)/shard_map/ppermute | solution.py:227
  118.9 1.3 %shard_map.97 = bf16[128,1792]{1,0:T(8,128)(2,1)} custom-call(s32[6]{0:T(128)S(1)} %stack.27.place_ref, bf16[128,896]{1,0:T(8,128)(2,1)S(1)} %collective-permute-done.20.refs_0_, bf16[128,896]{1,0:T(8,128)(2,1)S(1)} %collective-permute-done.24.refs_1_), custom_call_target="tpu_custom_call" | custom-call | bytes 917528 | tf_op jit(solution)/shard_map/pallas_call | solution.py:192
  (45 shorter events, 12.4 us)
Async XLA Ops:
  0.0 51.8 %copy-start.4 = (s32[16]{0:T(128)S(1)}, s32[16]{0:T(128)}, u32[]{:S(2)}) copy-start(s32[16]{0:T(128)} %order_ref.5) | copy-start | bytes 196
  0.0 94.0 %collective-permute-start.18 = (bf16[1024,896]{1,0:T(8,128)(2,1)}, bf16[1024,896]{1,0:T(8,128)(2,1)S(1)}, u32[]{:S(2)}, u32[]{:S(2)}) collective-permute-start(bf16[1024,896]{1,0:T(8,128)(2,1)} %w_ref.9), channel_id=1, source_target_pairs={{0,4},{1,5},{2,6},{3,7},{4,0},{5,1},{6,2},{7,3},{8,12},{9,13},{10,... | collective-permute-start | bytes 5505032 | tf_op jit(solution)/shard_map/ppermute | solution.py:227
  4.6 42.6 %copy-start.3 = (bf16[128,576]{1,0:T(8,128)(2,1)S(1)}, bf16[128,576]{1,0:T(8,128)(2,1)}, u32[]{:S(2)}) copy-start(bf16[128,576]{1,0:T(8,128)(2,1)} %shard_map.82.own_ref) | copy-start | bytes 442372
  4.6 8.9 %collective-permute-start.1 = (bf16[128,576]{1,0:T(8,128)(2,1)}, bf16[128,576]{1,0:T(8,128)(2,1)S(1)}, u32[]{:S(2)}, u32[]{:S(2)}) collective-permute-start(bf16[128,576]{1,0:T(8,128)(2,1)} %shard_map.82.own_ref), channel_id=1, source_target_pairs={{0,12},{1,17},{2,14},{3,19},{4,8},{5,21},{6,10},{7,23},{8,4},{9,25... | collective-permute-start | bytes 442376 | tf_op jit(solution)/shard_map/ppermute | solution.py:227
  6.2 40.5 %collective-permute-start = (bf16[128,576]{1,0:T(8,128)(2,1)}, bf16[128,576]{1,0:T(8,128)(2,1)S(1)}, u32[]{:S(2)}, u32[]{:S(2)}) collective-permute-start(bf16[128,576]{1,0:T(8,128)(2,1)} %shard_map.82.own_ref), channel_id=1, source_target_pairs={{0,4},{1,9},{2,6},{3,11},{4,0},{5,13},{6,2},{7,15},{8,12},{9,1},{1... | collective-permute-start | bytes 442376 | tf_op jit(solution)/shard_map/ppermute | solution.py:227
  46.7 5.1 %collective-permute-start.4 = (bf16[128,576]{1,0:T(8,128)(2,1)S(1)}, bf16[128,576]{1,0:T(8,128)(2,1)S(1)}, u32[]{:S(2)}, u32[]{:S(2)}) collective-permute-start(bf16[128,576]{1,0:T(8,128)(2,1)S(1)} %collective-permute-done.refs_0_), channel_id=1, source_target_pairs={{0,1},{1,0},{2,3},{3,2},{4,5},{5,4},{6,7},{7,6},{8,9},{9,8},{10,11... | collective-permute-start | bytes 442376 | tf_op jit(solution)/shard_map/ppermute | solution.py:227
  46.7 5.1 %collective-permute-start.5 = (bf16[128,576]{1,0:T(8,128)(2,1)S(1)}, bf16[128,576]{1,0:T(8,128)(2,1)S(1)}, u32[]{:S(2)}, u32[]{:S(2)}) collective-permute-start(bf16[128,576]{1,0:T(8,128)(2,1)S(1)} %collective-permute-done.1.refs_1_), channel_id=1, source_target_pairs={{0,1},{1,0},{2,3},{3,2},{4,5},{5,4},{6,7},{7,6},{8,9},{9,8},{10,11... | collective-permute-start | bytes 442376 | tf_op jit(solution)/shard_map/ppermute | solution.py:227
  47.2 9.7 %collective-permute-start.3 = (bf16[128,576]{1,0:T(8,128)(2,1)S(1)}, bf16[128,576]{1,0:T(8,128)(2,1)S(1)}, u32[]{:S(2)}, u32[]{:S(2)}) collective-permute-start(bf16[128,576]{1,0:T(8,128)(2,1)S(1)} %copy-done.3), channel_id=1, source_target_pairs={{1,29},{3,31},{5,25},{7,27},{9,21},{11,23},{13,17},{15,19},{17,13}... | collective-permute-start | bytes 442376 | tf_op jit(solution)/shard_map/ppermute | solution.py:227
  47.9 13.7 %collective-permute-start.2 = (bf16[128,576]{1,0:T(8,128)(2,1)S(1)}, bf16[128,576]{1,0:T(8,128)(2,1)S(1)}, u32[]{:S(2)}, u32[]{:S(2)}) collective-permute-start(bf16[128,576]{1,0:T(8,128)(2,1)S(1)} %copy-done.3), channel_id=1, source_target_pairs={{0,20},{1,25},{2,22},{3,27},{4,16},{5,29},{6,18},{7,31},{8,28},{9,... | collective-permute-start | bytes 442376 | tf_op jit(solution)/shard_map/ppermute | solution.py:227
  51.8 1.3 %copy-start = (bf16[8,128,576]{2,1,0:T(8,128)(2,1)S(1)}, bf16[8,128,576]{2,1,0:T(8,128)(2,1)}, u32[]{:S(2)}) copy-start(bf16[8,128,576]{2,1,0:T(8,128)(2,1)} %shard_map.83.q_ref) | copy-start | bytes 3538948
  53.1 11.7 %copy-start.2 = (bf16[512,1024]{1,0:T(8,128)(2,1)S(1)}, bf16[512,1024]{1,0:T(8,128)(2,1)}, u32[]{:S(2)}) copy-start(bf16[512,1024]{1,0:T(8,128)(2,1)} %w_ref.8) | copy-start | bytes 3145732
  61.5 1.4 %collective-permute-start.6 = (bf16[128,576]{1,0:T(8,128)(2,1)S(1)}, bf16[128,576]{1,0:T(8,128)(2,1)S(1)}, u32[]{:S(2)}, u32[]{:S(2)}) collective-permute-start(bf16[128,576]{1,0:T(8,128)(2,1)S(1)} %collective-permute-done.2.refs_0_), channel_id=1, source_target_pairs={{0,1},{1,0},{2,3},{3,2},{4,5},{5,4},{6,7},{7,6},{8,9},{9,8},{10,11... | collective-permute-start | bytes 442376 | tf_op jit(solution)/shard_map/ppermute | solution.py:227
  61.5 3.3 %collective-permute-start.7 = (bf16[128,576]{1,0:T(8,128)(2,1)S(1)}, bf16[128,576]{1,0:T(8,128)(2,1)S(1)}, u32[]{:S(2)}, u32[]{:S(2)}) collective-permute-start(bf16[128,576]{1,0:T(8,128)(2,1)S(1)} %collective-permute-done.3.refs_1_), channel_id=1, source_target_pairs={{1,0},{3,2},{5,4},{7,6},{9,8},{11,10},{13,12},{15,14},{17,16},{19,... | collective-permute-start | bytes 442376 | tf_op jit(solution)/shard_map/ppermute | solution.py:227
  67.5 22.2 %copy-start.1 = (bf16[1024,896]{1,0:T(8,128)(2,1)S(1)}, bf16[1024,896]{1,0:T(8,128)(2,1)}, u32[]{:S(2)}) copy-start(bf16[1024,896]{1,0:T(8,128)(2,1)} %w_ref.9) | copy-start | bytes 5505028
  67.5 8.1 %collective-permute-start.13 = (bf16[64,1024]{1,0:T(8,128)(2,1)S(1)}, bf16[64,1024]{1,0:T(8,128)(2,1)S(1)}, u32[]{:S(2)}, u32[]{:S(2)}) collective-permute-start(bf16[64,1024]{1,0:T(8,128)(2,1)S(1)} %shard_map.88.refs_0_), channel_id=1, source_target_pairs={{0,8},{1,9},{2,10},{3,11},{4,12},{5,13},{6,14},{7,15},{8,24},{9,25... | collective-permute-start | bytes 393224 | tf_op jit(solution)/shard_map/ppermute | solution.py:227
  73.1 6.9 %collective-permute-start.8 = (bf16[64,1024]{1,0:T(8,128)(2,1)S(1)}, bf16[64,1024]{1,0:T(8,128)(2,1)S(1)}, u32[]{:S(2)}, u32[]{:S(2)}) collective-permute-start(bf16[64,1024]{1,0:T(8,128)(2,1)S(1)} %shard_map.85.refs_0_), channel_id=1, source_target_pairs={{0,8},{1,9},{2,10},{3,11},{4,12},{5,13},{6,14},{7,15},{8,24},{9,25... | collective-permute-start | bytes 393224 | tf_op jit(solution)/shard_map/ppermute | solution.py:227
  75.6 6.8 %collective-permute-start.14 = (bf16[64,1024]{1,0:T(8,128)(2,1)S(1)}, bf16[64,1024]{1,0:T(8,128)(2,1)S(1)}, u32[]{:S(2)}, u32[]{:S(2)}) collective-permute-start(bf16[64,1024]{1,0:T(8,128)(2,1)S(1)} %collective-permute-done.13.refs_1_), channel_id=1, source_target_pairs={{0,8},{1,9},{2,10},{3,11},{4,12},{5,13},{6,14},{7,15},{8,24},{9,25... | collective-permute-start | bytes 393224 | tf_op jit(solution)/shard_map/ppermute | solution.py:227
  80.0 6.7 %collective-permute-start.9 = (bf16[64,1024]{1,0:T(8,128)(2,1)S(1)}, bf16[64,1024]{1,0:T(8,128)(2,1)S(1)}, u32[]{:S(2)}, u32[]{:S(2)}) collective-permute-start(bf16[64,1024]{1,0:T(8,128)(2,1)S(1)} %collective-permute-done.8.refs_1_), channel_id=1, source_target_pairs={{0,8},{1,9},{2,10},{3,11},{4,12},{5,13},{6,14},{7,15},{8,24},{9,25... | collective-permute-start | bytes 393224 | tf_op jit(solution)/shard_map/ppermute | solution.py:227
  82.4 7.3 %collective-permute-start.15 = (bf16[64,1024]{1,0:T(8,128)(2,1)S(1)}, bf16[64,1024]{1,0:T(8,128)(2,1)S(1)}, u32[]{:S(2)}, u32[]{:S(2)}) collective-permute-start(bf16[64,1024]{1,0:T(8,128)(2,1)S(1)} %collective-permute-done.14.refs_2_), channel_id=1, source_target_pairs={{0,8},{1,9},{2,10},{3,11},{4,12},{5,13},{6,14},{7,15},{8,24},{9,25... | collective-permute-start | bytes 393224 | tf_op jit(solution)/shard_map/ppermute | solution.py:227
  86.7 5.9 %collective-permute-start.10 = (bf16[64,1024]{1,0:T(8,128)(2,1)S(1)}, bf16[64,1024]{1,0:T(8,128)(2,1)S(1)}, u32[]{:S(2)}, u32[]{:S(2)}) collective-permute-start(bf16[64,1024]{1,0:T(8,128)(2,1)S(1)} %collective-permute-done.9.refs_2_), channel_id=1, source_target_pairs={{0,8},{1,9},{2,10},{3,11},{4,12},{5,13},{6,14},{7,15},{8,24},{9,25... | collective-permute-start | bytes 393224 | tf_op jit(solution)/shard_map/ppermute | solution.py:227
  91.0 6.2 %collective-permute-start.16 = (bf16[2,64,896]{2,1,0:T(8,128)(2,1)S(1)}, bf16[2,64,896]{2,1,0:T(8,128)(2,1)S(1)}, u32[]{:S(2)}, u32[]{:S(2)}) collective-permute-start(bf16[2,64,896]{2,1,0:T(8,128)(2,1)S(1)} %get-tuple-element.42), channel_id=1, source_target_pairs={{0,1},{1,0},{2,3},{3,2},{4,5},{5,4},{6,7},{7,6},{8,9},{9,8},{10,11... | collective-permute-start | bytes 688136 | tf_op jit(solution)/shard_map/ppermute | solution.py:227
  93.9 5.0 %collective-permute-start.11 = (bf16[2,64,896]{2,1,0:T(8,128)(2,1)S(1)}, bf16[2,64,896]{2,1,0:T(8,128)(2,1)S(1)}, u32[]{:S(2)}, u32[]{:S(2)}) collective-permute-start(bf16[2,64,896]{2,1,0:T(8,128)(2,1)S(1)} %get-tuple-element.38), channel_id=1, source_target_pairs={{0,1},{1,0},{2,3},{3,2},{4,5},{5,4},{6,7},{7,6},{8,9},{9,8},{10,11... | collective-permute-start | bytes 688136 | tf_op jit(solution)/shard_map/ppermute | solution.py:227
  95.3 4.2 %collective-permute-start.21 = (bf16[2,64,896]{2,1,0:T(8,128)(2,1)S(1)}, bf16[2,64,896]{2,1,0:T(8,128)(2,1)S(1)}, u32[]{:S(2)}, u32[]{:S(2)}) collective-permute-start(bf16[2,64,896]{2,1,0:T(8,128)(2,1)S(1)} %get-tuple-element.53), channel_id=1, source_target_pairs={{0,1},{1,0},{2,3},{3,2},{4,5},{5,4},{6,7},{7,6},{8,9},{9,8},{10,11... | collective-permute-start | bytes 688136 | tf_op jit(solution)/shard_map/ppermute | solution.py:227
  97.2 4.1 %collective-permute-start.19 = (bf16[2,64,896]{2,1,0:T(8,128)(2,1)S(1)}, bf16[2,64,896]{2,1,0:T(8,128)(2,1)S(1)}, u32[]{:S(2)}, u32[]{:S(2)}) collective-permute-start(bf16[2,64,896]{2,1,0:T(8,128)(2,1)S(1)} %get-tuple-element.46), channel_id=1, source_target_pairs={{0,1},{1,0},{2,3},{3,2},{4,5},{5,4},{6,7},{7,6},{8,9},{9,8},{10,11... | collective-permute-start | bytes 688136 | tf_op jit(solution)/shard_map/ppermute | solution.py:227
  97.3 6.1 %collective-permute-start.17 = (bf16[1,64,896]{2,1,0:T(8,128)(2,1)S(1)}, bf16[1,64,896]{2,1,0:T(8,128)(2,1)S(1)}, u32[]{:S(2)}, u32[]{:S(2)}) collective-permute-start(bf16[1,64,896]{2,1,0:T(8,128)(2,1)S(1)} %get-tuple-element.44), channel_id=1, source_target_pairs={{0,2},{1,3},{2,0},{3,1},{4,6},{5,7},{6,4},{7,5},{8,10},{9,11},{10,... | collective-permute-start | bytes 344072 | tf_op jit(solution)/shard_map/ppermute | solution.py:227
  99.0 6.9 %collective-permute-start.12 = (bf16[1,64,896]{2,1,0:T(8,128)(2,1)S(1)}, bf16[1,64,896]{2,1,0:T(8,128)(2,1)S(1)}, u32[]{:S(2)}, u32[]{:S(2)}) collective-permute-start(bf16[1,64,896]{2,1,0:T(8,128)(2,1)S(1)} %get-tuple-element.40), channel_id=1, source_target_pairs={{0,2},{1,3},{2,0},{3,1},{4,6},{5,7},{6,4},{7,5},{8,10},{9,11},{10,... | collective-permute-start | bytes 344072 | tf_op jit(solution)/shard_map/ppermute | solution.py:227
  99.6 8.7 %collective-permute-start.22 = (bf16[1,64,896]{2,1,0:T(8,128)(2,1)S(1)}, bf16[1,64,896]{2,1,0:T(8,128)(2,1)S(1)}, u32[]{:S(2)}, u32[]{:S(2)}) collective-permute-start(bf16[1,64,896]{2,1,0:T(8,128)(2,1)S(1)} %get-tuple-element.55), channel_id=1, source_target_pairs={{0,2},{1,3},{2,0},{3,1},{4,6},{5,7},{6,4},{7,5},{8,10},{9,11},{10,... | collective-permute-start | bytes 344072 | tf_op jit(solution)/shard_map/ppermute | solution.py:227
  101.3 9.0 %collective-permute-start.23 = (bf16[1,64,896]{2,1,0:T(8,128)(2,1)S(1)}, bf16[1,64,896]{2,1,0:T(8,128)(2,1)S(1)}, u32[]{:S(2)}, u32[]{:S(2)}) collective-permute-start(bf16[1,64,896]{2,1,0:T(8,128)(2,1)S(1)} %get-tuple-element.56), channel_id=1, source_target_pairs={{0,2},{1,3},{2,0},{3,1},{4,6},{5,7},{6,4},{7,5},{8,10},{9,11},{10,... | collective-permute-start | bytes 344072 | tf_op jit(solution)/shard_map/ppermute | solution.py:227
  105.9 5.2 %collective-permute-start.20 = (bf16[128,896]{1,0:T(8,128)(2,1)S(1)}, bf16[128,896]{1,0:T(8,128)(2,1)S(1)}, u32[]{:S(2)}, u32[]{:S(2)}) collective-permute-start(bf16[128,896]{1,0:T(8,128)(2,1)S(1)} %shard_map.93), channel_id=1, source_target_pairs={{0,0},{1,16},{2,8},{3,24},{4,4},{5,20},{6,12},{7,28},{8,1},{9,17},... | collective-permute-start | bytes 688136 | tf_op jit(solution)/shard_map/ppermute | solution.py:227
  110.3 8.5 %collective-permute-start.24 = (bf16[128,896]{1,0:T(8,128)(2,1)S(1)}, bf16[128,896]{1,0:T(8,128)(2,1)S(1)}, u32[]{:S(2)}, u32[]{:S(2)}) collective-permute-start(bf16[128,896]{1,0:T(8,128)(2,1)S(1)} %shard_map.96), channel_id=1, source_target_pairs={{0,8},{1,24},{2,0},{3,16},{4,12},{5,28},{6,4},{7,20},{8,9},{9,25},... | collective-permute-start | bytes 688136 | tf_op jit(solution)/shard_map/ppermute | solution.py:227

commit v4 on v3

--- a/solution.py
+++ b/solution.py
@@ -14,7 +14,6 @@
 VDIM = 128
 AXES = ("ctx", "head")
 MIB = 1024 * 1024
-COUNTS = ([1], [1])
 NT = (((1,), (1,)), ((), ()))
 
 
@@ -159,27 +158,6 @@
         out_ref[i * half : (i + 1) * half] = total.astype(out_ref.dtype)
 
 
-def output_kernel(counts, place_ref, *refs):
-    out_ref = refs[-1]
-    x = place_ref[3]
-    rows = out_ref.shape[0]
-    cols = refs[0].shape[1]
-    half = rows // 2
-
-    def rows_of(dx, span):
-        first = sum(counts[:dx])
-        if counts[dx] == 2:
-            return refs[first + span][...]
-        return refs[first][span * half : (span + 1) * half]
-
-    for at in range(len(counts)):
-        for span in range(2):
-            block = rows_of(0, span)
-            for dx in range(1, len(counts)):
-                block = jnp.where((x ^ at) == dx, rows_of(dx, span), block)
-            out_ref[span * half : (span + 1) * half, at * cols : (at + 1) * cols] = block
-
-
 def whole():
     return pl.BlockSpec(memory_space=pltpu.VMEM)
 
@@ -265,7 +243,7 @@
         return 2 * queries_n * heads * keys_n * (2 * LAT + ROPE)
 
     early = call(
-        functools.partial(early_kernel, pairs[:first], 2, scale),
+        functools.partial(early_kernel, pairs[:first], 4, scale),
         ((heads, rows, LAT + 128), f32),
         (span_order, place, queries, keys, *direct[:first], *passed[:first]),
         smem=2,
@@ -274,8 +252,9 @@
         flops=work(rows, n_early * rows),
         exps=rows * heads * n_early * rows,
     )
-    direct[first:], early = lax.optimization_barrier((direct[first:], early))
-    passed += [send(direct[i], to_other(pairs[i])) for i in range(first, len(pairs))]
+    for i in range(first, len(pairs)):
+        direct[i], early = lax.optimization_barrier((direct[i], early))
+        passed.append(send(direct[i], to_other(pairs[i])))
     blocks = []
     for span in range(2):
         heads_out = call(
@@ -294,7 +273,7 @@
         blocks.append(along)
 
     results = []
-    counts = COUNTS[0] * (xs - 1) + COUNTS[1]
+    counts = [1] * xs
     sums = {}
     for dx, count in enumerate(counts):
         for span in range(2):
@@ -332,12 +311,13 @@
             block = call(add_kernel, ((rows // count, cols), bf16), piece)
             flip = sums[dx, i][2]
             results.append(send(block, lambda z, x, y, k: (k * zl + (y ^ flip), x, z // 2, z % 2)))
-    return call(
-        functools.partial(output_kernel, counts),
-        ((rows, xs * cols), bf16),
-        (place, *results),
-        smem=1,
-    )
+    columns = []
+    for at in range(xs):
+        block = results[0]
+        for dx in range(1, xs):
+            block = jnp.where((x ^ at) == dx, results[dx], block)
+        columns.append(block)
+    return jnp.concatenate(columns, axis=1)
 
 
 def solution(mesh):

time: 122 us -> 120 us (0.984)
  waiting for transfers between devices: 68.9 us -> 65.7 us
  starting transfers between devices: 29.3 us -> 31.6 us
  Pallas kernels: 20.5 us -> 18.8 us
    ppermute x25, waiting for transfers between devices: 68.9 us -> 65.7 us  [send(): return lax.ppermute(value, AXES, pairs)]
    ppermute x25, starting transfers between devices: 29.3 us -> 31.6 us  [send(): return lax.ppermute(value, AXES, pairs)]
    pallas_call x16 -> x15, Pallas kernels: 20.5 us -> 18.8 us  [call(): pl.pallas_call(kernel, out_shape=shapes, in_specs=[pl.BlockSpec(memory_sp...]
  transfers between devices with their start and end apart: 25 -> 25, of which waited for: 16 -> 15; matrix products, arithmetic and copies ran while one was open for 0% -> 0% of each run, Pallas kernels for 16% -> 16%
where the time goes in v4:
time: 120 us; the launch traced here: 118 us
  waiting for transfers between devices  65.7 us (55%)
  starting transfers between devices  31.6 us (26%)
  Pallas kernels  18.8 us (16%)
  local copies, waits for them, and re-layouts  1.41 us (1%)
    ppermute x25, waiting for transfers between devices, send(): return lax.ppermute(value, AXES, pairs)  65.7 us
    ppermute x25, starting transfers between devices, send(): return lax.ppermute(value, AXES, pairs)  31.6 us
    pallas_call x15, Pallas kernels, call(): pl.pallas_call(kernel, out_shape=shapes, in_specs=[pl.BlockSpec(memory_sp...  18.8 us
  transfers between devices with their start and end apart: 25, of which 15 were waited for; matrix products, arithmetic and copies ran while one was open for 0% of the time, Pallas kernels for 16%

profile of v4, /device:TPU:0, one launch (start us, length us, event | category | flops | bytes accessed | tf_op | source)
XLA Modules:
  0.0 118.5 jit_solution(3783511460452660946)
XLA Ops:
  0.0 3.0 %collective-permute-start = (bf16[1024,896]{1,0:T(8,128)(2,1)}, bf16[1024,896]{1,0:T(8,128)(2,1)S(1)}, u32[]{:S(2)}, u32[]{:S(2)}) collective-permute-start(bf16[1024,896]{1,0:T(8,128)(2,1)} %w_ref.9), channel_id=1, source_target_pairs={{0,4},{1,5},{2,6},{3,7},{4,0},{5,1},{6,2},{7,3},{8,12},{9,13},{10,... | collective-permute-start | bytes 5505032 | tf_op jit(solution)/shard_map/ppermute | solution.py:205
  3.0 1.6 %shard_map.82.own_ref = bf16[128,576]{1,0:T(8,128)(2,1)} custom-call(bf16[128,512]{1,0:T(8,128)(2,1)} %latent_ref.1, bf16[64,128]{1,0:T(8,128)(2,1)} %bitcast.7), custom_call_target="tpu_custom_call" | custom-call | bytes 294912 | tf_op jit(solution)/shard_map/pallas_call | solution.py:170
  4.6 1.5 %collective-permute-start.2 = (bf16[128,576]{1,0:T(8,128)(2,1)}, bf16[128,576]{1,0:T(8,128)(2,1)S(1)}, u32[]{:S(2)}, u32[]{:S(2)}) collective-permute-start(bf16[128,576]{1,0:T(8,128)(2,1)} %shard_map.82.own_ref), channel_id=1, source_target_pairs={{0,12},{1,17},{2,14},{3,19},{4,8},{5,21},{6,10},{7,23},{8,4},{9,25... | collective-permute-start | bytes 442376 | tf_op jit(solution)/shard_map/ppermute | solution.py:205
  6.2 1.5 %collective-permute-start.1 = (bf16[128,576]{1,0:T(8,128)(2,1)}, bf16[128,576]{1,0:T(8,128)(2,1)S(1)}, u32[]{:S(2)}, u32[]{:S(2)}) collective-permute-start(bf16[128,576]{1,0:T(8,128)(2,1)} %shard_map.82.own_ref), channel_id=1, source_target_pairs={{0,4},{1,9},{2,6},{3,11},{4,0},{5,13},{6,2},{7,15},{8,12},{9,1},{1... | collective-permute-start | bytes 442376 | tf_op jit(solution)/shard_map/ppermute | solution.py:205
  7.7 2.9 %shard_map.83.q_ref = bf16[8,128,576]{2,1,0:T(8,128)(2,1)} custom-call(bf16[128,1024]{1,0:T(8,128)(2,1)} %q_ref.1, bf16[128,512]{1,0:T(8,128)(2,1)} %rope_ref.1, bf16[512,1024]{1,0:T(8,128)(2,1)} %w_ref.5), custom_call_target="tpu_custom_call" | custom-call | flops 134217728 | bytes 2621440 | tf_op jit(solution)/shard_map/pallas_call | solution.py:170
  10.6 3.0 %collective-permute-done.2.refs_1_ = bf16[128,576]{1,0:T(8,128)(2,1)S(1)} collective-permute-done((bf16[128,576]{1,0:T(8,128)(2,1)}, bf16[128,576]{1,0:T(8,128)(2,1)S(1)}, u32[]{:S(2)}, u32[]{:S(2)}) %collective-permute-start.2) | collective-permute-done | bytes 147488 | tf_op jit(solution)/shard_map/ppermute | solution.py:205
  13.5 33.2 %collective-permute-done.1.refs_0_ = bf16[128,576]{1,0:T(8,128)(2,1)S(1)} collective-permute-done((bf16[128,576]{1,0:T(8,128)(2,1)}, bf16[128,576]{1,0:T(8,128)(2,1)S(1)}, u32[]{:S(2)}, u32[]{:S(2)}) %collective-permute-start.1) | collective-permute-done | bytes 147488 | tf_op jit(solution)/shard_map/ppermute | solution.py:205
  47.2 3.8 %collective-permute-start.4 = (bf16[128,576]{1,0:T(8,128)(2,1)S(1)}, bf16[128,576]{1,0:T(8,128)(2,1)S(1)}, u32[]{:S(2)}, u32[]{:S(2)}) collective-permute-start(bf16[128,576]{1,0:T(8,128)(2,1)S(1)} %copy-done.3), channel_id=1, source_target_pairs={{0,20},{1,25},{2,22},{3,27},{4,16},{5,29},{6,18},{7,31},{8,28},{9,... | collective-permute-start | bytes 442376 | tf_op jit(solution)/shard_map/ppermute | solution.py:205
  51.8 1.3 %copy-done = bf16[8,128,576]{2,1,0:T(8,128)(2,1)S(1)} copy-done((bf16[8,128,576]{2,1,0:T(8,128)(2,1)S(1)}, bf16[8,128,576]{2,1,0:T(8,128)(2,1)}, u32[]{:S(2)}) %copy-start) | copy-done | bytes 1179672
  53.1 3.4 %shard_map.84.early_ref = f32[8,128,640]{2,1,0:T(8,128)S(1)} custom-call(s32[16]{0:T(128)S(1)} %copy-done.4, s32[6]{0:T(128)S(1)} %stack.24.place_ref, bf16[8,128,576]{2,1,0:T(8,128)(2,1)S(1)} %copy-done, bf16[128,576]{1,0:T(8,128)(2,1)S(1)} %copy-done.3, bf16[128,576]{1,0:T(8,128)(2,1)S(1)} %collective-permute-done.1.refs_0_, ...), custom_call_target="tpu_custom_call" | custom-call | flops 1426063360 | bytes 4538456 | tf_op jit(solution)/shard_map/pallas_call | solution.py:170
  56.5 4.9 %collective-permute-done.4.refs_0_ = bf16[128,576]{1,0:T(8,128)(2,1)S(1)} collective-permute-done((bf16[128,576]{1,0:T(8,128)(2,1)S(1)}, bf16[128,576]{1,0:T(8,128)(2,1)S(1)}, u32[]{:S(2)}, u32[]{:S(2)}) %collective-permute-start.4) | collective-permute-done | bytes 147488 | tf_op jit(solution)/shard_map/ppermute | solution.py:205
  64.9 2.6 %shard_map.88.refs_0_ = bf16[64,1024]{1,0:T(8,128)(2,1)S(1)} custom-call(s32[16]{0:T(128)S(1)} %copy-done.4, s32[6]{0:T(128)S(1)} %stack.24.place_ref, bf16[8,128,576]{2,1,0:T(8,128)(2,1)S(1)} %copy-done, bf16[512,1024]{1,0:T(8,128)(2,1)S(1)} %copy-done.2, f32[8,128,640]{2,1,0:T(8,128)S(1)} %shard_map.84.early_ref, ...), custom_call_target="tpu_custom_call" | custom-call | flops 494927872 | bytes 5570648 | tf_op jit(solution)/shard_map/pallas_call | solution.py:170
  68.0 2.6 %shard_map.85.refs_0_ = bf16[64,1024]{1,0:T(8,128)(2,1)S(1)} custom-call(s32[16]{0:T(128)S(1)} %copy-done.4, s32[6]{0:T(128)S(1)} %stack.24.place_ref, bf16[8,128,576]{2,1,0:T(8,128)(2,1)S(1)} %copy-done, bf16[512,1024]{1,0:T(8,128)(2,1)S(1)} %copy-done.2, f32[8,128,640]{2,1,0:T(8,128)S(1)} %shard_map.84.early_ref, ...), custom_call_target="tpu_custom_call" | custom-call | flops 494927872 | bytes 5570648 | tf_op jit(solution)/shard_map/pallas_call | solution.py:170
  70.6 3.9 %collective-permute-start.9 = (bf16[64,1024]{1,0:T(8,128)(2,1)S(1)}, bf16[64,1024]{1,0:T(8,128)(2,1)S(1)}, u32[]{:S(2)}, u32[]{:S(2)}) collective-permute-start(bf16[64,1024]{1,0:T(8,128)(2,1)S(1)} %shard_map.85.refs_0_), channel_id=1, source_target_pairs={{0,8},{1,9},{2,10},{3,11},{4,12},{5,13},{6,14},{7,15},{8,24},{9,25... | collective-permute-start | bytes 393224 | tf_op jit(solution)/shard_map/ppermute | solution.py:205
  75.2 3.2 %collective-permute-done.9.refs_1_ = bf16[64,1024]{1,0:T(8,128)(2,1)S(1)} collective-permute-done((bf16[64,1024]{1,0:T(8,128)(2,1)S(1)}, bf16[64,1024]{1,0:T(8,128)(2,1)S(1)}, u32[]{:S(2)}, u32[]{:S(2)}) %collective-permute-start.9) | collective-permute-done | bytes 131104 | tf_op jit(solution)/shard_map/ppermute | solution.py:205
  78.4 2.5 %collective-permute-start.10 = (bf16[64,1024]{1,0:T(8,128)(2,1)S(1)}, bf16[64,1024]{1,0:T(8,128)(2,1)S(1)}, u32[]{:S(2)}, u32[]{:S(2)}) collective-permute-start(bf16[64,1024]{1,0:T(8,128)(2,1)S(1)} %collective-permute-done.9.refs_1_), channel_id=1, source_target_pairs={{0,8},{1,9},{2,10},{3,11},{4,12},{5,13},{6,14},{7,15},{8,24},{9,25... | collective-permute-start | bytes 393224 | tf_op jit(solution)/shard_map/ppermute | solution.py:205
  81.2 2.5 %collective-permute-start.16 = (bf16[64,1024]{1,0:T(8,128)(2,1)S(1)}, bf16[64,1024]{1,0:T(8,128)(2,1)S(1)}, u32[]{:S(2)}, u32[]{:S(2)}) collective-permute-start(bf16[64,1024]{1,0:T(8,128)(2,1)S(1)} %collective-permute-done.15.refs_2_), channel_id=1, source_target_pairs={{0,8},{1,9},{2,10},{3,11},{4,12},{5,13},{6,14},{7,15},{8,24},{9,25... | collective-permute-start | bytes 393224 | tf_op jit(solution)/shard_map/ppermute | solution.py:205
  83.7 1.8 %collective-permute-done.10.refs_2_ = bf16[64,1024]{1,0:T(8,128)(2,1)S(1)} collective-permute-done((bf16[64,1024]{1,0:T(8,128)(2,1)S(1)}, bf16[64,1024]{1,0:T(8,128)(2,1)S(1)}, u32[]{:S(2)}, u32[]{:S(2)}) %collective-permute-start.10) | collective-permute-done | bytes 131104 | tf_op jit(solution)/shard_map/ppermute | solution.py:205
  85.5 1.6 %collective-permute-start.11 = (bf16[64,1024]{1,0:T(8,128)(2,1)S(1)}, bf16[64,1024]{1,0:T(8,128)(2,1)S(1)}, u32[]{:S(2)}, u32[]{:S(2)}) collective-permute-start(bf16[64,1024]{1,0:T(8,128)(2,1)S(1)} %collective-permute-done.10.refs_2_), channel_id=1, source_target_pairs={{0,8},{1,9},{2,10},{3,11},{4,12},{5,13},{6,14},{7,15},{8,24},{9,25... | collective-permute-start | bytes 393224 | tf_op jit(solution)/shard_map/ppermute | solution.py:205
  87.1 1.4 %collective-permute-done.16.refs_3_ = bf16[64,1024]{1,0:T(8,128)(2,1)S(1)} collective-permute-done((bf16[64,1024]{1,0:T(8,128)(2,1)S(1)}, bf16[64,1024]{1,0:T(8,128)(2,1)S(1)}, u32[]{:S(2)}, u32[]{:S(2)}) %collective-permute-start.16) | collective-permute-done | bytes 131104 | tf_op jit(solution)/shard_map/ppermute | solution.py:205
  88.5 1.3 %shard_map.94 = (f32[2,64,896]{2,1,0:T(8,128)S(1)}, bf16[2,64,896]{2,1,0:T(8,128)(2,1)S(1)}) custom-call(s32[6]{0:T(128)S(1)} %stack.24.place_ref, bf16[1024,896]{1,0:T(8,128)(2,1)S(1)} %copy-done.1, bf16[64,1024]{1,0:T(8,128)(2,1)S(1)} %shard_map.88.refs_0_, bf16[64,1024]{1,0:T(8,128)(2,1)S(1)} %collective-permute-done.14.refs_1_, ...), custom_call_target="tpu_custom_call" | custom-call | flops 469762048 | bytes 3047448 | tf_op jit(solution)/shard_map/pallas_call | solution.py:170
  89.9 1.4 %collective-permute-done.11.refs_3_ = bf16[64,1024]{1,0:T(8,128)(2,1)S(1)} collective-permute-done((bf16[64,1024]{1,0:T(8,128)(2,1)S(1)}, bf16[64,1024]{1,0:T(8,128)(2,1)S(1)}, u32[]{:S(2)}, u32[]{:S(2)}) %collective-permute-start.11) | collective-permute-done | bytes 131104 | tf_op jit(solution)/shard_map/ppermute | solution.py:205
  91.3 1.3 %shard_map.92 = (f32[2,64,896]{2,1,0:T(8,128)S(1)}, bf16[2,64,896]{2,1,0:T(8,128)(2,1)S(1)}) custom-call(s32[6]{0:T(128)S(1)} %stack.24.place_ref, bf16[1024,896]{1,0:T(8,128)(2,1)S(1)} %copy-done.1, bf16[64,1024]{1,0:T(8,128)(2,1)S(1)} %shard_map.85.refs_0_, bf16[64,1024]{1,0:T(8,128)(2,1)S(1)} %collective-permute-done.9.refs_1_, ...), custom_call_target="tpu_custom_call" | custom-call | flops 469762048 | bytes 3047448 | tf_op jit(solution)/shard_map/pallas_call | solution.py:170
  92.7 1.3 %shard_map.89 = (f32[2,64,896]{2,1,0:T(8,128)S(1)}, bf16[2,64,896]{2,1,0:T(8,128)(2,1)S(1)}) custom-call(s32[6]{0:T(128)S(1)} %stack.24.place_ref, bf16[1024,896]{1,0:T(8,128)(2,1)S(1)} %collective-permute-done.w_ref, bf16[64,1024]{1,0:T(8,128)(2,1)S(1)} %shard_map.88.refs_0_, bf16[64,1024]{1,0:T(8,128)(2,1)S(1)} %collective-permute-done.14.refs_1_, ...), custom_call_target="tpu_custom_call" | custom-call | flops 469762048 | bytes 3047448 | tf_op jit(solution)/shard_map/pallas_call | solution.py:170
  94.6 1.3 %shard_map.86 = (f32[2,64,896]{2,1,0:T(8,128)S(1)}, bf16[2,64,896]{2,1,0:T(8,128)(2,1)S(1)}) custom-call(s32[6]{0:T(128)S(1)} %stack.24.place_ref, bf16[1024,896]{1,0:T(8,128)(2,1)S(1)} %collective-permute-done.w_ref, bf16[64,1024]{1,0:T(8,128)(2,1)S(1)} %shard_map.85.refs_0_, bf16[64,1024]{1,0:T(8,128)(2,1)S(1)} %collective-permute-done.9.refs_1_, ...), custom_call_target="tpu_custom_call" | custom-call | flops 469762048 | bytes 3047448 | tf_op jit(solution)/shard_map/pallas_call | solution.py:170
  96.1 1.6 %collective-permute-start.23 = (bf16[1,64,896]{2,1,0:T(8,128)(2,1)S(1)}, bf16[1,64,896]{2,1,0:T(8,128)(2,1)S(1)}, u32[]{:S(2)}, u32[]{:S(2)}) collective-permute-start(bf16[1,64,896]{2,1,0:T(8,128)(2,1)S(1)} %get-tuple-element.54), channel_id=1, source_target_pairs={{0,2},{1,3},{2,0},{3,1},{4,6},{5,7},{6,4},{7,5},{8,10},{9,11},{10,... | collective-permute-start | bytes 344072 | tf_op jit(solution)/shard_map/ppermute | solution.py:205
  98.4 1.6 %collective-permute-start.18 = (bf16[1,64,896]{2,1,0:T(8,128)(2,1)S(1)}, bf16[1,64,896]{2,1,0:T(8,128)(2,1)S(1)}, u32[]{:S(2)}, u32[]{:S(2)}) collective-permute-start(bf16[1,64,896]{2,1,0:T(8,128)(2,1)S(1)} %get-tuple-element.46), channel_id=1, source_target_pairs={{0,2},{1,3},{2,0},{3,1},{4,6},{5,7},{6,4},{7,5},{8,10},{9,11},{10,... | collective-permute-start | bytes 344072 | tf_op jit(solution)/shard_map/ppermute | solution.py:205
  100.6 1.6 %collective-permute-done.23.refs_3_ = bf16[1,64,896]{2,1,0:T(8,128)(2,1)S(1)} collective-permute-done((bf16[1,64,896]{2,1,0:T(8,128)(2,1)S(1)}, bf16[1,64,896]{2,1,0:T(8,128)(2,1)S(1)}, u32[]{:S(2)}, u32[]{:S(2)}) %collective-permute-start.23) | collective-permute-done | bytes 114720 | tf_op jit(solution)/shard_map/ppermute | solution.py:205
  102.2 2.5 %collective-permute-done.21.refs_1_ = bf16[1,64,896]{2,1,0:T(8,128)(2,1)S(1)} collective-permute-done((bf16[1,64,896]{2,1,0:T(8,128)(2,1)S(1)}, bf16[1,64,896]{2,1,0:T(8,128)(2,1)S(1)}, u32[]{:S(2)}, u32[]{:S(2)}) %collective-permute-start.21) | collective-permute-done | bytes 114720 | tf_op jit(solution)/shard_map/ppermute | solution.py:205
  105.4 1.7 %collective-permute-done.18.refs_3_ = bf16[1,64,896]{2,1,0:T(8,128)(2,1)S(1)} collective-permute-done((bf16[1,64,896]{2,1,0:T(8,128)(2,1)S(1)}, bf16[1,64,896]{2,1,0:T(8,128)(2,1)S(1)}, u32[]{:S(2)}, u32[]{:S(2)}) %collective-permute-start.18) | collective-permute-done | bytes 114720 | tf_op jit(solution)/shard_map/ppermute | solution.py:205
  107.1 2.0 %collective-permute-done.13.refs_1_ = bf16[1,64,896]{2,1,0:T(8,128)(2,1)S(1)} collective-permute-done((bf16[1,64,896]{2,1,0:T(8,128)(2,1)S(1)}, bf16[1,64,896]{2,1,0:T(8,128)(2,1)S(1)}, u32[]{:S(2)}, u32[]{:S(2)}) %collective-permute-start.13) | collective-permute-done | bytes 114720 | tf_op jit(solution)/shard_map/ppermute | solution.py:205
  109.9 7.8 %collective-permute-done.19 = bf16[128,896]{1,0:T(8,128)(2,1)S(1)} collective-permute-done((bf16[128,896]{1,0:T(8,128)(2,1)S(1)}, bf16[128,896]{1,0:T(8,128)(2,1)S(1)}, u32[]{:S(2)}, u32[]{:S(2)}) %collective-permute-start.19) | collective-permute-done | bytes 229408 | tf_op jit(solution)/shard_map/ppermute | solution.py:205
  (46 shorter events, 10.8 us)
Async XLA Ops:
  0.0 51.8 %copy-start.4 = (s32[16]{0:T(128)S(1)}, s32[16]{0:T(128)}, u32[]{:S(2)}) copy-start(s32[16]{0:T(128)} %order_ref.5) | copy-start | bytes 196
  0.0 92.7 %collective-permute-start = (bf16[1024,896]{1,0:T(8,128)(2,1)}, bf16[1024,896]{1,0:T(8,128)(2,1)S(1)}, u32[]{:S(2)}, u32[]{:S(2)}) collective-permute-start(bf16[1024,896]{1,0:T(8,128)(2,1)} %w_ref.9), channel_id=1, source_target_pairs={{0,4},{1,5},{2,6},{3,7},{4,0},{5,1},{6,2},{7,3},{8,12},{9,13},{10,... | collective-permute-start | bytes 5505032 | tf_op jit(solution)/shard_map/ppermute | solution.py:205
  4.6 42.6 %copy-start.3 = (bf16[128,576]{1,0:T(8,128)(2,1)S(1)}, bf16[128,576]{1,0:T(8,128)(2,1)}, u32[]{:S(2)}) copy-start(bf16[128,576]{1,0:T(8,128)(2,1)} %shard_map.82.own_ref) | copy-start | bytes 442372
  4.6 8.9 %collective-permute-start.2 = (bf16[128,576]{1,0:T(8,128)(2,1)}, bf16[128,576]{1,0:T(8,128)(2,1)S(1)}, u32[]{:S(2)}, u32[]{:S(2)}) collective-permute-start(bf16[128,576]{1,0:T(8,128)(2,1)} %shard_map.82.own_ref), channel_id=1, source_target_pairs={{0,12},{1,17},{2,14},{3,19},{4,8},{5,21},{6,10},{7,23},{8,4},{9,25... | collective-permute-start | bytes 442376 | tf_op jit(solution)/shard_map/ppermute | solution.py:205
  6.2 40.5 %collective-permute-start.1 = (bf16[128,576]{1,0:T(8,128)(2,1)}, bf16[128,576]{1,0:T(8,128)(2,1)S(1)}, u32[]{:S(2)}, u32[]{:S(2)}) collective-permute-start(bf16[128,576]{1,0:T(8,128)(2,1)} %shard_map.82.own_ref), channel_id=1, source_target_pairs={{0,4},{1,9},{2,6},{3,11},{4,0},{5,13},{6,2},{7,15},{8,12},{9,1},{1... | collective-permute-start | bytes 442376 | tf_op jit(solution)/shard_map/ppermute | solution.py:205
  46.7 5.1 %collective-permute-start.5 = (bf16[128,576]{1,0:T(8,128)(2,1)S(1)}, bf16[128,576]{1,0:T(8,128)(2,1)S(1)}, u32[]{:S(2)}, u32[]{:S(2)}) collective-permute-start(bf16[128,576]{1,0:T(8,128)(2,1)S(1)} %collective-permute-done.1.refs_0_), channel_id=1, source_target_pairs={{0,1},{1,0},{2,3},{3,2},{4,5},{5,4},{6,7},{7,6},{8,9},{9,8},{10,11... | collective-permute-start | bytes 442376 | tf_op jit(solution)/shard_map/ppermute | solution.py:205
  46.7 5.1 %collective-permute-start.6 = (bf16[128,576]{1,0:T(8,128)(2,1)S(1)}, bf16[128,576]{1,0:T(8,128)(2,1)S(1)}, u32[]{:S(2)}, u32[]{:S(2)}) collective-permute-start(bf16[128,576]{1,0:T(8,128)(2,1)S(1)} %collective-permute-done.2.refs_1_), channel_id=1, source_target_pairs={{0,1},{1,0},{2,3},{3,2},{4,5},{5,4},{6,7},{7,6},{8,9},{9,8},{10,11... | collective-permute-start | bytes 442376 | tf_op jit(solution)/shard_map/ppermute | solution.py:205
  47.2 14.1 %collective-permute-start.4 = (bf16[128,576]{1,0:T(8,128)(2,1)S(1)}, bf16[128,576]{1,0:T(8,128)(2,1)S(1)}, u32[]{:S(2)}, u32[]{:S(2)}) collective-permute-start(bf16[128,576]{1,0:T(8,128)(2,1)S(1)} %copy-done.3), channel_id=1, source_target_pairs={{0,20},{1,25},{2,22},{3,27},{4,16},{5,29},{6,18},{7,31},{8,28},{9,... | collective-permute-start | bytes 442376 | tf_op jit(solution)/shard_map/ppermute | solution.py:205
  51.0 10.4 %collective-permute-start.3 = (bf16[128,576]{1,0:T(8,128)(2,1)S(1)}, bf16[128,576]{1,0:T(8,128)(2,1)S(1)}, u32[]{:S(2)}, u32[]{:S(2)}) collective-permute-start(bf16[128,576]{1,0:T(8,128)(2,1)S(1)} %copy-done.3), channel_id=1, source_target_pairs={{1,29},{3,31},{5,25},{7,27},{9,21},{11,23},{13,17},{15,19},{17,13}... | collective-permute-start | bytes 442376 | tf_op jit(solution)/shard_map/ppermute | solution.py:205
  51.8 1.3 %copy-start = (bf16[8,128,576]{2,1,0:T(8,128)(2,1)S(1)}, bf16[8,128,576]{2,1,0:T(8,128)(2,1)}, u32[]{:S(2)}) copy-start(bf16[8,128,576]{2,1,0:T(8,128)(2,1)} %shard_map.83.q_ref) | copy-start | bytes 3538948
  53.1 11.8 %copy-start.2 = (bf16[512,1024]{1,0:T(8,128)(2,1)S(1)}, bf16[512,1024]{1,0:T(8,128)(2,1)}, u32[]{:S(2)}) copy-start(bf16[512,1024]{1,0:T(8,128)(2,1)} %w_ref.7) | copy-start | bytes 3145732
  61.4 3.3 %collective-permute-start.8 = (bf16[128,576]{1,0:T(8,128)(2,1)S(1)}, bf16[128,576]{1,0:T(8,128)(2,1)S(1)}, u32[]{:S(2)}, u32[]{:S(2)}) collective-permute-start(bf16[128,576]{1,0:T(8,128)(2,1)S(1)} %collective-permute-done.3.refs_1_), channel_id=1, source_target_pairs={{1,0},{3,2},{5,4},{7,6},{9,8},{11,10},{13,12},{15,14},{17,16},{19,... | collective-permute-start | bytes 442376 | tf_op jit(solution)/shard_map/ppermute | solution.py:205
  62.6 2.2 %collective-permute-start.7 = (bf16[128,576]{1,0:T(8,128)(2,1)S(1)}, bf16[128,576]{1,0:T(8,128)(2,1)S(1)}, u32[]{:S(2)}, u32[]{:S(2)}) collective-permute-start(bf16[128,576]{1,0:T(8,128)(2,1)S(1)} %collective-permute-done.4.refs_0_), channel_id=1, source_target_pairs={{0,1},{1,0},{2,3},{3,2},{4,5},{5,4},{6,7},{7,6},{8,9},{9,8},{10,11... | collective-permute-start | bytes 442376 | tf_op jit(solution)/shard_map/ppermute | solution.py:205
  67.5 21.0 %copy-start.1 = (bf16[1024,896]{1,0:T(8,128)(2,1)S(1)}, bf16[1024,896]{1,0:T(8,128)(2,1)}, u32[]{:S(2)}) copy-start(bf16[1024,896]{1,0:T(8,128)(2,1)} %w_ref.9) | copy-start | bytes 5505028
  67.5 7.0 %collective-permute-start.14 = (bf16[64,1024]{1,0:T(8,128)(2,1)S(1)}, bf16[64,1024]{1,0:T(8,128)(2,1)S(1)}, u32[]{:S(2)}, u32[]{:S(2)}) collective-permute-start(bf16[64,1024]{1,0:T(8,128)(2,1)S(1)} %shard_map.88.refs_0_), channel_id=1, source_target_pairs={{0,8},{1,9},{2,10},{3,11},{4,12},{5,13},{6,14},{7,15},{8,24},{9,25... | collective-permute-start | bytes 393224 | tf_op jit(solution)/shard_map/ppermute | solution.py:205
  70.6 7.8 %collective-permute-start.9 = (bf16[64,1024]{1,0:T(8,128)(2,1)S(1)}, bf16[64,1024]{1,0:T(8,128)(2,1)S(1)}, u32[]{:S(2)}, u32[]{:S(2)}) collective-permute-start(bf16[64,1024]{1,0:T(8,128)(2,1)S(1)} %shard_map.85.refs_0_), channel_id=1, source_target_pairs={{0,8},{1,9},{2,10},{3,11},{4,12},{5,13},{6,14},{7,15},{8,24},{9,25... | collective-permute-start | bytes 393224 | tf_op jit(solution)/shard_map/ppermute | solution.py:205
  74.5 6.7 %collective-permute-start.15 = (bf16[64,1024]{1,0:T(8,128)(2,1)S(1)}, bf16[64,1024]{1,0:T(8,128)(2,1)S(1)}, u32[]{:S(2)}, u32[]{:S(2)}) collective-permute-start(bf16[64,1024]{1,0:T(8,128)(2,1)S(1)} %collective-permute-done.14.refs_1_), channel_id=1, source_target_pairs={{0,8},{1,9},{2,10},{3,11},{4,12},{5,13},{6,14},{7,15},{8,24},{9,25... | collective-permute-start | bytes 393224 | tf_op jit(solution)/shard_map/ppermute | solution.py:205
  78.4 7.1 %collective-permute-start.10 = (bf16[64,1024]{1,0:T(8,128)(2,1)S(1)}, bf16[64,1024]{1,0:T(8,128)(2,1)S(1)}, u32[]{:S(2)}, u32[]{:S(2)}) collective-permute-start(bf16[64,1024]{1,0:T(8,128)(2,1)S(1)} %collective-permute-done.9.refs_1_), channel_id=1, source_target_pairs={{0,8},{1,9},{2,10},{3,11},{4,12},{5,13},{6,14},{7,15},{8,24},{9,25... | collective-permute-start | bytes 393224 | tf_op jit(solution)/shard_map/ppermute | solution.py:205
  81.2 7.3 %collective-permute-start.16 = (bf16[64,1024]{1,0:T(8,128)(2,1)S(1)}, bf16[64,1024]{1,0:T(8,128)(2,1)S(1)}, u32[]{:S(2)}, u32[]{:S(2)}) collective-permute-start(bf16[64,1024]{1,0:T(8,128)(2,1)S(1)} %collective-permute-done.15.refs_2_), channel_id=1, source_target_pairs={{0,8},{1,9},{2,10},{3,11},{4,12},{5,13},{6,14},{7,15},{8,24},{9,25... | collective-permute-start | bytes 393224 | tf_op jit(solution)/shard_map/ppermute | solution.py:205
  85.5 5.9 %collective-permute-start.11 = (bf16[64,1024]{1,0:T(8,128)(2,1)S(1)}, bf16[64,1024]{1,0:T(8,128)(2,1)S(1)}, u32[]{:S(2)}, u32[]{:S(2)}) collective-permute-start(bf16[64,1024]{1,0:T(8,128)(2,1)S(1)} %collective-permute-done.10.refs_2_), channel_id=1, source_target_pairs={{0,8},{1,9},{2,10},{3,11},{4,12},{5,13},{6,14},{7,15},{8,24},{9,25... | collective-permute-start | bytes 393224 | tf_op jit(solution)/shard_map/ppermute | solution.py:205
  89.8 6.2 %collective-permute-start.22 = (bf16[2,64,896]{2,1,0:T(8,128)(2,1)S(1)}, bf16[2,64,896]{2,1,0:T(8,128)(2,1)S(1)}, u32[]{:S(2)}, u32[]{:S(2)}) collective-permute-start(bf16[2,64,896]{2,1,0:T(8,128)(2,1)S(1)} %get-tuple-element.52), channel_id=1, source_target_pairs={{0,1},{1,0},{2,3},{3,2},{4,5},{5,4},{6,7},{7,6},{8,9},{9,8},{10,11... | collective-permute-start | bytes 688136 | tf_op jit(solution)/shard_map/ppermute | solution.py:205
  92.6 5.0 %collective-permute-start.20 = (bf16[2,64,896]{2,1,0:T(8,128)(2,1)S(1)}, bf16[2,64,896]{2,1,0:T(8,128)(2,1)S(1)}, u32[]{:S(2)}, u32[]{:S(2)}) collective-permute-start(bf16[2,64,896]{2,1,0:T(8,128)(2,1)S(1)} %get-tuple-element.48), channel_id=1, source_target_pairs={{0,1},{1,0},{2,3},{3,2},{4,5},{5,4},{6,7},{7,6},{8,9},{9,8},{10,11... | collective-permute-start | bytes 688136 | tf_op jit(solution)/shard_map/ppermute | solution.py:205
  94.1 4.2 %collective-permute-start.17 = (bf16[2,64,896]{2,1,0:T(8,128)(2,1)S(1)}, bf16[2,64,896]{2,1,0:T(8,128)(2,1)S(1)}, u32[]{:S(2)}, u32[]{:S(2)}) collective-permute-start(bf16[2,64,896]{2,1,0:T(8,128)(2,1)S(1)} %get-tuple-element.44), channel_id=1, source_target_pairs={{0,1},{1,0},{2,3},{3,2},{4,5},{5,4},{6,7},{7,6},{8,9},{9,8},{10,11... | collective-permute-start | bytes 688136 | tf_op jit(solution)/shard_map/ppermute | solution.py:205
  95.9 4.0 %collective-permute-start.12 = (bf16[2,64,896]{2,1,0:T(8,128)(2,1)S(1)}, bf16[2,64,896]{2,1,0:T(8,128)(2,1)S(1)}, u32[]{:S(2)}, u32[]{:S(2)}) collective-permute-start(bf16[2,64,896]{2,1,0:T(8,128)(2,1)S(1)} %get-tuple-element.40), channel_id=1, source_target_pairs={{0,1},{1,0},{2,3},{3,2},{4,5},{5,4},{6,7},{7,6},{8,9},{9,8},{10,11... | collective-permute-start | bytes 688136 | tf_op jit(solution)/shard_map/ppermute | solution.py:205
  96.1 6.1 %collective-permute-start.23 = (bf16[1,64,896]{2,1,0:T(8,128)(2,1)S(1)}, bf16[1,64,896]{2,1,0:T(8,128)(2,1)S(1)}, u32[]{:S(2)}, u32[]{:S(2)}) collective-permute-start(bf16[1,64,896]{2,1,0:T(8,128)(2,1)S(1)} %get-tuple-element.54), channel_id=1, source_target_pairs={{0,2},{1,3},{2,0},{3,1},{4,6},{5,7},{6,4},{7,5},{8,10},{9,11},{10,... | collective-permute-start | bytes 344072 | tf_op jit(solution)/shard_map/ppermute | solution.py:205
  97.7 6.9 %collective-permute-start.21 = (bf16[1,64,896]{2,1,0:T(8,128)(2,1)S(1)}, bf16[1,64,896]{2,1,0:T(8,128)(2,1)S(1)}, u32[]{:S(2)}, u32[]{:S(2)}) collective-permute-start(bf16[1,64,896]{2,1,0:T(8,128)(2,1)S(1)} %get-tuple-element.50), channel_id=1, source_target_pairs={{0,2},{1,3},{2,0},{3,1},{4,6},{5,7},{6,4},{7,5},{8,10},{9,11},{10,... | collective-permute-start | bytes 344072 | tf_op jit(solution)/shard_map/ppermute | solution.py:205
  98.4 8.7 %collective-permute-start.18 = (bf16[1,64,896]{2,1,0:T(8,128)(2,1)S(1)}, bf16[1,64,896]{2,1,0:T(8,128)(2,1)S(1)}, u32[]{:S(2)}, u32[]{:S(2)}) collective-permute-start(bf16[1,64,896]{2,1,0:T(8,128)(2,1)S(1)} %get-tuple-element.46), channel_id=1, source_target_pairs={{0,2},{1,3},{2,0},{3,1},{4,6},{5,7},{6,4},{7,5},{8,10},{9,11},{10,... | collective-permute-start | bytes 344072 | tf_op jit(solution)/shard_map/ppermute | solution.py:205
  100.0 9.0 %collective-permute-start.13 = (bf16[1,64,896]{2,1,0:T(8,128)(2,1)S(1)}, bf16[1,64,896]{2,1,0:T(8,128)(2,1)S(1)}, u32[]{:S(2)}, u32[]{:S(2)}) collective-permute-start(bf16[1,64,896]{2,1,0:T(8,128)(2,1)S(1)} %get-tuple-element.42), channel_id=1, source_target_pairs={{0,2},{1,3},{2,0},{3,1},{4,6},{5,7},{6,4},{7,5},{8,10},{9,11},{10,... | collective-permute-start | bytes 344072 | tf_op jit(solution)/shard_map/ppermute | solution.py:205
  104.7 5.2 %collective-permute-start.24 = (bf16[128,896]{1,0:T(8,128)(2,1)S(1)}, bf16[128,896]{1,0:T(8,128)(2,1)S(1)}, u32[]{:S(2)}, u32[]{:S(2)}) collective-permute-start(bf16[128,896]{1,0:T(8,128)(2,1)S(1)} %shard_map.96), channel_id=1, source_target_pairs={{0,0},{1,16},{2,8},{3,24},{4,4},{5,20},{6,12},{7,28},{8,1},{9,17},... | collective-permute-start | bytes 688136 | tf_op jit(solution)/shard_map/ppermute | solution.py:205
  109.1 8.5 %collective-permute-start.19 = (bf16[128,896]{1,0:T(8,128)(2,1)S(1)}, bf16[128,896]{1,0:T(8,128)(2,1)S(1)}, u32[]{:S(2)}, u32[]{:S(2)}) collective-permute-start(bf16[128,896]{1,0:T(8,128)(2,1)S(1)} %shard_map.91), channel_id=1, source_target_pairs={{0,8},{1,24},{2,0},{3,16},{4,12},{5,28},{6,4},{7,20},{8,9},{9,25},... | collective-permute-start | bytes 688136 | tf_op jit(solution)/shard_map/ppermute | solution.py:205

commit v5 on v4

--- a/solution.py
+++ b/solution.py
@@ -133,7 +133,8 @@
     half = blocks[0].shape[0]
     for step, block in enumerate(blocks):
         member = ring_member((ring_place(place_ref[2], zs) + zs - step) % zs, zs)
-        at = jnp.where(member // zl == k, 0, zl) + member % zl
+        distance = member ^ place_ref[2]
+        at = jnp.where(distance // zl == k, 0, zl) + distance % zl
         tokens[pl.ds(pl.multiple_of(at * half, half), half), :] = block[...]
     part = jnp.dot(tokens[...], w_ref[...], preferred_element_type=jnp.float32)
     part = part.reshape(zs, half, -1)
@@ -310,7 +311,9 @@
                 piece, last = lax.optimization_barrier((piece, last))
             block = call(add_kernel, ((rows // count, cols), bf16), piece)
             flip = sums[dx, i][2]
-            results.append(send(block, lambda z, x, y, k: (k * zl + (y ^ flip), x, z // 2, z % 2)))
+            results.append(
+                send(block, lambda z, x, y, k: (z ^ (k * zl + (y ^ flip)), x, z // 2, z % 2))
+            )
     columns = []
     for at in range(xs):
         block = results[0]

time: 120 us -> 121 us (level)
  the two profiles are of different devices: /device:TPU:0 before, /device:TPU:1 now
where the time goes in v5:
time: 121 us; the launch traced here: 120 us
  starting transfers between devices  76.8 us (63%)
  waiting for transfers between devices  22.3 us (18%)
  Pallas kernels  18.8 us (16%)
  local copies, waits for them, and re-layouts  1.41 us (1%)
    ppermute x25, starting transfers between devices, send(): return lax.ppermute(value, AXES, pairs)  76.8 us
    ppermute x25, waiting for transfers between devices, send(): return lax.ppermute(value, AXES, pairs)  22.3 us
    pallas_call x15, Pallas kernels, call(): pl.pallas_call(kernel, out_shape=shapes, in_specs=[pl.BlockSpec(memory_sp...  18.8 us
  transfers between devices with their start and end apart: 25, of which 14 were waited for; matrix products, arithmetic and copies ran while one was open for 0% of the time, Pallas kernels for 16%

profile of v5, /device:TPU:1, one launch (start us, length us, event | category | flops | bytes accessed | tf_op | source)
XLA Modules:
  0.0 120.3 jit_solution(2984890936132529879)
XLA Ops:
  0.0 2.0 %collective-permute-start = (bf16[1024,896]{1,0:T(8,128)(2,1)}, bf16[1024,896]{1,0:T(8,128)(2,1)S(1)}, u32[]{:S(2)}, u32[]{:S(2)}) collective-permute-start(bf16[1024,896]{1,0:T(8,128)(2,1)} %w_ref.9), channel_id=1, source_target_pairs={{0,4},{1,5},{2,6},{3,7},{4,0},{5,1},{6,2},{7,3},{8,12},{9,13},{10,... | collective-permute-start | bytes 5505032 | tf_op jit(solution)/shard_map/ppermute | solution.py:206
  2.0 1.6 %shard_map.82.own_ref = bf16[128,576]{1,0:T(8,128)(2,1)} custom-call(bf16[128,512]{1,0:T(8,128)(2,1)} %latent_ref.1, bf16[64,128]{1,0:T(8,128)(2,1)} %bitcast.7), custom_call_target="tpu_custom_call" | custom-call | bytes 294912 | tf_op jit(solution)/shard_map/pallas_call | solution.py:171
  3.7 2.3 %collective-permute-start.2 = (bf16[128,576]{1,0:T(8,128)(2,1)}, bf16[128,576]{1,0:T(8,128)(2,1)S(1)}, u32[]{:S(2)}, u32[]{:S(2)}) collective-permute-start(bf16[128,576]{1,0:T(8,128)(2,1)} %shard_map.82.own_ref), channel_id=1, source_target_pairs={{0,12},{1,17},{2,14},{3,19},{4,8},{5,21},{6,10},{7,23},{8,4},{9,25... | collective-permute-start | bytes 442376 | tf_op jit(solution)/shard_map/ppermute | solution.py:206
  7.3 2.9 %shard_map.83.q_ref = bf16[8,128,576]{2,1,0:T(8,128)(2,1)} custom-call(bf16[128,1024]{1,0:T(8,128)(2,1)} %q_ref.1, bf16[128,512]{1,0:T(8,128)(2,1)} %rope_ref.1, bf16[512,1024]{1,0:T(8,128)(2,1)} %w_ref.5), custom_call_target="tpu_custom_call" | custom-call | flops 134217728 | bytes 2621440 | tf_op jit(solution)/shard_map/pallas_call | solution.py:171
  11.0 1.8 %collective-permute-done.1.refs_0_ = bf16[128,576]{1,0:T(8,128)(2,1)S(1)} collective-permute-done((bf16[128,576]{1,0:T(8,128)(2,1)}, bf16[128,576]{1,0:T(8,128)(2,1)S(1)}, u32[]{:S(2)}, u32[]{:S(2)}) %collective-permute-start.1) | collective-permute-done | bytes 147488 | tf_op jit(solution)/shard_map/ppermute | solution.py:206
  12.8 33.9 %collective-permute-start.5 = (bf16[128,576]{1,0:T(8,128)(2,1)S(1)}, bf16[128,576]{1,0:T(8,128)(2,1)S(1)}, u32[]{:S(2)}, u32[]{:S(2)}) collective-permute-start(bf16[128,576]{1,0:T(8,128)(2,1)S(1)} %collective-permute-done.1.refs_0_), channel_id=1, source_target_pairs={{0,1},{1,0},{2,3},{3,2},{4,5},{5,4},{6,7},{7,6},{8,9},{9,8},{10,11... | collective-permute-start | bytes 442376 | tf_op jit(solution)/shard_map/ppermute | solution.py:206
  46.7 3.6 %collective-permute-start.4 = (bf16[128,576]{1,0:T(8,128)(2,1)S(1)}, bf16[128,576]{1,0:T(8,128)(2,1)S(1)}, u32[]{:S(2)}, u32[]{:S(2)}) collective-permute-start(bf16[128,576]{1,0:T(8,128)(2,1)S(1)} %copy-done.3), channel_id=1, source_target_pairs={{0,20},{1,25},{2,22},{3,27},{4,16},{5,29},{6,18},{7,31},{8,28},{9,... | collective-permute-start | bytes 442376 | tf_op jit(solution)/shard_map/ppermute | solution.py:206
  50.3 2.8 %collective-permute-start.3 = (bf16[128,576]{1,0:T(8,128)(2,1)S(1)}, bf16[128,576]{1,0:T(8,128)(2,1)S(1)}, u32[]{:S(2)}, u32[]{:S(2)}) collective-permute-start(bf16[128,576]{1,0:T(8,128)(2,1)S(1)} %copy-done.3), channel_id=1, source_target_pairs={{1,29},{3,31},{5,25},{7,27},{9,21},{11,23},{13,17},{15,19},{17,13}... | collective-permute-start | bytes 442376 | tf_op jit(solution)/shard_map/ppermute | solution.py:206
  54.6 3.4 %shard_map.84.early_ref = f32[8,128,640]{2,1,0:T(8,128)S(1)} custom-call(s32[16]{0:T(128)S(1)} %copy-done.4, s32[6]{0:T(128)S(1)} %stack.24.place_ref, bf16[8,128,576]{2,1,0:T(8,128)(2,1)S(1)} %copy-done, bf16[128,576]{1,0:T(8,128)(2,1)S(1)} %copy-done.3, bf16[128,576]{1,0:T(8,128)(2,1)S(1)} %collective-permute-done.1.refs_0_, ...), custom_call_target="tpu_custom_call" | custom-call | flops 1426063360 | bytes 4538456 | tf_op jit(solution)/shard_map/pallas_call | solution.py:171
  59.1 4.1 %collective-permute-start.8 = (bf16[128,576]{1,0:T(8,128)(2,1)S(1)}, bf16[128,576]{1,0:T(8,128)(2,1)S(1)}, u32[]{:S(2)}, u32[]{:S(2)}) collective-permute-start(bf16[128,576]{1,0:T(8,128)(2,1)S(1)} %collective-permute-done.3.refs_1_), channel_id=1, source_target_pairs={{1,0},{3,2},{5,4},{7,6},{9,8},{11,10},{13,12},{15,14},{17,16},{19,... | collective-permute-start | bytes 442376 | tf_op jit(solution)/shard_map/ppermute | solution.py:206
  64.7 2.6 %shard_map.88.refs_0_ = bf16[64,1024]{1,0:T(8,128)(2,1)S(1)} custom-call(s32[16]{0:T(128)S(1)} %copy-done.4, s32[6]{0:T(128)S(1)} %stack.24.place_ref, bf16[8,128,576]{2,1,0:T(8,128)(2,1)S(1)} %copy-done, bf16[512,1024]{1,0:T(8,128)(2,1)S(1)} %copy-done.2, f32[8,128,640]{2,1,0:T(8,128)S(1)} %shard_map.84.early_ref, ...), custom_call_target="tpu_custom_call" | custom-call | flops 494927872 | bytes 5570648 | tf_op jit(solution)/shard_map/pallas_call | solution.py:171
  67.6 2.6 %shard_map.85.refs_0_ = bf16[64,1024]{1,0:T(8,128)(2,1)S(1)} custom-call(s32[16]{0:T(128)S(1)} %copy-done.4, s32[6]{0:T(128)S(1)} %stack.24.place_ref, bf16[8,128,576]{2,1,0:T(8,128)(2,1)S(1)} %copy-done, bf16[512,1024]{1,0:T(8,128)(2,1)S(1)} %copy-done.2, f32[8,128,640]{2,1,0:T(8,128)S(1)} %shard_map.84.early_ref, ...), custom_call_target="tpu_custom_call" | custom-call | flops 494927872 | bytes 5570648 | tf_op jit(solution)/shard_map/pallas_call | solution.py:171
  70.2 3.6 %collective-permute-start.9 = (bf16[64,1024]{1,0:T(8,128)(2,1)S(1)}, bf16[64,1024]{1,0:T(8,128)(2,1)S(1)}, u32[]{:S(2)}, u32[]{:S(2)}) collective-permute-start(bf16[64,1024]{1,0:T(8,128)(2,1)S(1)} %shard_map.85.refs_0_), channel_id=1, source_target_pairs={{0,8},{1,9},{2,10},{3,11},{4,12},{5,13},{6,14},{7,15},{8,24},{9,25... | collective-permute-start | bytes 393224 | tf_op jit(solution)/shard_map/ppermute | solution.py:206
  73.9 2.4 %collective-permute-done.9.refs_1_ = bf16[64,1024]{1,0:T(8,128)(2,1)S(1)} collective-permute-done((bf16[64,1024]{1,0:T(8,128)(2,1)S(1)}, bf16[64,1024]{1,0:T(8,128)(2,1)S(1)}, u32[]{:S(2)}, u32[]{:S(2)}) %collective-permute-start.9) | collective-permute-done | bytes 131104 | tf_op jit(solution)/shard_map/ppermute | solution.py:206
  76.3 2.2 %collective-permute-start.10 = (bf16[64,1024]{1,0:T(8,128)(2,1)S(1)}, bf16[64,1024]{1,0:T(8,128)(2,1)S(1)}, u32[]{:S(2)}, u32[]{:S(2)}) collective-permute-start(bf16[64,1024]{1,0:T(8,128)(2,1)S(1)} %collective-permute-done.9.refs_1_), channel_id=1, source_target_pairs={{0,8},{1,9},{2,10},{3,11},{4,12},{5,13},{6,14},{7,15},{8,24},{9,25... | collective-permute-start | bytes 393224 | tf_op jit(solution)/shard_map/ppermute | solution.py:206
  79.1 2.2 %collective-permute-start.16 = (bf16[64,1024]{1,0:T(8,128)(2,1)S(1)}, bf16[64,1024]{1,0:T(8,128)(2,1)S(1)}, u32[]{:S(2)}, u32[]{:S(2)}) collective-permute-start(bf16[64,1024]{1,0:T(8,128)(2,1)S(1)} %collective-permute-done.15.refs_2_), channel_id=1, source_target_pairs={{0,8},{1,9},{2,10},{3,11},{4,12},{5,13},{6,14},{7,15},{8,24},{9,25... | collective-permute-start | bytes 393224 | tf_op jit(solution)/shard_map/ppermute | solution.py:206
  81.4 1.9 %collective-permute-start.11 = (bf16[64,1024]{1,0:T(8,128)(2,1)S(1)}, bf16[64,1024]{1,0:T(8,128)(2,1)S(1)}, u32[]{:S(2)}, u32[]{:S(2)}) collective-permute-start(bf16[64,1024]{1,0:T(8,128)(2,1)S(1)} %collective-permute-done.10.refs_2_), channel_id=1, source_target_pairs={{0,8},{1,9},{2,10},{3,11},{4,12},{5,13},{6,14},{7,15},{8,24},{9,25... | collective-permute-start | bytes 393224 | tf_op jit(solution)/shard_map/ppermute | solution.py:206
  83.3 1.8 %collective-permute-done.16.refs_3_ = bf16[64,1024]{1,0:T(8,128)(2,1)S(1)} collective-permute-done((bf16[64,1024]{1,0:T(8,128)(2,1)S(1)}, bf16[64,1024]{1,0:T(8,128)(2,1)S(1)}, u32[]{:S(2)}, u32[]{:S(2)}) %collective-permute-start.16) | collective-permute-done | bytes 131104 | tf_op jit(solution)/shard_map/ppermute | solution.py:206
  85.1 1.3 %shard_map.94 = (f32[2,64,896]{2,1,0:T(8,128)S(1)}, bf16[2,64,896]{2,1,0:T(8,128)(2,1)S(1)}) custom-call(s32[6]{0:T(128)S(1)} %stack.24.place_ref, bf16[1024,896]{1,0:T(8,128)(2,1)S(1)} %copy-done.1, bf16[64,1024]{1,0:T(8,128)(2,1)S(1)} %shard_map.88.refs_0_, bf16[64,1024]{1,0:T(8,128)(2,1)S(1)} %collective-permute-done.14.refs_1_, ...), custom_call_target="tpu_custom_call" | custom-call | flops 469762048 | bytes 3047448 | tf_op jit(solution)/shard_map/pallas_call | solution.py:171
  86.4 3.5 %collective-permute-start.22 = (bf16[2,64,896]{2,1,0:T(8,128)(2,1)S(1)}, bf16[2,64,896]{2,1,0:T(8,128)(2,1)S(1)}, u32[]{:S(2)}, u32[]{:S(2)}) collective-permute-start(bf16[2,64,896]{2,1,0:T(8,128)(2,1)S(1)} %get-tuple-element.52), channel_id=1, source_target_pairs={{0,1},{1,0},{2,3},{3,2},{4,5},{5,4},{6,7},{7,6},{8,9},{9,8},{10,11... | collective-permute-start | bytes 688136 | tf_op jit(solution)/shard_map/ppermute | solution.py:206
  89.9 1.3 %shard_map.92 = (f32[2,64,896]{2,1,0:T(8,128)S(1)}, bf16[2,64,896]{2,1,0:T(8,128)(2,1)S(1)}) custom-call(s32[6]{0:T(128)S(1)} %stack.24.place_ref, bf16[1024,896]{1,0:T(8,128)(2,1)S(1)} %copy-done.1, bf16[64,1024]{1,0:T(8,128)(2,1)S(1)} %shard_map.85.refs_0_, bf16[64,1024]{1,0:T(8,128)(2,1)S(1)} %collective-permute-done.9.refs_1_, ...), custom_call_target="tpu_custom_call" | custom-call | flops 469762048 | bytes 3047448 | tf_op jit(solution)/shard_map/pallas_call | solution.py:171
  91.2 1.5 %collective-permute-start.20 = (bf16[2,64,896]{2,1,0:T(8,128)(2,1)S(1)}, bf16[2,64,896]{2,1,0:T(8,128)(2,1)S(1)}, u32[]{:S(2)}, u32[]{:S(2)}) collective-permute-start(bf16[2,64,896]{2,1,0:T(8,128)(2,1)S(1)} %get-tuple-element.48), channel_id=1, source_target_pairs={{0,1},{1,0},{2,3},{3,2},{4,5},{5,4},{6,7},{7,6},{8,9},{9,8},{10,11... | collective-permute-start | bytes 688136 | tf_op jit(solution)/shard_map/ppermute | solution.py:206
  92.7 1.3 %shard_map.89 = (f32[2,64,896]{2,1,0:T(8,128)S(1)}, bf16[2,64,896]{2,1,0:T(8,128)(2,1)S(1)}) custom-call(s32[6]{0:T(128)S(1)} %stack.24.place_ref, bf16[1024,896]{1,0:T(8,128)(2,1)S(1)} %collective-permute-done.w_ref, bf16[64,1024]{1,0:T(8,128)(2,1)S(1)} %shard_map.88.refs_0_, bf16[64,1024]{1,0:T(8,128)(2,1)S(1)} %collective-permute-done.14.refs_1_, ...), custom_call_target="tpu_custom_call" | custom-call | flops 469762048 | bytes 3047448 | tf_op jit(solution)/shard_map/pallas_call | solution.py:171
  94.1 1.3 %shard_map.86 = (f32[2,64,896]{2,1,0:T(8,128)S(1)}, bf16[2,64,896]{2,1,0:T(8,128)(2,1)S(1)}) custom-call(s32[6]{0:T(128)S(1)} %stack.24.place_ref, bf16[1024,896]{1,0:T(8,128)(2,1)S(1)} %collective-permute-done.w_ref, bf16[64,1024]{1,0:T(8,128)(2,1)S(1)} %shard_map.85.refs_0_, bf16[64,1024]{1,0:T(8,128)(2,1)S(1)} %collective-permute-done.9.refs_1_, ...), custom_call_target="tpu_custom_call" | custom-call | flops 469762048 | bytes 3047448 | tf_op jit(solution)/shard_map/pallas_call | solution.py:171
  96.1 1.3 %collective-permute-start.23 = (bf16[1,64,896]{2,1,0:T(8,128)(2,1)S(1)}, bf16[1,64,896]{2,1,0:T(8,128)(2,1)S(1)}, u32[]{:S(2)}, u32[]{:S(2)}) collective-permute-start(bf16[1,64,896]{2,1,0:T(8,128)(2,1)S(1)} %get-tuple-element.54), channel_id=1, source_target_pairs={{0,2},{1,3},{2,0},{3,1},{4,6},{5,7},{6,4},{7,5},{8,10},{9,11},{10,... | collective-permute-start | bytes 344072 | tf_op jit(solution)/shard_map/ppermute | solution.py:206
  97.8 1.3 %collective-permute-start.18 = (bf16[1,64,896]{2,1,0:T(8,128)(2,1)S(1)}, bf16[1,64,896]{2,1,0:T(8,128)(2,1)S(1)}, u32[]{:S(2)}, u32[]{:S(2)}) collective-permute-start(bf16[1,64,896]{2,1,0:T(8,128)(2,1)S(1)} %get-tuple-element.46), channel_id=1, source_target_pairs={{0,2},{1,3},{2,0},{3,1},{4,6},{5,7},{6,4},{7,5},{8,10},{9,11},{10,... | collective-permute-start | bytes 344072 | tf_op jit(solution)/shard_map/ppermute | solution.py:206
  99.5 1.3 %collective-permute-done.23.refs_3_ = bf16[1,64,896]{2,1,0:T(8,128)(2,1)S(1)} collective-permute-done((bf16[1,64,896]{2,1,0:T(8,128)(2,1)S(1)}, bf16[1,64,896]{2,1,0:T(8,128)(2,1)S(1)}, u32[]{:S(2)}, u32[]{:S(2)}) %collective-permute-start.23) | collective-permute-done | bytes 114720 | tf_op jit(solution)/shard_map/ppermute | solution.py:206
  100.8 2.5 %collective-permute-done.21.refs_1_ = bf16[1,64,896]{2,1,0:T(8,128)(2,1)S(1)} collective-permute-done((bf16[1,64,896]{2,1,0:T(8,128)(2,1)S(1)}, bf16[1,64,896]{2,1,0:T(8,128)(2,1)S(1)}, u32[]{:S(2)}, u32[]{:S(2)}) %collective-permute-start.21) | collective-permute-done | bytes 114720 | tf_op jit(solution)/shard_map/ppermute | solution.py:206
  103.3 2.9 %collective-permute-start.24 = (bf16[128,896]{1,0:T(8,128)(2,1)S(1)}, bf16[128,896]{1,0:T(8,128)(2,1)S(1)}, u32[]{:S(2)}, u32[]{:S(2)}) collective-permute-start(bf16[128,896]{1,0:T(8,128)(2,1)S(1)} %shard_map.96), channel_id=1, source_target_pairs={{0,0},{1,16},{2,8},{3,24},{4,4},{5,20},{6,12},{7,28},{8,9},{9,25},... | collective-permute-start | bytes 688136 | tf_op jit(solution)/shard_map/ppermute | solution.py:206
  106.2 2.0 %collective-permute-done.13.refs_1_ = bf16[1,64,896]{2,1,0:T(8,128)(2,1)S(1)} collective-permute-done((bf16[1,64,896]{2,1,0:T(8,128)(2,1)S(1)}, bf16[1,64,896]{2,1,0:T(8,128)(2,1)S(1)}, u32[]{:S(2)}, u32[]{:S(2)}) %collective-permute-start.13) | collective-permute-done | bytes 114720 | tf_op jit(solution)/shard_map/ppermute | solution.py:206
  108.2 4.7 %collective-permute-start.19 = (bf16[128,896]{1,0:T(8,128)(2,1)S(1)}, bf16[128,896]{1,0:T(8,128)(2,1)S(1)}, u32[]{:S(2)}, u32[]{:S(2)}) collective-permute-start(bf16[128,896]{1,0:T(8,128)(2,1)S(1)} %shard_map.91), channel_id=1, source_target_pairs={{0,8},{1,24},{2,0},{3,16},{4,12},{5,28},{6,4},{7,20},{8,1},{9,17},... | collective-permute-start | bytes 688136 | tf_op jit(solution)/shard_map/ppermute | solution.py:206
  113.1 6.3 %collective-permute-done.19 = bf16[128,896]{1,0:T(8,128)(2,1)S(1)} collective-permute-done((bf16[128,896]{1,0:T(8,128)(2,1)S(1)}, bf16[128,896]{1,0:T(8,128)(2,1)S(1)}, u32[]{:S(2)}, u32[]{:S(2)}) %collective-permute-start.19) | collective-permute-done | bytes 229408 | tf_op jit(solution)/shard_map/ppermute | solution.py:206
  (46 shorter events, 9.7 us)
Async XLA Ops:
  0.0 53.3 %copy-start.4 = (s32[16]{0:T(128)S(1)}, s32[16]{0:T(128)}, u32[]{:S(2)}) copy-start(s32[16]{0:T(128)} %order_ref.5) | copy-start | bytes 196
  0.0 92.7 %collective-permute-start = (bf16[1024,896]{1,0:T(8,128)(2,1)}, bf16[1024,896]{1,0:T(8,128)(2,1)S(1)}, u32[]{:S(2)}, u32[]{:S(2)}) collective-permute-start(bf16[1024,896]{1,0:T(8,128)(2,1)} %w_ref.9), channel_id=1, source_target_pairs={{0,4},{1,5},{2,6},{3,7},{4,0},{5,1},{6,2},{7,3},{8,12},{9,13},{10,... | collective-permute-start | bytes 5505032 | tf_op jit(solution)/shard_map/ppermute | solution.py:206
  3.7 43.0 %copy-start.3 = (bf16[128,576]{1,0:T(8,128)(2,1)S(1)}, bf16[128,576]{1,0:T(8,128)(2,1)}, u32[]{:S(2)}) copy-start(bf16[128,576]{1,0:T(8,128)(2,1)} %shard_map.82.own_ref) | copy-start | bytes 442372
  3.7 7.3 %collective-permute-start.2 = (bf16[128,576]{1,0:T(8,128)(2,1)}, bf16[128,576]{1,0:T(8,128)(2,1)S(1)}, u32[]{:S(2)}, u32[]{:S(2)}) collective-permute-start(bf16[128,576]{1,0:T(8,128)(2,1)} %shard_map.82.own_ref), channel_id=1, source_target_pairs={{0,12},{1,17},{2,14},{3,19},{4,8},{5,21},{6,10},{7,23},{8,4},{9,25... | collective-permute-start | bytes 442376 | tf_op jit(solution)/shard_map/ppermute | solution.py:206
  6.0 6.8 %collective-permute-start.1 = (bf16[128,576]{1,0:T(8,128)(2,1)}, bf16[128,576]{1,0:T(8,128)(2,1)S(1)}, u32[]{:S(2)}, u32[]{:S(2)}) collective-permute-start(bf16[128,576]{1,0:T(8,128)(2,1)} %shard_map.82.own_ref), channel_id=1, source_target_pairs={{0,4},{1,9},{2,6},{3,11},{4,0},{5,13},{6,2},{7,15},{8,12},{9,1},{1... | collective-permute-start | bytes 442376 | tf_op jit(solution)/shard_map/ppermute | solution.py:206
  12.8 40.5 %collective-permute-start.5 = (bf16[128,576]{1,0:T(8,128)(2,1)S(1)}, bf16[128,576]{1,0:T(8,128)(2,1)S(1)}, u32[]{:S(2)}, u32[]{:S(2)}) collective-permute-start(bf16[128,576]{1,0:T(8,128)(2,1)S(1)} %collective-permute-done.1.refs_0_), channel_id=1, source_target_pairs={{0,1},{1,0},{2,3},{3,2},{4,5},{5,4},{6,7},{7,6},{8,9},{9,8},{10,11... | collective-permute-start | bytes 442376 | tf_op jit(solution)/shard_map/ppermute | solution.py:206
  46.7 6.6 %collective-permute-start.6 = (bf16[128,576]{1,0:T(8,128)(2,1)S(1)}, bf16[128,576]{1,0:T(8,128)(2,1)S(1)}, u32[]{:S(2)}, u32[]{:S(2)}) collective-permute-start(bf16[128,576]{1,0:T(8,128)(2,1)S(1)} %collective-permute-done.2.refs_1_), channel_id=1, source_target_pairs={{0,1},{1,0},{2,3},{3,2},{4,5},{5,4},{6,7},{7,6},{8,9},{9,8},{10,11... | collective-permute-start | bytes 442376 | tf_op jit(solution)/shard_map/ppermute | solution.py:206
  46.7 11.3 %collective-permute-start.4 = (bf16[128,576]{1,0:T(8,128)(2,1)S(1)}, bf16[128,576]{1,0:T(8,128)(2,1)S(1)}, u32[]{:S(2)}, u32[]{:S(2)}) collective-permute-start(bf16[128,576]{1,0:T(8,128)(2,1)S(1)} %copy-done.3), channel_id=1, source_target_pairs={{0,20},{1,25},{2,22},{3,27},{4,16},{5,29},{6,18},{7,31},{8,28},{9,... | collective-permute-start | bytes 442376 | tf_op jit(solution)/shard_map/ppermute | solution.py:206
  50.3 8.8 %collective-permute-start.3 = (bf16[128,576]{1,0:T(8,128)(2,1)S(1)}, bf16[128,576]{1,0:T(8,128)(2,1)S(1)}, u32[]{:S(2)}, u32[]{:S(2)}) collective-permute-start(bf16[128,576]{1,0:T(8,128)(2,1)S(1)} %copy-done.3), channel_id=1, source_target_pairs={{1,29},{3,31},{5,25},{7,27},{9,21},{11,23},{13,17},{15,19},{17,13}... | collective-permute-start | bytes 442376 | tf_op jit(solution)/shard_map/ppermute | solution.py:206
  53.3 1.3 %copy-start = (bf16[8,128,576]{2,1,0:T(8,128)(2,1)S(1)}, bf16[8,128,576]{2,1,0:T(8,128)(2,1)}, u32[]{:S(2)}) copy-start(bf16[8,128,576]{2,1,0:T(8,128)(2,1)} %shard_map.83.q_ref) | copy-start | bytes 3538948
  54.6 10.1 %copy-start.2 = (bf16[512,1024]{1,0:T(8,128)(2,1)S(1)}, bf16[512,1024]{1,0:T(8,128)(2,1)}, u32[]{:S(2)}) copy-start(bf16[512,1024]{1,0:T(8,128)(2,1)} %w_ref.7) | copy-start | bytes 3145732
  59.1 5.1 %collective-permute-start.8 = (bf16[128,576]{1,0:T(8,128)(2,1)S(1)}, bf16[128,576]{1,0:T(8,128)(2,1)S(1)}, u32[]{:S(2)}, u32[]{:S(2)}) collective-permute-start(bf16[128,576]{1,0:T(8,128)(2,1)S(1)} %collective-permute-done.3.refs_1_), channel_id=1, source_target_pairs={{1,0},{3,2},{5,4},{7,6},{9,8},{11,10},{13,12},{15,14},{17,16},{19,... | collective-permute-start | bytes 442376 | tf_op jit(solution)/shard_map/ppermute | solution.py:206
  63.3 1.5 %collective-permute-start.7 = (bf16[128,576]{1,0:T(8,128)(2,1)S(1)}, bf16[128,576]{1,0:T(8,128)(2,1)S(1)}, u32[]{:S(2)}, u32[]{:S(2)}) collective-permute-start(bf16[128,576]{1,0:T(8,128)(2,1)S(1)} %collective-permute-done.4.refs_0_), channel_id=1, source_target_pairs={{0,1},{1,0},{2,3},{3,2},{4,5},{5,4},{6,7},{7,6},{8,9},{9,8},{10,11... | collective-permute-start | bytes 442376 | tf_op jit(solution)/shard_map/ppermute | solution.py:206
  67.4 17.7 %copy-start.1 = (bf16[1024,896]{1,0:T(8,128)(2,1)S(1)}, bf16[1024,896]{1,0:T(8,128)(2,1)}, u32[]{:S(2)}) copy-start(bf16[1024,896]{1,0:T(8,128)(2,1)} %w_ref.9) | copy-start | bytes 5505028
  67.4 6.4 %collective-permute-start.14 = (bf16[64,1024]{1,0:T(8,128)(2,1)S(1)}, bf16[64,1024]{1,0:T(8,128)(2,1)S(1)}, u32[]{:S(2)}, u32[]{:S(2)}) collective-permute-start(bf16[64,1024]{1,0:T(8,128)(2,1)S(1)} %shard_map.88.refs_0_), channel_id=1, source_target_pairs={{0,8},{1,9},{2,10},{3,11},{4,12},{5,13},{6,14},{7,15},{8,24},{9,25... | collective-permute-start | bytes 393224 | tf_op jit(solution)/shard_map/ppermute | solution.py:206
  70.2 6.0 %collective-permute-start.9 = (bf16[64,1024]{1,0:T(8,128)(2,1)S(1)}, bf16[64,1024]{1,0:T(8,128)(2,1)S(1)}, u32[]{:S(2)}, u32[]{:S(2)}) collective-permute-start(bf16[64,1024]{1,0:T(8,128)(2,1)S(1)} %shard_map.85.refs_0_), channel_id=1, source_target_pairs={{0,8},{1,9},{2,10},{3,11},{4,12},{5,13},{6,14},{7,15},{8,24},{9,25... | collective-permute-start | bytes 393224 | tf_op jit(solution)/shard_map/ppermute | solution.py:206
  73.8 5.3 %collective-permute-start.15 = (bf16[64,1024]{1,0:T(8,128)(2,1)S(1)}, bf16[64,1024]{1,0:T(8,128)(2,1)S(1)}, u32[]{:S(2)}, u32[]{:S(2)}) collective-permute-start(bf16[64,1024]{1,0:T(8,128)(2,1)S(1)} %collective-permute-done.14.refs_1_), channel_id=1, source_target_pairs={{0,8},{1,9},{2,10},{3,11},{4,12},{5,13},{6,14},{7,15},{8,24},{9,25... | collective-permute-start | bytes 393224 | tf_op jit(solution)/shard_map/ppermute | solution.py:206
  76.3 5.1 %collective-permute-start.10 = (bf16[64,1024]{1,0:T(8,128)(2,1)S(1)}, bf16[64,1024]{1,0:T(8,128)(2,1)S(1)}, u32[]{:S(2)}, u32[]{:S(2)}) collective-permute-start(bf16[64,1024]{1,0:T(8,128)(2,1)S(1)} %collective-permute-done.9.refs_1_), channel_id=1, source_target_pairs={{0,8},{1,9},{2,10},{3,11},{4,12},{5,13},{6,14},{7,15},{8,24},{9,25... | collective-permute-start | bytes 393224 | tf_op jit(solution)/shard_map/ppermute | solution.py:206
  79.1 6.0 %collective-permute-start.16 = (bf16[64,1024]{1,0:T(8,128)(2,1)S(1)}, bf16[64,1024]{1,0:T(8,128)(2,1)S(1)}, u32[]{:S(2)}, u32[]{:S(2)}) collective-permute-start(bf16[64,1024]{1,0:T(8,128)(2,1)S(1)} %collective-permute-done.15.refs_2_), channel_id=1, source_target_pairs={{0,8},{1,9},{2,10},{3,11},{4,12},{5,13},{6,14},{7,15},{8,24},{9,25... | collective-permute-start | bytes 393224 | tf_op jit(solution)/shard_map/ppermute | solution.py:206
  81.4 8.5 %collective-permute-start.11 = (bf16[64,1024]{1,0:T(8,128)(2,1)S(1)}, bf16[64,1024]{1,0:T(8,128)(2,1)S(1)}, u32[]{:S(2)}, u32[]{:S(2)}) collective-permute-start(bf16[64,1024]{1,0:T(8,128)(2,1)S(1)} %collective-permute-done.10.refs_2_), channel_id=1, source_target_pairs={{0,8},{1,9},{2,10},{3,11},{4,12},{5,13},{6,14},{7,15},{8,24},{9,25... | collective-permute-start | bytes 393224 | tf_op jit(solution)/shard_map/ppermute | solution.py:206
  86.4 9.6 %collective-permute-start.22 = (bf16[2,64,896]{2,1,0:T(8,128)(2,1)S(1)}, bf16[2,64,896]{2,1,0:T(8,128)(2,1)S(1)}, u32[]{:S(2)}, u32[]{:S(2)}) collective-permute-start(bf16[2,64,896]{2,1,0:T(8,128)(2,1)S(1)} %get-tuple-element.52), channel_id=1, source_target_pairs={{0,1},{1,0},{2,3},{3,2},{4,5},{5,4},{6,7},{7,6},{8,9},{9,8},{10,11... | collective-permute-start | bytes 688136 | tf_op jit(solution)/shard_map/ppermute | solution.py:206
  91.2 6.2 %collective-permute-start.20 = (bf16[2,64,896]{2,1,0:T(8,128)(2,1)S(1)}, bf16[2,64,896]{2,1,0:T(8,128)(2,1)S(1)}, u32[]{:S(2)}, u32[]{:S(2)}) collective-permute-start(bf16[2,64,896]{2,1,0:T(8,128)(2,1)S(1)} %get-tuple-element.48), channel_id=1, source_target_pairs={{0,1},{1,0},{2,3},{3,2},{4,5},{5,4},{6,7},{7,6},{8,9},{9,8},{10,11... | collective-permute-start | bytes 688136 | tf_op jit(solution)/shard_map/ppermute | solution.py:206
  94.1 3.7 %collective-permute-start.17 = (bf16[2,64,896]{2,1,0:T(8,128)(2,1)S(1)}, bf16[2,64,896]{2,1,0:T(8,128)(2,1)S(1)}, u32[]{:S(2)}, u32[]{:S(2)}) collective-permute-start(bf16[2,64,896]{2,1,0:T(8,128)(2,1)S(1)} %get-tuple-element.44), channel_id=1, source_target_pairs={{0,1},{1,0},{2,3},{3,2},{4,5},{5,4},{6,7},{7,6},{8,9},{9,8},{10,11... | collective-permute-start | bytes 688136 | tf_op jit(solution)/shard_map/ppermute | solution.py:206
  95.5 3.7 %collective-permute-start.12 = (bf16[2,64,896]{2,1,0:T(8,128)(2,1)S(1)}, bf16[2,64,896]{2,1,0:T(8,128)(2,1)S(1)}, u32[]{:S(2)}, u32[]{:S(2)}) collective-permute-start(bf16[2,64,896]{2,1,0:T(8,128)(2,1)S(1)} %get-tuple-element.40), channel_id=1, source_target_pairs={{0,1},{1,0},{2,3},{3,2},{4,5},{5,4},{6,7},{7,6},{8,9},{9,8},{10,11... | collective-permute-start | bytes 688136 | tf_op jit(solution)/shard_map/ppermute | solution.py:206
  96.1 4.7 %collective-permute-start.23 = (bf16[1,64,896]{2,1,0:T(8,128)(2,1)S(1)}, bf16[1,64,896]{2,1,0:T(8,128)(2,1)S(1)}, u32[]{:S(2)}, u32[]{:S(2)}) collective-permute-start(bf16[1,64,896]{2,1,0:T(8,128)(2,1)S(1)} %get-tuple-element.54), channel_id=1, source_target_pairs={{0,2},{1,3},{2,0},{3,1},{4,6},{5,7},{6,4},{7,5},{8,10},{9,11},{10,... | collective-permute-start | bytes 344072 | tf_op jit(solution)/shard_map/ppermute | solution.py:206
  97.5 5.8 %collective-permute-start.21 = (bf16[1,64,896]{2,1,0:T(8,128)(2,1)S(1)}, bf16[1,64,896]{2,1,0:T(8,128)(2,1)S(1)}, u32[]{:S(2)}, u32[]{:S(2)}) collective-permute-start(bf16[1,64,896]{2,1,0:T(8,128)(2,1)S(1)} %get-tuple-element.50), channel_id=1, source_target_pairs={{0,2},{1,3},{2,0},{3,1},{4,6},{5,7},{6,4},{7,5},{8,10},{9,11},{10,... | collective-permute-start | bytes 344072 | tf_op jit(solution)/shard_map/ppermute | solution.py:206
  97.8 8.4 %collective-permute-start.18 = (bf16[1,64,896]{2,1,0:T(8,128)(2,1)S(1)}, bf16[1,64,896]{2,1,0:T(8,128)(2,1)S(1)}, u32[]{:S(2)}, u32[]{:S(2)}) collective-permute-start(bf16[1,64,896]{2,1,0:T(8,128)(2,1)S(1)} %get-tuple-element.46), channel_id=1, source_target_pairs={{0,2},{1,3},{2,0},{3,1},{4,6},{5,7},{6,4},{7,5},{8,10},{9,11},{10,... | collective-permute-start | bytes 344072 | tf_op jit(solution)/shard_map/ppermute | solution.py:206
  99.2 9.0 %collective-permute-start.13 = (bf16[1,64,896]{2,1,0:T(8,128)(2,1)S(1)}, bf16[1,64,896]{2,1,0:T(8,128)(2,1)S(1)}, u32[]{:S(2)}, u32[]{:S(2)}) collective-permute-start(bf16[1,64,896]{2,1,0:T(8,128)(2,1)S(1)} %get-tuple-element.42), channel_id=1, source_target_pairs={{0,2},{1,3},{2,0},{3,1},{4,6},{5,7},{6,4},{7,5},{8,10},{9,11},{10,... | collective-permute-start | bytes 344072 | tf_op jit(solution)/shard_map/ppermute | solution.py:206
  103.3 9.8 %collective-permute-start.24 = (bf16[128,896]{1,0:T(8,128)(2,1)S(1)}, bf16[128,896]{1,0:T(8,128)(2,1)S(1)}, u32[]{:S(2)}, u32[]{:S(2)}) collective-permute-start(bf16[128,896]{1,0:T(8,128)(2,1)S(1)} %shard_map.96), channel_id=1, source_target_pairs={{0,0},{1,16},{2,8},{3,24},{4,4},{5,20},{6,12},{7,28},{8,9},{9,25},... | collective-permute-start | bytes 688136 | tf_op jit(solution)/shard_map/ppermute | solution.py:206
  108.2 11.2 %collective-permute-start.19 = (bf16[128,896]{1,0:T(8,128)(2,1)S(1)}, bf16[128,896]{1,0:T(8,128)(2,1)S(1)}, u32[]{:S(2)}, u32[]{:S(2)}) collective-permute-start(bf16[128,896]{1,0:T(8,128)(2,1)S(1)} %shard_map.91), channel_id=1, source_target_pairs={{0,8},{1,24},{2,0},{3,16},{4,12},{5,28},{6,4},{7,20},{8,1},{9,17},... | collective-permute-start | bytes 688136 | tf_op jit(solution)/shard_map/ppermute | solution.py:206
